TPU v7x, 512 devices: a whole 4x4x16 slice. The times are simulated.
512 devices in a mesh: tile: 128 (over z, x, core), layer: 4 (over y).
Axes of the slice: x: 4, y: 4, z: 16, core: 2. Of those that a mesh axis runs over, the one named last changes fastest.
Arguments:
- head_start: float32 [8, 8192, 512], P('layer', 'tile'), may hold values from -2 to 0.5
- soil_class: int32 [8, 8192, 512], P('layer', 'tile'), may hold values from 0 to 11
- land_mask: int32 [8192, 512], P('tile'), may hold values 0 or 1
- ks_table: float32 [12], replicated, may hold values from 0.2 to 5
- alpha_table: float32 [12], replicated, may hold values from 0.5 to 2
- store_table: float32 [12], replicated, may hold values from 0.5 to 2
- section: float32 [2048, 128], P('tile'), may hold values from -6 to 6
- cross_owner: int32 [128, 256], P('tile'), may hold values from 0 to 127, as said below
- cross_local: int32 [128, 256], P('tile'), may hold values from 0 to 15
- node_cell: int32 [128, 256, 128], P('tile'), may hold values from -1 to 32767, as said below
- bed_cond: float32 [128, 256, 128], P('tile'), may hold values from 0.5 to 4
Outputs:
- head: float32 [8, 8192, 512], P('layer', 'tile')
- inflow: float32 [2048, 128], P('tile', 'layer')
Inputs may be any that keep to these rules, and one draw needn't show every extreme that they name: `cross_owner`: no strip's row names one owner in more than 2 slots, and in every row some owner is named in exactly 2 slots. `node_cell`: -1 marks a node outside the strip; other values index the strip's top-layer cells row-major over 64 x 512. In each strip the slots with nodes come first, the rest are padding with every node -1.
All inputs are finite; a program needn't handle non-finite values. No bound on the sum of `land_mask` on one device may be relied on, other than what follows from the above.
Results may differ from a plain program's by a relative error of at most 0.00002.
Values sent between devices are 32-bit elements; how exact they have to be, the bound alone decides.
A program may use at most 64 MiB of HBM per device.

v0:
```python
import jax
import jax.numpy as jnp
from jax import lax
from jax.sharding import PartitionSpec as P

ITERS = 2
SWEEPS = 3


LATERAL = 1.0
VERTICAL = 2.0
GRAVITY = 1.0
NEIGHBOURS = (
    (0, -1, VERTICAL),
    (0, 1, VERTICAL),
    (1, -1, LATERAL),
    (1, 1, LATERAL),
    (2, -1, LATERAL),
    (2, 1, LATERAL),
)


def with_halo(block, sides, width):
    for axis, dim in sides:
        count = lax.axis_size(axis)
        forward = [(i, i + 1) for i in range(count - 1)]
        backward = [(target, source) for source, target in forward]
        low = lax.ppermute(
            lax.slice_in_dim(block, block.shape[dim] - width, None, axis=dim), axis, forward
        )
        high = lax.ppermute(lax.slice_in_dim(block, 0, width, axis=dim), axis, backward)
        block = jnp.concatenate([low, block, high], axis=dim)
    return block


def from_root(value, axis, source):
    kept = jnp.where(lax.axis_index(axis) == source, value, 0).astype(value.dtype)
    return lax.psum(kept, axis)


def beside(padded, axis_id, step):
    spans = [slice(1, -1), slice(1, -1), slice(1, -1)]
    spans[axis_id] = slice(1 + step, padded.shape[axis_id] - 1 + step)
    return padded[tuple(spans)]


def neighbor_weights(cond_pad, open_pad):
    centre = cond_pad[1:-1, 1:-1, 1:-1]
    centre_open = open_pad[1:-1, 1:-1, 1:-1]
    result = []
    for axis_id, step, factor in NEIGHBOURS:
        far = beside(cond_pad, axis_id, step)
        far_open = beside(open_pad, axis_id, step)
        result.append(factor * 2.0 * centre_open * far_open / (centre + far))
    return result


def relax(head_pad, weights, store, head_old, riv_diag, riv_rhs):
    total = store * head_old
    diagonal_sum = store
    for weight, (axis_id, step, factor) in zip(weights, NEIGHBOURS):
        total = total + weight * beside(head_pad, axis_id, step)
        diagonal_sum = diagonal_sum + weight
    total = total + GRAVITY * (weights[0] - weights[1]) + riv_rhs
    return total / (diagonal_sum + riv_diag)


def lookup(values_table, classes):
    result = jnp.zeros(classes.shape, jnp.float32)
    for class_id in range(values_table.shape[0]):
        result = jnp.where(classes == class_id, values_table[class_id], result)
    return result


def pad_dims(field, chosen_dims):
    widths = [(1, 1) if place in chosen_dims else (0, 0) for place in range(field.ndim)]
    return jnp.pad(field, widths)


def pick_heads(top_head, cells):
    breadth = top_head.shape[1]
    slots, width = cells.shape
    group = 16
    grouped = cells.reshape(slots // group, group * width)
    columns = jnp.arange(breadth, dtype=jnp.int32)[None, :]

    def one_group(flat_cells):
        picked_rows = jnp.take(top_head, flat_cells // breadth, axis=0)
        hit = columns == (flat_cells % breadth)[:, None]
        return jnp.sum(jnp.where(hit, picked_rows, 0.0), axis=1)

    return lax.map(one_group, grouped).reshape(slots, width)


def on_device(
    head_start,
    soil_class,
    land_mask,
    ks_table,
    alpha_table,
    store_table,
    section,
    cross_owner,
    cross_local,
    node_cell,
    bed_cond,
):
    layers, across, breadth = head_start.shape
    reach_rows = section.shape[0]
    node_count = section.shape[1]
    tile_count = lax.axis_size("tile")
    quarter = node_count // lax.axis_size("layer")
    node_first = lax.axis_index("layer") * quarter
    ks = lookup(ks_table, soil_class)
    alpha = lookup(alpha_table, soil_class)
    store = lookup(store_table, soil_class)
    landf = land_mask.astype(jnp.float32)[None]
    owners = cross_owner[0]
    positions = cross_local[0]
    node_cells = node_cell[0]
    bed_given = bed_cond[0]
    whole_section = lax.all_gather(section, "tile", axis=0, tiled=True)
    slot_section = jnp.take(whole_section, owners * reach_rows + positions, axis=0)
    in_tile = node_cells >= 0
    flat_index = jnp.where(in_tile, node_cells, across * breadth)
    bed_terms = jnp.where(in_tile, bed_given, 0.0)
    diag_top = (
        jnp.zeros((across * breadth,), jnp.float32)
        .at[flat_index.reshape(-1)]
        .add(bed_terms.reshape(-1), mode="drop")
    )
    rhs_top = (
        jnp.zeros((across * breadth,), jnp.float32)
        .at[flat_index.reshape(-1)]
        .add((bed_terms * slot_section).reshape(-1), mode="drop")
    )
    top_diag = diag_top.reshape(across, breadth)
    top_rhs = rhs_top.reshape(across, breadth)
    head_old, ks_here, alpha_here, store_here, land_here = (head_start, ks, alpha, store, landf)
    on_top = (lax.axis_index("layer") == 0).astype(jnp.float32)
    riv_diag = jnp.zeros((layers, across, breadth), jnp.float32).at[0].set(top_diag * on_top)
    riv_rhs = jnp.zeros((layers, across, breadth), jnp.float32).at[0].set(top_rhs * on_top)

    def head_halo(field):
        return pad_dims(with_halo(field, (("tile", 1), ("layer", 0)), 1), (2,))

    head = head_old
    for picard in range(ITERS):
        head_pad = head_halo(head)
        conduct = ks_here * jnp.exp(alpha_here * jnp.minimum(head, 0.0))
        both_pad = pad_dims(
            with_halo(jnp.stack([conduct, conduct * land_here]), (("tile", 2), ("layer", 1)), 1),
            (3,),
        )
        cond_pad = both_pad[0]
        open_pad = both_pad[1]
        weights = neighbor_weights(cond_pad, open_pad)
        for sweep in range(SWEEPS):
            if sweep > 0:
                head_pad = head_halo(head)
            head = relax(head_pad, weights, store_here, head_old, riv_diag, riv_rhs)
    top_head = from_root(head[0], "layer", 0)
    my_cells = lax.dynamic_slice_in_dim(node_cells, node_first, quarter, 1)
    my_bed = lax.dynamic_slice_in_dim(bed_given, node_first, quarter, 1)
    my_section = lax.dynamic_slice_in_dim(slot_section, node_first, quarter, 1)
    my_inside = my_cells >= 0
    node_head = pick_heads(top_head, jnp.where(my_inside, my_cells, 0))
    slot_in = jnp.where(my_inside, my_bed * (node_head - my_section), 0.0)
    dense = (
        jnp.zeros((reach_rows * tile_count, quarter), jnp.float32)
        .at[owners * reach_rows + positions]
        .add(slot_in)
    )
    inflow = lax.psum_scatter(dense, "tile", scatter_dimension=0, tiled=True)
    return (head, inflow)


def solution(mesh):
    placed = (
        P("layer", "tile", None),
        P("layer", "tile", None),
        P("tile", None),
        P(),
        P(),
        P(),
        P("tile", None),
        P("tile", None),
        P("tile", None),
        P("tile", None, None),
        P("tile", None, None),
    )
    return jax.shard_map(
        on_device,
        mesh=mesh,
        in_specs=placed,
        out_specs=(P("layer", "tile", None), P("tile", "layer")),
        check_vma=False,
    )
```

profile of v0, /device:TPU:1, one launch (start us, length us, event | category | flops | bytes accessed | tf_op | source)
XLA Modules:
  0.0 1022.1 jit_solution(11896485293692213495)
XLA Ops:
  11.7 17.8 %fusion.107 = (f32[1,2,64,512]{3,2,1,0:T(8,128)S(1)}, f32[2,64,512]{2,1,0:T(8,128)S(1)}, f32[2,64,512]{2,1,0:T(8,128)S(1)}, pred[2,64,512]{2,1,0:T(8,128)(4,1)S(...) fusion(f32[2,64,512]{2,1,0:T(8,128)} %param.17, ...), kind=kLoop, calls=%fused_computation.316 | loop fusion | flops 2555904 | bytes 2097248 | tf_op jit(solution)/shard_map/stack | solution.py:152
  29.7 8.8 collective-permute-start.1
  42.8 3.2 collective-permute-start.4
  48.9 4.0 collective-permute-start.6
  54.3 4.0 collective-permute-start.2
  59.4 4.3 collective-permute-done.3
  66.3 8.5 add_add_fusion.1
  75.8 106.2 %all-gather.2.cloned.1.call-done = f32[2048,128]{1,0:T(8,128)} async-done(((f32[16,128]{1,0:T(8,128)}), f32[2048,128]{1,0:T(8,128)}) %all-gather.2.cloned.1.call-update) | async-done | bytes 1048592 | tf_op jit(solution)/shard_map/all_gather | solution.py:122
  185.7 171.3 %scatter_custom_fusion.1 = f32[32768]{0:T(1024)S(1)} fusion(s32[32768]{0:T(1024)} %bitcast.101, f32[32768]{0:T(1024)S(1)} %get-tuple-element.136, f32[]{:T(128)} %constant.189.clone.1), kind=kCustom, calls=%fused_computation.302 | custom fusion | flops 32768 | bytes 131584 | tf_op jit(solution)/shard_map/scatter-add | solution.py:130
  358.6 171.2 %scatter_custom_fusion = f32[32768]{0:T(1024)S(1)} fusion(s32[32768]{0:T(1024)} %bitcast.102, f32[32768]{0:T(1024)} %get-tuple-element.134, f32[]{:T(128)} %constant.189.clone.1), kind=kCustom, calls=%fused_computation.304 | custom fusion | flops 32768 | bytes 131584 | tf_op jit(solution)/shard_map/scatter-add | solution.py:135
  536.2 3.4 collective-permute-start.8
  541.7 4.0 collective-permute-start.10
  552.1 3.7 collective-permute-start.12
  557.9 4.7 collective-permute-start.14
  569.1 4.2 collective-permute-start.20
  575.3 3.6 collective-permute-start.16
  581.2 4.7 collective-permute-start.18
  587.2 4.4 collective-permute-start.22
  599.9 5.4 collective-permute-start.24
  607.4 4.7 collective-permute-start.26
  617.0 5.8 collective-permute-start.28
  625.5 4.7 collective-permute-start.30
  633.9 72.3 %all-reduce.10.cloned.1.call-done = f32[64,512]{1,0:T(8,128)} async-done(((f32[64,512]{1,0:T(8,128)}), f32[64,512]{1,0:T(8,128)}) %all-reduce.10.cloned.1.call-update) | async-done | bytes 131088 | tf_op jit(solution)/shard_map/psum | solution.py:38
  706.3 54.5 %while.15 = (s32[]{:T(128)}, f32[16,512]{1,0:T(8,128)S(1)}, s32[16,512]{1,0:T(8,128)S(1)}, f32[64,512]{1,0:T(8,128)}, s32[]{:T(128)}, /*index=5*/s32[]{:T(128)}) while((s32[]{:T(128)}, f32[16,512]{1,0:T(8,128)S(1)}, s32[16,512]{1,0:T(8,128)S(1)}, f32[64,512]{1,0:T(8,128)}, s32[]{:T(128)}, /*index=5*/s32[]{:T(128)}) %tuple.130), condition=%wide.region_5.6_spmd.clone, body=%wide.region_3.5_spmd.clone.sunk | while | flops 1074690 | bytes 3175509 | solution.py:92
  706.3 3.0 gather_fusion
  709.8 2.9 gather_fusion
  713.2 2.9 gather_fusion
  716.6 2.9 gather_fusion
  720.0 2.9 gather_fusion
  737.0 2.9 gather_fusion
  740.4 2.9 gather_fusion
  763.5 252.1 %reduce-scatter.2.cloned.1.call-done = f32[16,32]{1,0:T(8,128)} async-done(((f32[2048,32]{1,0:T(8,128)}), f32[16,32]{1,0:T(8,128)}) %reduce-scatter.2.cloned.1.call-update) | async-done | bytes 2064 | tf_op jit(solution)/shard_map/reduce_scatter | solution.py:174
  (283 shorter events, 108.7 us)
Async XLA Ops:
  7.2 174.8 %all-gather.2.cloned.1.call-start = ((), (), s32[]{:S(2)}) async-start(), calls=%async_computation.1 | async-start | bytes 1056768 | tf_op jit(solution)/shard_map/all_gather | solution.py:122
  29.7 23.2 %collective-permute-start.1 = (f32[2,2,1,512]{3,2,1,0:T(1,128)S(1)}, f32[2,2,1,512]{3,2,1,0:T(1,128)S(1)}, u32[]{:S(2)}, u32[]{:S(2)}) collective-permute-start(f32[2,2,1,512]{3,2,1,0:T(1,128)S(1)} %get-tuple-element.168), channel_id=1, source_target_pairs={{4,0},{8,4},{12,8},{16,12},{20,16},{24,20},{28,24},{32,28},{36,32}... | collective-permute-start | bytes 24584 | tf_op jit(solution)/shard_map/ppermute | solution.py:31
  38.5 14.4 %collective-permute-start = (f32[2,2,1,512]{3,2,1,0:T(1,128)S(1)}, f32[2,2,1,512]{3,2,1,0:T(1,128)S(1)}, u32[]{:S(2)}, u32[]{:S(2)}) collective-permute-start(f32[2,2,1,512]{3,2,1,0:T(1,128)S(1)} %get-tuple-element.167), channel_id=1, source_target_pairs={{0,4},{4,8},{8,12},{12,16},{16,20},{20,24},{24,28},{28,32},{32,36}... | collective-permute-start | bytes 24584 | tf_op jit(solution)/shard_map/ppermute | solution.py:28
  40.4 7.1 collective-permute-start.5
  42.8 4.7 collective-permute-start.4
  46.0 660.2 %all-reduce.10.cloned.1.call-start = ((), (), s32[]{:S(2)}) async-start(), calls=%async_computation.2 | async-start | bytes 262144 | tf_op jit(solution)/shard_map/psum | solution.py:38
  47.6 11.5 %collective-permute-start.7 = (f32[1,66,512]{2,1,0:T(8,128)S(1)}, f32[1,66,512]{2,1,0:T(8,128)S(1)}, u32[]{:S(2)}, u32[]{:S(2)}) collective-permute-start(f32[1,66,512]{2,1,0:T(8,128)S(1)} %get-tuple-element.180), channel_id=1, source_target_pairs={{1,0},{2,1},{3,2},{5,4},{6,5},{7,6},{9,8},{10,9},{11,10},{13,12},{... | collective-permute-start | bytes 405512 | tf_op jit(solution)/shard_map/ppermute | solution.py:31
  48.9 10.3 %collective-permute-start.6 = (f32[1,66,512]{2,1,0:T(8,128)S(1)}, f32[1,66,512]{2,1,0:T(8,128)S(1)}, u32[]{:S(2)}, u32[]{:S(2)}) collective-permute-start(f32[1,66,512]{2,1,0:T(8,128)S(1)} %get-tuple-element.179), channel_id=1, source_target_pairs={{0,1},{1,2},{2,3},{4,5},{5,6},{6,7},{8,9},{9,10},{10,11},{12,13},{... | collective-permute-start | bytes 405512 | tf_op jit(solution)/shard_map/ppermute | solution.py:28
  53.0 10.6 %collective-permute-start.3 = (f32[2,1,66,512]{3,2,1,0:T(8,128)S(1)}, f32[2,1,66,512]{3,2,1,0:T(8,128)S(1)}, u32[]{:S(2)}, u32[]{:S(2)}) collective-permute-start(f32[2,1,66,512]{3,2,1,0:T(8,128)S(1)} %get-tuple-element.164), channel_id=1, source_target_pairs={{1,0},{2,1},{3,2},{5,4},{6,5},{7,6},{9,8},{10,9},{11,10},{13,12},{... | collective-permute-start | bytes 811016 | tf_op jit(solution)/shard_map/ppermute | solution.py:31
  54.3 10.3 %collective-permute-start.2 = (f32[2,1,66,512]{3,2,1,0:T(8,128)S(1)}, f32[2,1,66,512]{3,2,1,0:T(8,128)S(1)}, u32[]{:S(2)}, u32[]{:S(2)}) collective-permute-start(f32[2,1,66,512]{3,2,1,0:T(8,128)S(1)} %get-tuple-element.163), channel_id=1, source_target_pairs={{0,1},{1,2},{2,3},{4,5},{5,6},{6,7},{8,9},{9,10},{10,11},{12,13},{... | collective-permute-start | bytes 811016 | tf_op jit(solution)/shard_map/ppermute | solution.py:28
  534.0 5.6 collective-permute-start.9
  540.4 7.0 collective-permute-start.11
  541.7 7.5 collective-permute-start.10
  550.0 5.8 collective-permute-start.13
  556.6 7.2 collective-permute-start.15
  557.9 7.6 collective-permute-start.14
  567.2 11.8 %collective-permute-start.21 = (f32[2,1,512]{2,1,0:T(1,128)S(1)}, f32[2,1,512]{2,1,0:T(1,128)S(1)}, u32[]{:S(2)}, u32[]{:S(2)}) collective-permute-start(f32[2,1,512]{2,1,0:T(1,128)S(1)} %get-tuple-element.186), channel_id=1, source_target_pairs={{4,0},{8,4},{12,8},{16,12},{20,16},{24,20},{28,24},{32,28},{36,32}... | collective-permute-start | bytes 12296 | tf_op jit(solution)/shard_map/ppermute | solution.py:31
  569.1 9.9 collective-permute-start.20
  573.4 5.6 collective-permute-start.17
  579.9 15.6 %collective-permute-start.19 = (f32[2,1,66,512]{3,2,1,0:T(8,128)S(1)}, f32[2,1,66,512]{3,2,1,0:T(8,128)S(1)}, u32[]{:S(2)}, u32[]{:S(2)}) collective-permute-start(f32[2,1,66,512]{3,2,1,0:T(8,128)S(1)} %get-tuple-element.162), channel_id=1, source_target_pairs={{1,0},{2,1},{3,2},{5,4},{6,5},{7,6},{9,8},{10,9},{11,10},{13,12},{... | collective-permute-start | bytes 811016 | tf_op jit(solution)/shard_map/ppermute | solution.py:31
  581.2 14.3 %collective-permute-start.18 = (f32[2,1,66,512]{3,2,1,0:T(8,128)S(1)}, f32[2,1,66,512]{3,2,1,0:T(8,128)S(1)}, u32[]{:S(2)}, u32[]{:S(2)}) collective-permute-start(f32[2,1,66,512]{3,2,1,0:T(8,128)S(1)} %get-tuple-element.161), channel_id=1, source_target_pairs={{0,1},{1,2},{2,3},{4,5},{5,6},{6,7},{8,9},{9,10},{10,11},{12,13},{... | collective-permute-start | bytes 811016 | tf_op jit(solution)/shard_map/ppermute | solution.py:28
  585.9 7.4 collective-permute-start.23
  587.2 7.9 collective-permute-start.22
  598.0 7.4 collective-permute-start.25
  599.9 6.1 collective-permute-start.24
  606.1 6.6 collective-permute-start.27
  607.4 6.8 collective-permute-start.26
  615.0 7.8 collective-permute-start.29
  617.0 6.6 collective-permute-start.28
  624.3 6.8 collective-permute-start.31
  625.5 6.8 collective-permute-start.30
  633.8 381.7 %reduce-scatter.2.cloned.1.call-start = ((), (), s32[]{:S(2)}) async-start(), calls=%async_computation.3 | async-start | bytes 1056768 | tf_op jit(solution)/shard_map/reduce_scatter | solution.py:174
  (27 other events, 535.7 us)
Sparse Core Ops, SparseCore 0:
  46.1 135.7 all-gather.1
  634.0 72.2 all-reduce.9
  763.6 251.9 reduce-scatter.1
where the time goes:
time: 1030 us; the launch traced here: 1020 us
  waiting for transfers between devices  453 us (44%)
  other arithmetic  393 us (38%)
  starting transfers between devices  100 us (10%)
  local copies, waits for them, and re-layouts  59.6 us (6%)
  between operations  14.7 us (1%)
    reduce_scatter x1, waiting for transfers between devices, on_device(): inflow = lax.psum_scatter(dense, 'tile', scatter_dimension=0, tiled=True)  252 us
    scatter-add x1, other arithmetic, on_device(): diag_top = jnp.zeros((across * breadth,), jnp.float32).at[flat_index.resh...  171 us
    scatter-add x1, other arithmetic, on_device(): rhs_top = jnp.zeros((across * breadth,), jnp.float32).at[flat_index.resha...  171 us
    all_gather x1, waiting for transfers between devices, on_device(): whole_section = lax.all_gather(section, 'tile', axis=0, tiled=True)  106 us
    psum x1, waiting for transfers between devices, from_root(): return lax.psum(kept, axis)  72.3 us
    ppermute x16, starting transfers between devices, with_halo(): lax.ppermute(lax.slice_in_dim(block, block.shape[dim] - width, None, axis...  66.7 us
    gather x16, local copies, waits for them, and re-layouts, one_group(): picked_rows = jnp.take(top_head, flat_cells // breadth, axis=0)  47 us
    ppermute x16, starting transfers between devices, with_halo(): lax.ppermute(lax.slice_in_dim(block, 0, width, axis=dim), axis, backward)  33.5 us
  transfers between devices with their start and end apart: 35, of which 20 were waited for; matrix products, arithmetic and copies ran while one was open for 1% of the time, Pallas kernels for 0%

commit v1 on v0

v1 whole, which is shorter than its diff:
```python
import jax
import jax.numpy as jnp
from jax import lax
from jax.experimental import pallas as pl
from jax.experimental.pallas import tpu as pltpu
from jax.sharding import PartitionSpec as P

ITERS = 2
SWEEPS = 3
GHOST = ITERS * SWEEPS


LATERAL = 1.0
VERTICAL = 2.0
GRAVITY = 1.0
NEIGHBOURS = (
    (0, -1, VERTICAL),
    (0, 1, VERTICAL),
    (1, -1, LATERAL),
    (1, 1, LATERAL),
    (2, -1, LATERAL),
    (2, 1, LATERAL),
)
CHUNK = 512


def beside(padded, axis_id, step):
    spans = [slice(1, -1), slice(1, -1), slice(1, -1)]
    spans[axis_id] = slice(1 + step, padded.shape[axis_id] - 1 + step)
    return padded[tuple(spans)]


def neighbor_weights(cond_pad, open_pad):
    centre = cond_pad[1:-1, 1:-1, 1:-1]
    centre_open = open_pad[1:-1, 1:-1, 1:-1]
    result = []
    for axis_id, step, factor in NEIGHBOURS:
        far = beside(cond_pad, axis_id, step)
        far_open = beside(open_pad, axis_id, step)
        result.append(factor * 2.0 * centre_open * far_open / (centre + far))
    return result


def relax(head_pad, weights, store, head_old, riv_diag, riv_rhs):
    total = store * head_old
    diagonal_sum = store
    for weight, (axis_id, step, factor) in zip(weights, NEIGHBOURS):
        total = total + weight * beside(head_pad, axis_id, step)
        diagonal_sum = diagonal_sum + weight
    total = total + GRAVITY * (weights[0] - weights[1]) + riv_rhs
    return total / (diagonal_sum + riv_diag)


def lookup(values_table, classes):
    result = jnp.zeros(classes.shape, jnp.float32)
    for class_id in range(values_table.shape[0]):
        result = jnp.where(classes == class_id, values_table[class_id], result)
    return result


def split3(value):
    high = value.astype(jnp.bfloat16).astype(jnp.float32)
    rest = value - high
    middle = rest.astype(jnp.bfloat16).astype(jnp.float32)
    low = rest - middle
    return high, middle, low


def scatter_kernel(rows_ref, cols_ref, diag_in_ref, rhs_in_ref, diag_ref, rhs_ref, acc_ref):
    step = pl.program_id(0)
    grid_rows, breadth = diag_ref.shape
    chunk = rows_ref.shape[1]

    @pl.when(step == 0)
    def _():
        acc_ref[...] = jnp.zeros_like(acc_ref)

    rows = rows_ref[...]

    @pl.when(jnp.max(rows) >= 0)
    def _():
        hit = lax.broadcasted_iota(jnp.int32, (grid_rows, chunk), 0) == rows
        pieces = []
        for value in (diag_in_ref[...], rhs_in_ref[...]):
            for piece in split3(value):
                pieces.append(jnp.where(hit, piece, 0.0).astype(jnp.bfloat16))
        left = jnp.concatenate(pieces, axis=0)
        cols = cols_ref[...]
        column_hit = lax.broadcasted_iota(jnp.int32, (breadth, chunk), 0) == cols
        right = jnp.where(column_hit, 1.0, 0.0).astype(jnp.bfloat16)
        acc_ref[...] += lax.dot_general(
            left, right, (((1,), (1,)), ((), ())), preferred_element_type=jnp.float32
        )

    @pl.when(step == pl.num_programs(0) - 1)
    def _():
        acc = acc_ref[...]
        g = grid_rows
        diag_ref[...] = acc[0:g] + acc[g : 2 * g] + acc[2 * g : 3 * g]
        rhs_ref[...] = acc[3 * g : 4 * g] + acc[4 * g : 5 * g] + acc[5 * g : 6 * g]


def river_terms(rows, cols, diag_values, rhs_values, grid_rows, breadth):
    count = rows.shape[1]
    lane = pl.BlockSpec((1, CHUNK), lambda i: (0, i))
    whole = pl.BlockSpec((grid_rows, breadth), lambda i: (0, 0))
    return pl.pallas_call(
        scatter_kernel,
        grid=(count // CHUNK,),
        in_specs=[lane, lane, lane, lane],
        out_specs=[whole, whole],
        out_shape=[
            jax.ShapeDtypeStruct((grid_rows, breadth), jnp.float32),
            jax.ShapeDtypeStruct((grid_rows, breadth), jnp.float32),
        ],
        scratch_shapes=[pltpu.VMEM((6 * grid_rows, breadth), jnp.float32)],
        cost_estimate=pl.CostEstimate(
            flops=2 * 6 * grid_rows * breadth * count,
            transcendentals=0,
            bytes_accessed=16 * count + 8 * grid_rows * breadth,
        ),
    )(rows, cols, diag_values, rhs_values)


def gather_kernel(top_ref, rows_ref, cols_ref, out_ref):
    grid_rows, breadth = top_ref.shape
    chunk = rows_ref.shape[1]
    stacked = jnp.concatenate(
        [piece.astype(jnp.bfloat16) for piece in split3(top_ref[...])], axis=0
    )
    cols = cols_ref[...]
    column_hit = lax.broadcasted_iota(jnp.int32, (breadth, chunk), 0) == cols
    right = jnp.where(column_hit, 1.0, 0.0).astype(jnp.bfloat16)
    picked = jnp.dot(stacked, right, preferred_element_type=jnp.float32)
    g = grid_rows
    by_row = picked[0:g] + picked[g : 2 * g] + picked[2 * g : 3 * g]
    rows = rows_ref[...]
    hit = lax.broadcasted_iota(jnp.int32, (grid_rows, chunk), 0) == rows
    out_ref[...] = jnp.sum(jnp.where(hit, by_row, 0.0), axis=0, keepdims=True)


def node_heads(top, rows, cols):
    grid_rows, breadth = top.shape
    count = rows.shape[1]
    lane = pl.BlockSpec((1, CHUNK), lambda i: (0, i))
    return pl.pallas_call(
        gather_kernel,
        grid=(count // CHUNK,),
        in_specs=[pl.BlockSpec((grid_rows, breadth), lambda i: (0, 0)), lane, lane],
        out_specs=lane,
        out_shape=jax.ShapeDtypeStruct((1, count), jnp.float32),
        cost_estimate=pl.CostEstimate(
            flops=2 * 3 * grid_rows * breadth * count,
            transcendentals=0,
            bytes_accessed=12 * count + 4 * grid_rows * breadth,
        ),
    )(top, rows, cols)


def with_ghost(block, axis, dim, width):
    count = lax.axis_size(axis)
    forward = [(i, i + 1) for i in range(count - 1)]
    backward = [(i + 1, i) for i in range(count - 1)]
    size = block.shape[dim]
    above = lax.ppermute(lax.slice_in_dim(block, size - width, size, axis=dim), axis, forward)
    below = lax.ppermute(lax.slice_in_dim(block, 0, width, axis=dim), axis, backward)
    return jnp.concatenate([above, block, below], axis=dim)


def on_device(
    head_start,
    soil_class,
    land_mask,
    ks_table,
    alpha_table,
    store_table,
    section,
    cross_owner,
    cross_local,
    node_cell,
    bed_cond,
):
    own_layers, across, breadth = head_start.shape
    reach_rows, node_count = section.shape
    tile_count = lax.axis_size("tile")
    layer_count = lax.axis_size("layer")
    tile = lax.axis_index("tile")
    layer = lax.axis_index("layer")
    quarter = node_count // layer_count
    node_first = layer * quarter

    planes = jnp.concatenate(
        [head_start, soil_class.astype(jnp.float32), land_mask.astype(jnp.float32)[None]], axis=0
    )
    planes = with_ghost(planes, "tile", 1, GHOST)
    extent = across + 2 * GHOST
    fields = planes[: 2 * own_layers].reshape(2, own_layers, extent, breadth)
    fields = lax.all_gather(fields, "layer", axis=1, tiled=True)
    global_row = tile * across - GHOST + lax.broadcasted_iota(jnp.int32, (1, extent, 1), 1)
    inside = (global_row >= 0) & (global_row < tile_count * across)
    head_old = jnp.where(inside, fields[0], 0.0)
    classes = fields[1].astype(jnp.int32)
    ks_here = jnp.where(inside, lookup(ks_table, classes), 1.0)
    alpha_here = jnp.where(inside, lookup(alpha_table, classes), 0.0)
    store_here = jnp.where(inside, lookup(store_table, classes), 1.0)
    land_here = jnp.where(inside, planes[2 * own_layers][None], 0.0)

    owners = cross_owner[0]
    positions = cross_local[0]
    node_cells = node_cell[0]
    bed_given = bed_cond[0]
    slots = owners.shape[0]
    per_owner = slots // tile_count
    order = jnp.arange(slots, dtype=jnp.int32)
    same = owners[:, None] == owners[None, :]
    rank = jnp.sum((same & (order[None, :] < order[:, None])).astype(jnp.int32), axis=1)
    place = owners * per_owner + rank
    at_place = place[None, :] == order[:, None]
    wanted = jnp.sum(jnp.where(at_place, positions[None, :], 0), axis=1)
    asked = lax.all_to_all(wanted, "tile", 0, 0, tiled=True)
    reply = jnp.take(section, asked, axis=0)
    sorted_section = lax.all_to_all(reply, "tile", 0, 0, tiled=True)
    slot_section = jnp.take(sorted_section, place, axis=0)

    in_tile = node_cells >= 0
    bed_terms = jnp.where(in_tile, bed_given, 0.0)
    cell_rows = jnp.where(in_tile, node_cells // breadth, -1)
    cell_cols = jnp.where(in_tile, node_cells % breadth, 0)
    top_diag, top_rhs = river_terms(
        cell_rows.reshape(1, -1),
        cell_cols.reshape(1, -1),
        bed_terms.reshape(1, -1),
        (bed_terms * slot_section).reshape(1, -1),
        across,
        breadth,
    )
    river = with_ghost(jnp.stack([top_diag, top_rhs]), "tile", 1, GHOST)
    layers = head_old.shape[0]
    riv_diag = jnp.pad(river[0][None], ((0, layers - 1), (0, 0), (0, 0)))
    riv_rhs = jnp.pad(river[1][None], ((0, layers - 1), (0, 0), (0, 0)))

    head = head_old
    for picard in range(ITERS):
        conduct = ks_here * jnp.exp(alpha_here * jnp.minimum(head, 0.0))
        cond_pad = jnp.pad(conduct, 1)
        open_pad = jnp.pad(conduct * land_here, 1)
        weights = neighbor_weights(cond_pad, open_pad)
        for sweep in range(SWEEPS):
            head = relax(jnp.pad(head, 1), weights, store_here, head_old, riv_diag, riv_rhs)
    kept = lax.dynamic_slice_in_dim(head[:, GHOST : GHOST + across], layer * own_layers, own_layers, 0)

    top_head = head[0, GHOST : GHOST + across]
    my_cells = lax.dynamic_slice_in_dim(node_cells, node_first, quarter, 1)
    my_bed = lax.dynamic_slice_in_dim(bed_given, node_first, quarter, 1)
    my_section = lax.dynamic_slice_in_dim(slot_section, node_first, quarter, 1)
    my_inside = my_cells >= 0
    picked = node_heads(
        top_head,
        jnp.where(my_inside, my_cells // breadth, -1).reshape(1, -1),
        jnp.where(my_inside, my_cells % breadth, 0).reshape(1, -1),
    ).reshape(slots, quarter)
    slot_in = jnp.where(my_inside, my_bed * (picked - my_section), 0.0)
    sorted_in = jnp.take(slot_in, jnp.sum(jnp.where(at_place, order[None, :], 0), axis=1), axis=0)
    arrived = lax.all_to_all(sorted_in, "tile", 0, 0, tiled=True)
    target = asked[None, :] == jnp.arange(reach_rows, dtype=jnp.int32)[:, None]
    inflow = jnp.sum(jnp.where(target[:, :, None], arrived[None], 0.0), axis=1)
    return (kept, inflow)


def solution(mesh):
    placed = (
        P("layer", "tile", None),
        P("layer", "tile", None),
        P("tile", None),
        P(),
        P(),
        P(),
        P("tile", None),
        P("tile", None),
        P("tile", None),
        P("tile", None, None),
        P("tile", None, None),
    )
    return jax.shard_map(
        on_device,
        mesh=mesh,
        in_specs=placed,
        out_specs=(P("layer", "tile", None), P("tile", "layer")),
        check_vma=False,
    )
```

time: 1030 us -> 275 us (0.27)
  waiting for transfers between devices: 453 us -> 32.4 us
  other arithmetic: 393 us -> 101 us
  Pallas kernels: 0 us -> 50.1 us
  local copies, waits for them, and re-layouts: 59.6 us -> 11.2 us
  starting transfers between devices: 100 us -> 63 us
    scatter-add x3 -> x0, other arithmetic: 345 us -> none  [the longest x1 171 us: on_device(): diag_top = jnp.zeros((across * breadth,), jnp.float32).at[flat_index.resh...]
    reduce_scatter x1 -> x0, waiting for transfers between devices: 252 us -> none  [on_device(): inflow = lax.psum_scatter(dense, 'tile', scatter_dimension=0, tiled=True)]
    all_gather x1, waiting for transfers between devices: 106 us -> 0.02 us  [on_device(): fields = lax.all_gather(fields, 'layer', axis=1, tiled=True)]
    ppermute x32 -> x4, starting transfers between devices: 100 us -> 12.3 us  [the longest x2 7.59 us: with_ghost(): lax.ppermute(lax.slice_in_dim(block, 0, width, axis=dim), axis, backward)]
    psum x1 -> x0, waiting for transfers between devices: 72.3 us -> none  [from_root(): return lax.psum(kept, axis)]
    div x5, other arithmetic: 1.18 us -> 58.7 us  [relax(): return total / (diagonal_sum + riv_diag)]
    all_to_all x0 -> x3, starting transfers between devices: none -> 50.7 us  [the longest x1 20.4 us: on_device(): asked = lax.all_to_all(wanted, 'tile', 0, 0, tiled=True)]
    pallas_call x0 -> x2, Pallas kernels: none -> 50.1 us  [the longest x1 40.5 us: river_terms(): pl.pallas_call(scatter_kernel, grid=(count // CHUNK,), in_specs=[lane, la...]
  transfers between devices with their start and end apart: 35 -> 8, of which waited for: 20 -> 4; matrix products, arithmetic and copies ran while one was open for 1% -> 6% of each run, Pallas kernels for 0% -> 15%
where the time goes in v1:
time: 275 us; the launch traced here: 272 us
  other arithmetic  101 us (37%)
  starting transfers between devices  63 us (23%)
  Pallas kernels  50.1 us (18%)
  waiting for transfers between devices  32.4 us (12%)
  between operations  14.6 us (5%)
  local copies, waits for them, and re-layouts  11.2 us (4%)
    div x5, other arithmetic, relax(): return total / (diagonal_sum + riv_diag)  58.7 us
    pallas_call x1, Pallas kernels, river_terms(): pl.pallas_call(scatter_kernel, grid=(count // CHUNK,), in_specs=[lane, la...  40.5 us
    mul x3, other arithmetic, on_device(): open_pad = jnp.pad(conduct * land_here, 1)  27.1 us
    all_to_all x1, starting transfers between devices, on_device(): asked = lax.all_to_all(wanted, 'tile', 0, 0, tiled=True)  20.4 us
    all_to_all x1, starting transfers between devices, on_device(): sorted_section = lax.all_to_all(reply, 'tile', 0, 0, tiled=True)  16.1 us
    all_to_all x1, waiting for transfers between devices, on_device(): arrived = lax.all_to_all(sorted_in, 'tile', 0, 0, tiled=True)  15.1 us
    all_to_all x1, waiting for transfers between devices, on_device(): sorted_section = lax.all_to_all(reply, 'tile', 0, 0, tiled=True)  14.5 us
    all_to_all x1, starting transfers between devices, on_device(): arrived = lax.all_to_all(sorted_in, 'tile', 0, 0, tiled=True)  14.2 us
  transfers between devices with their start and end apart: 8, of which 4 were waited for; matrix products, arithmetic and copies ran while one was open for 6% of the time, Pallas kernels for 15%

profile of v1, /device:TPU:1, one launch (start us, length us, event | category | flops | bytes accessed | tf_op | source)
XLA Modules:
  0.0 271.9 jit_solution(5701514721085481819)
XLA Ops:
  7.2 1.0 convert_reduce_fusion
  8.9 0.8 select_reduce_fusion.1
  10.5 20.4 %all-to-all-start = ((s32[128,2,1]{1,2,0:T(1,128)}), s32[128,2,1]{1,2,0:T(1,128)S(1)}, u32[]{:S(2)}, u32[]{:S(2)}) async-start(s32[128,2,1]{1,2,0:T(1,128)} %bitcast.49), calls=%async_computation | async-start | bytes 131072 | tf_op jit(solution)/shard_map/all_to_all | solution.py:220
  30.9 0.9 convert_bitcast_fusion
  31.8 1.0 convert_element_type.27
  33.6 2.8 %collective-permute-start.1 = (f32[5,6,512]{2,1,0:T(8,128)S(1)}, f32[5,6,512]{2,1,0:T(8,128)S(1)}, u32[]{:S(2)}, u32[]{:S(2)}) collective-permute-start(f32[5,6,512]{2,1,0:T(8,128)S(1)} %get-tuple-element.49), channel_id=1, source_target_pairs={{4,0},{8,4},{12,8},{16,12},{20,16},{24,20},{28,24},{32,28},{36,32}... | collective-permute-start | bytes 184328 | tf_op jit(solution)/shard_map/ppermute | solution.py:166
  36.4 2.8 %collective-permute-start = (f32[5,6,512]{2,1,0:T(8,128)S(1)}, f32[5,6,512]{2,1,0:T(8,128)S(1)}, u32[]{:S(2)}, u32[]{:S(2)}) collective-permute-start(f32[5,6,512]{2,1,0:T(8,128)S(1)} %get-tuple-element.48), channel_id=1, source_target_pairs={{0,4},{4,8},{8,12},{12,16},{16,20},{20,24},{24,28},{28,32},{32,36}... | collective-permute-start | bytes 184328 | tf_op jit(solution)/shard_map/ppermute | solution.py:165
  39.2 1.7 fusion.123
  43.2 0.9 compare_select_fusion.8
  44.1 1.6 all-to-all-done
  48.0 0.9 broadcast_select_fusion.1
  48.9 16.1 %all-to-all-start.1 = ((f32[128,2,128]{2,1,0:T(2,128)}), f32[128,2,128]{2,1,0:T(2,128)S(1)}, u32[]{:S(2)}, u32[]{:S(2)}) async-start(f32[128,2,128]{2,1,0:T(2,128)} %broadcast_select_fusion.1), calls=%async_computation.1 | async-start | bytes 262144 | tf_op jit(solution)/shard_map/all_to_all | solution.py:222
  65.5 0.9 slice.442
  66.5 14.5 %all-to-all-done.1 = f32[128,2,128]{2,1,0:T(2,128)S(1)} async-done(((f32[128,2,128]{2,1,0:T(2,128)}), f32[128,2,128]{2,1,0:T(2,128)S(1)}, u32[]{:S(2)}, u32[]{:S(2)}) %all-to-all-start.1) | async-done | bytes 131104 | tf_op jit(solution)/shard_map/all_to_all | solution.py:222
  81.8 1.0 fusion.140
  82.8 40.5 %shard_map.122 = (f32[64,512]{1,0:T(8,128)}, f32[64,512]{1,0:T(8,128)}) custom-call(s32[1,32768]{1,0:T(1,128)} %get-tuple-element.55.rows_ref, s32[1,32768]{1,0:T(1,128)} %get-tuple-element.54.cols_ref, f32[1,32768]{1,0:T(1,128)} %get-tuple-element.47.diag_in_ref, f32[1,32768]{1,0:T(1,128)} %get-tuple-element.46.rhs_in_ref), custom_call_target="tpu_custom_call" | custom-call | flops 12884901888 | bytes 786432 | tf_op jit(solution)/shard_map/pallas_call | solution.py:107
  124.2 4.8 %collective-permute-start.3 = (f32[2,6,512]{2,1,0:T(8,128)S(1)}, f32[2,6,512]{2,1,0:T(8,128)S(1)}, u32[]{:S(2)}, u32[]{:S(2)}) collective-permute-start(f32[2,6,512]{2,1,0:T(8,128)S(1)} %get-tuple-element.53), channel_id=1, source_target_pairs={{4,0},{8,4},{12,8},{16,12},{20,16},{24,20},{28,24},{32,28},{36,32}... | collective-permute-start | bytes 73736 | tf_op jit(solution)/shard_map/ppermute | solution.py:166
  129.0 1.9 collective-permute-start.2
  131.0 1.1 collective-permute-done.2
  132.2 22.6 %broadcast_multiply_fusion.1 = (f32[8,76,512]{2,1,0:T(8,128)}, f32[8,76,512]{2,1,0:T(8,128)}, f32[8,76,512]{2,1,0:T(8,128)}, f32[8,76,512]{2,1,0:T(8,128)}, f32[...) fusion(f32[76,512]{1,0:T(8,128)S(1)} %fusion.122, ...), kind=kLoop, calls=%fused_computation.201 | loop fusion | flops 13697024 | bytes 12607660 | tf_op jit(solution)/shard_map/mul | solution.py:246
  154.7 26.8 %fusion.115 = (f32[8,76,512]{2,1,0:T(8,128)}, f32[8,76,512]{2,1,0:T(8,128)S(1)}, f32[8,76,512]{2,1,0:T(8,128)S(1)}, f32[8,76,512]{2,1,0:T(8,128)}, f32[8,76,512]...) fusion(f32[1,76,512]{2,1,0:T(8,128)S(1)} %get-tuple-element.51,, ...), kind=kLoop, calls=%fused_computation.193 | loop fusion | flops 17743872 | bytes 20234364 | tf_op jit(solution)/shard_map/div | solution.py:51
  181.6 8.4 %fusion.116 = f32[8,76,512]{2,1,0:T(8,128)S(1)} fusion(f32[1,76,512]{2,1,0:T(8,128)S(1)} %get-tuple-element.51, f32[8,76,512]{2,1,0:T(8,128)} %get-tuple-element.26, f32[8,76,512]{2,1,0:T(8,128)} %get-tuple-element.25, f32[8,76,512]{2,1,0:T(8,128)} %get-tuple-element.19, f32[8,76,512]{2,1,0:T(8,128)} %get-tuple-element.24, ...), kind=kLoop, calls=%fused_computation.194 | loop fusion | flops 6848512 | bytes 14008320 | tf_op jit(solution)/shard_map/div | solution.py:51
  190.8 4.4 %broadcast_multiply_fusion = (f32[8,76,512]{2,1,0:T(8,128)}, f32[8,76,512]{2,1,0:T(8,128)}, f32[8,76,512]{2,1,0:T(8,128)}) fusion(f32[76,512]{1,0:T(8,128)S(1)} %fusion.122, f32[8,76,512]{2,1,0:T(8,128)S(1)} %copy-done.13, f32[8,76,512]{2,1,0:T(8,128)S(1)} %copy-done.12, f32[1,76,512]{2,1,0:T(8,128)S(1)} %get-tuple-element.50, ...), kind=kLoop, calls=%fused_computation.200 | loop fusion | flops 8093696 | bytes 19144704 | tf_op jit(solution)/shard_map/mul | solution.py:246
  195.2 14.3 %fusion.118 = (f32[8,76,512]{2,1,0:T(8,128)}, f32[8,76,512]{2,1,0:T(8,128)S(1)}, f32[8,76,512]{2,1,0:T(8,128)S(1)}, f32[8,76,512]{2,1,0:T(8,128)S(1)}, f32[8,76,...) fusion(f32[1,76,512]{2,1,0:T(8,128)S(1)} %get-tuple-element.51, ...), kind=kLoop, calls=%fused_computation.196 | loop fusion | flops 13385728 | bytes 16498688 | tf_op jit(solution)/shard_map/div | solution.py:51
  209.6 6.4 %fusion.119 = f32[8,76,512]{2,1,0:T(8,128)S(1)} fusion(f32[1,76,512]{2,1,0:T(8,128)S(1)} %get-tuple-element.51, f32[8,76,512]{2,1,0:T(8,128)} %get-tuple-element.13, f32[8,76,512]{2,1,0:T(8,128)} %get-tuple-element.12, f32[8,76,512]{2,1,0:T(8,128)} %get-tuple-element.8, f32[8,76,512]{2,1,0:T(8,128)S(1)} %get-tuple-element.11, ...), kind=kLoop, calls=%fused_computation.197 | loop fusion | flops 6848512 | bytes 14008320 | tf_op jit(solution)/shard_map/div | solution.py:51
  216.0 2.8 %fusion.120 = f32[8,76,512]{2,1,0:T(8,128)S(1)} fusion(f32[1,76,512]{2,1,0:T(8,128)S(1)} %get-tuple-element.51, f32[8,76,512]{2,1,0:T(8,128)S(1)} %copy-done.2, f32[8,76,512]{2,1,0:T(8,128)S(1)} %copy-done.1, f32[8,76,512]{2,1,0:T(8,128)S(1)} %fusion.119, f32[8,76,512]{2,1,0:T(8,128)S(1)} %get-tuple-element.11, f32[8,76,512]{2,1,0:T(8,128)S(1)} %get-tuple-element.10, ...), kind=kLoop, calls=%fused_computation.198 | loop fusion | flops 6848512 | bytes 14008320 | tf_op jit(solution)/shard_map/div | solution.py:51
  218.9 1.1 copy-done.14
  220.6 9.5 %shard_map.123 = f32[1,8192]{1,0:T(1,128)} custom-call(f32[64,512]{1,0:T(8,128)} %slice_bitcast_fusion.1.top_ref, s32[1,8192]{1,0:T(1,128)} %get-tuple-element.57.rows_ref, s32[1,8192]{1,0:T(1,128)} %get-tuple-element.56.cols_ref), custom_call_target="tpu_custom_call" | custom-call | flops 1610612736 | bytes 229376 | tf_op jit(solution)/shard_map/pallas_call | solution.py:146
  230.6 1.5 reduce.9
  233.1 0.9 broadcast_select_fusion
  234.0 14.2 %all-to-all-start.2 = ((f32[128,2,32]{2,1,0:T(2,128)}), f32[128,2,32]{2,1,0:T(2,128)S(1)}, u32[]{:S(2)}, u32[]{:S(2)}) async-start(f32[128,2,32]{2,1,0:T(2,128)} %broadcast_select_fusion), calls=%async_computation.2 | async-start | bytes 262144 | tf_op jit(solution)/shard_map/all_to_all | solution.py:264
  249.1 15.1 %all-to-all-done.2 = f32[128,2,32]{2,1,0:T(2,128)S(1)} async-done(((f32[128,2,32]{2,1,0:T(2,128)}), f32[128,2,32]{2,1,0:T(2,128)S(1)}, u32[]{:S(2)}, u32[]{:S(2)}) %all-to-all-start.2) | async-done | bytes 32800 | tf_op jit(solution)/shard_map/all_to_all | solution.py:264
  (95 shorter events, 13.8 us)
Async XLA Ops:
  7.2 40.1 %copy-start = (f32[16,128]{1,0:T(8,128)S(1)}, f32[16,128]{1,0:T(8,128)}, u32[]{:S(2)}) copy-start(f32[16,128]{1,0:T(8,128)} %param.17) | copy-start | bytes 24580
  7.2 32.0 %copy-start.24 = (s32[1,256]{1,0:T(1,128)S(1)}, s32[1,256]{1,0:T(1,128)}, u32[]{:S(2)}) copy-start(s32[1,256]{1,0:T(1,128)} %param.18) | copy-start | bytes 3076
  7.2 32.0 %copy-start.17 = (s32[1,256,128]{2,1,0:T(8,128)S(1)}, s32[1,256,128]{2,1,0:T(8,128)}, u32[]{:S(2)}) copy-start(s32[1,256,128]{2,1,0:T(8,128)} %param.20) | copy-start | bytes 393220
  7.2 33.7 %copy-start.21 = (f32[12]{0:T(128)S(1)}, f32[12]{0:T(128)}, u32[]{:S(2)}) copy-start(f32[12]{0:T(128)} %param.15) | copy-start | bytes 148
  7.2 34.4 %copy-start.22 = (f32[12]{0:T(128)S(1)}, f32[12]{0:T(128)}, u32[]{:S(2)}) copy-start(f32[12]{0:T(128)} %param.14) | copy-start | bytes 148
  7.2 35.1 %copy-start.23 = (f32[12]{0:T(128)S(1)}, f32[12]{0:T(128)}, u32[]{:S(2)}) copy-start(f32[12]{0:T(128)} %param.16) | copy-start | bytes 148
  10.5 35.2 %all-to-all-start = ((s32[128,2,1]{1,2,0:T(1,128)}), s32[128,2,1]{1,2,0:T(1,128)S(1)}, u32[]{:S(2)}, u32[]{:S(2)}) async-start(s32[128,2,1]{1,2,0:T(1,128)} %bitcast.49), calls=%async_computation | async-start | bytes 131072 | tf_op jit(solution)/shard_map/all_to_all | solution.py:220
  33.6 31.8 %collective-permute-start.1 = (f32[5,6,512]{2,1,0:T(8,128)S(1)}, f32[5,6,512]{2,1,0:T(8,128)S(1)}, u32[]{:S(2)}, u32[]{:S(2)}) collective-permute-start(f32[5,6,512]{2,1,0:T(8,128)S(1)} %get-tuple-element.49), channel_id=1, source_target_pairs={{4,0},{8,4},{12,8},{16,12},{20,16},{24,20},{28,24},{32,28},{36,32}... | collective-permute-start | bytes 184328 | tf_op jit(solution)/shard_map/ppermute | solution.py:166
  36.4 29.0 %collective-permute-start = (f32[5,6,512]{2,1,0:T(8,128)S(1)}, f32[5,6,512]{2,1,0:T(8,128)S(1)}, u32[]{:S(2)}, u32[]{:S(2)}) collective-permute-start(f32[5,6,512]{2,1,0:T(8,128)S(1)} %get-tuple-element.48), channel_id=1, source_target_pairs={{0,4},{4,8},{8,12},{12,16},{16,20},{20,24},{24,28},{28,32},{32,36}... | collective-permute-start | bytes 184328 | tf_op jit(solution)/shard_map/ppermute | solution.py:165
  43.1 22.3 %copy-start.16 = (f32[2,64,512]{2,1,0:T(8,128)S(1)}, f32[2,64,512]{2,1,0:T(8,128)}, u32[]{:S(2)}) copy-start(f32[2,64,512]{2,1,0:T(8,128)} %param.11) | copy-start | bytes 786436
  48.9 32.1 %all-to-all-start.1 = ((f32[128,2,128]{2,1,0:T(2,128)}), f32[128,2,128]{2,1,0:T(2,128)S(1)}, u32[]{:S(2)}, u32[]{:S(2)}) async-start(f32[128,2,128]{2,1,0:T(2,128)} %broadcast_select_fusion.1), calls=%async_computation.1 | async-start | bytes 262144 | tf_op jit(solution)/shard_map/all_to_all | solution.py:222
  65.0 67.2 %all-gather.2.cloned.1.call-start = ((), (), s32[]{:S(2)}) async-start(), calls=%async_computation.3 | async-start | bytes 3276800 | tf_op jit(solution)/shard_map/all_gather | solution.py:198
  66.4 15.4 %copy-start.20 = (f32[1,256,128]{2,1,0:T(8,128)S(1)}, f32[1,256,128]{2,1,0:T(8,128)}, u32[]{:S(2)}) copy-start(f32[1,256,128]{2,1,0:T(8,128)} %param.21) | copy-start | bytes 393220
  123.3 8.7 %copy-start.18 = (f32[64,512]{1,0:T(8,128)S(1)}, f32[64,512]{1,0:T(8,128)}, u32[]{:S(2)}) copy-start(f32[64,512]{1,0:T(8,128)} %get-tuple-element.4) | copy-start | bytes 393220
  123.3 8.7 %copy-start.19 = (f32[64,512]{1,0:T(8,128)S(1)}, f32[64,512]{1,0:T(8,128)}, u32[]{:S(2)}) copy-start(f32[64,512]{1,0:T(8,128)} %get-tuple-element.5) | copy-start | bytes 393220
  124.2 6.8 %collective-permute-start.3 = (f32[2,6,512]{2,1,0:T(8,128)S(1)}, f32[2,6,512]{2,1,0:T(8,128)S(1)}, u32[]{:S(2)}, u32[]{:S(2)}) collective-permute-start(f32[2,6,512]{2,1,0:T(8,128)S(1)} %get-tuple-element.53), channel_id=1, source_target_pairs={{4,0},{8,4},{12,8},{16,12},{20,16},{24,20},{28,24},{32,28},{36,32}... | collective-permute-start | bytes 73736 | tf_op jit(solution)/shard_map/ppermute | solution.py:166
  129.0 3.1 %collective-permute-start.2 = (f32[2,6,512]{2,1,0:T(8,128)S(1)}, f32[2,6,512]{2,1,0:T(8,128)S(1)}, u32[]{:S(2)}, u32[]{:S(2)}) collective-permute-start(f32[2,6,512]{2,1,0:T(8,128)S(1)} %get-tuple-element.52), channel_id=1, source_target_pairs={{0,4},{4,8},{8,12},{12,16},{16,20},{20,24},{24,28},{28,32},{32,36}... | collective-permute-start | bytes 73736 | tf_op jit(solution)/shard_map/ppermute | solution.py:165
  181.5 8.5 %copy-start.5 = (f32[8,76,512]{2,1,0:T(8,128)S(1)}, f32[8,76,512]{2,1,0:T(8,128)}, u32[]{:S(2)}) copy-start(f32[8,76,512]{2,1,0:T(8,128)} %get-tuple-element.22) | copy-start | bytes 3735556
  181.5 8.5 %copy-start.6 = (f32[8,76,512]{2,1,0:T(8,128)S(1)}, f32[8,76,512]{2,1,0:T(8,128)}, u32[]{:S(2)}) copy-start(f32[8,76,512]{2,1,0:T(8,128)} %get-tuple-element.23) | copy-start | bytes 3735556
  181.5 8.5 %copy-start.7 = (f32[8,76,512]{2,1,0:T(8,128)S(1)}, f32[8,76,512]{2,1,0:T(8,128)}, u32[]{:S(2)}) copy-start(f32[8,76,512]{2,1,0:T(8,128)} %get-tuple-element.24) | copy-start | bytes 3735556
  181.5 8.5 %copy-start.8 = (f32[8,76,512]{2,1,0:T(8,128)S(1)}, f32[8,76,512]{2,1,0:T(8,128)}, u32[]{:S(2)}) copy-start(f32[8,76,512]{2,1,0:T(8,128)} %get-tuple-element.25) | copy-start | bytes 3735556
  181.6 8.5 %copy-start.9 = (f32[8,76,512]{2,1,0:T(8,128)S(1)}, f32[8,76,512]{2,1,0:T(8,128)}, u32[]{:S(2)}) copy-start(f32[8,76,512]{2,1,0:T(8,128)} %get-tuple-element.26) | copy-start | bytes 3735556
  181.6 8.5 %copy-start.10 = (f32[8,76,512]{2,1,0:T(8,128)S(1)}, f32[8,76,512]{2,1,0:T(8,128)}, u32[]{:S(2)}) copy-start(f32[8,76,512]{2,1,0:T(8,128)} %get-tuple-element.27) | copy-start | bytes 3735556
  181.6 8.5 %copy-start.11 = (f32[8,76,512]{2,1,0:T(8,128)S(1)}, f32[8,76,512]{2,1,0:T(8,128)}, u32[]{:S(2)}) copy-start(f32[8,76,512]{2,1,0:T(8,128)} %get-tuple-element.28) | copy-start | bytes 3735556
  181.6 8.8 %copy-start.12 = (f32[8,76,512]{2,1,0:T(8,128)S(1)}, f32[8,76,512]{2,1,0:T(8,128)}, u32[]{:S(2)}) copy-start(f32[8,76,512]{2,1,0:T(8,128)} %get-tuple-element.32) | copy-start | bytes 3735556
  181.6 9.2 %copy-start.13 = (f32[8,76,512]{2,1,0:T(8,128)S(1)}, f32[8,76,512]{2,1,0:T(8,128)}, u32[]{:S(2)}) copy-start(f32[8,76,512]{2,1,0:T(8,128)} %get-tuple-element.33) | copy-start | bytes 3735556
  209.5 6.4 %copy-start.1 = (f32[8,76,512]{2,1,0:T(8,128)S(1)}, f32[8,76,512]{2,1,0:T(8,128)}, u32[]{:S(2)}) copy-start(f32[8,76,512]{2,1,0:T(8,128)} %get-tuple-element.12) | copy-start | bytes 3735556
  209.5 6.4 %copy-start.2 = (f32[8,76,512]{2,1,0:T(8,128)S(1)}, f32[8,76,512]{2,1,0:T(8,128)}, u32[]{:S(2)}) copy-start(f32[8,76,512]{2,1,0:T(8,128)} %get-tuple-element.13) | copy-start | bytes 3735556
  209.5 6.4 %copy-start.3 = (f32[8,76,512]{2,1,0:T(8,128)S(1)}, f32[8,76,512]{2,1,0:T(8,128)}, u32[]{:S(2)}) copy-start(f32[8,76,512]{2,1,0:T(8,128)} %get-tuple-element.14) | copy-start | bytes 3735556
  209.5 6.4 %copy-start.4 = (f32[8,76,512]{2,1,0:T(8,128)S(1)}, f32[8,76,512]{2,1,0:T(8,128)}, u32[]{:S(2)}) copy-start(f32[8,76,512]{2,1,0:T(8,128)} %get-tuple-element.15) | copy-start | bytes 3735556
  230.1 18.1 %copy-start.15 = (f32[8,76,512]{2,1,0:T(8,128)S(1)}, f32[8,76,512]{2,1,0:T(8,128)}, u32[]{:S(2)}) copy-start(f32[8,76,512]{2,1,0:T(8,128)} %copy-done.14) | copy-start | bytes 3735556
  234.0 30.3 %all-to-all-start.2 = ((f32[128,2,32]{2,1,0:T(2,128)}), f32[128,2,32]{2,1,0:T(2,128)S(1)}, u32[]{:S(2)}, u32[]{:S(2)}) async-start(f32[128,2,32]{2,1,0:T(2,128)} %broadcast_select_fusion), calls=%async_computation.2 | async-start | bytes 262144 | tf_op jit(solution)/shard_map/all_to_all | solution.py:264
  (1 other events, 1.1 us)
Sparse Core Ops, SparseCore 0:
  67.9 43.8 all-gather.1

commit v2 on v1

--- a/solution.py
+++ b/solution.py
@@ -1,3 +1,5 @@
+import functools
+
 import jax
 import jax.numpy as jnp
 from jax import lax
@@ -7,7 +9,7 @@
 
 ITERS = 2
 SWEEPS = 3
-GHOST = ITERS * SWEEPS
+GHOST = 8
 
 
 LATERAL = 1.0
@@ -155,6 +157,108 @@
             bytes_accessed=12 * count + 4 * grid_rows * breadth,
         ),
     )(top, rows, cols)
+
+
+def stencil_kernel(total_rows, tables_ref, fields_ref, land_ref, river_ref, out_ref,
+                   ks_s, alpha_s, store_s, old_s, cond_s, open_s, w_s, heads_s):
+    layers, rows, breadth = out_ref.shape
+    classes_n = tables_ref.shape[1]
+    tile = lax.axis_index("tile")
+    row_id = lax.broadcasted_iota(jnp.int32, (rows, breadth), 0)
+    col_id = lax.broadcasted_iota(jnp.int32, (rows, breadth), 1)
+    grow = tile * (rows - 2 * GHOST) - GHOST + row_id
+    inside = (grow >= 0) & (grow < total_rows)
+    land = jnp.where(inside, land_ref[...], 0.0)
+    moves = []
+    for axis, size, ident in ((0, rows, row_id), (1, breadth, col_id)):
+        for shift in (1, size - 1):
+            adjacent = jnp.abs(pltpu.roll(ident, shift, axis) - ident) == 1
+            moves.append((axis, shift, adjacent))
+
+    def shifted(x):
+        return [jnp.where(adjacent, pltpu.roll(x, shift, axis), 0.0) for axis, shift, adjacent in moves]
+
+    def init(z, carry):
+        classes = fields_ref[1, z].astype(jnp.int32)
+        looked = [jnp.zeros((rows, breadth), jnp.float32) for _ in range(3)]
+        for class_id in range(classes_n):
+            hit = classes == class_id
+            looked = [jnp.where(hit, tables_ref[t, class_id], looked[t]) for t in range(3)]
+        ks_s[z] = jnp.where(inside, looked[0], 1.0)
+        alpha_s[z] = jnp.where(inside, looked[1], 0.0)
+        store_s[z] = jnp.where(inside, looked[2], 1.0)
+        old_s[z] = jnp.where(inside, fields_ref[0, z], 0.0)
+        return carry
+
+    lax.fori_loop(0, layers, init, 0)
+    source = old_s
+    count = 0
+    for picard in range(ITERS):
+
+        def conduct(z, carry, source=source):
+            k = ks_s[z] * jnp.exp(alpha_s[z] * jnp.minimum(source[z], 0.0))
+            cond_s[z] = k
+            open_s[z] = k * land
+            return carry
+
+        lax.fori_loop(0, layers, conduct, 0)
+
+        def weigh(z, carry):
+            c = cond_s[z]
+            co = open_s[z]
+            above = jnp.maximum(z - 1, 0)
+            below = jnp.minimum(z + 1, layers - 1)
+            far = [jnp.where(z > 0, cond_s[above], 0.0), jnp.where(z < layers - 1, cond_s[below], 0.0)]
+            far_open = [jnp.where(z > 0, open_s[above], 0.0), jnp.where(z < layers - 1, open_s[below], 0.0)]
+            far += shifted(c)
+            far_open += shifted(co)
+            for i, (_, _, factor) in enumerate(NEIGHBOURS):
+                w_s[i, z] = factor * 2.0 * co * far_open[i] / (c + far[i])
+            return carry
+
+        lax.fori_loop(0, layers, weigh, 0)
+        for sweep in range(SWEEPS):
+            last = picard == ITERS - 1 and sweep == SWEEPS - 1
+            target = out_ref if last else heads_s.at[count % 2]
+            count += 1
+
+            def relax_layer(z, carry, source=source, target=target):
+                h = source[z]
+                above = jnp.maximum(z - 1, 0)
+                below = jnp.minimum(z + 1, layers - 1)
+                near = [jnp.where(z > 0, source[above], 0.0), jnp.where(z < layers - 1, source[below], 0.0)]
+                near += shifted(h)
+                st = store_s[z]
+                total = st * old_s[z]
+                diagonal_sum = st
+                for i in range(len(NEIGHBOURS)):
+                    w = w_s[i, z]
+                    total = total + w * near[i]
+                    diagonal_sum = diagonal_sum + w
+                top = z == 0
+                total = total + GRAVITY * (w_s[0, z] - w_s[1, z]) + jnp.where(top, river_ref[1], 0.0)
+                target[z] = total / (diagonal_sum + jnp.where(top, river_ref[0], 0.0))
+                return carry
+
+            lax.fori_loop(0, layers, relax_layer, 0)
+            source = target
+
+
+def stencil(tables, fields, land, river, total_rows):
+    _, layers, rows, breadth = fields.shape
+    vmem = pl.BlockSpec(memory_space=pltpu.VMEM)
+    field = pltpu.VMEM((layers, rows, breadth), jnp.float32)
+    cells = layers * rows * breadth
+    return pl.pallas_call(
+        functools.partial(stencil_kernel, total_rows),
+        in_specs=[pl.BlockSpec(memory_space=pltpu.SMEM), vmem, vmem, vmem],
+        out_specs=vmem,
+        out_shape=jax.ShapeDtypeStruct((layers, rows, breadth), jnp.float32),
+        scratch_shapes=[field] * 6
+        + [pltpu.VMEM((6, layers, rows, breadth), jnp.float32), pltpu.VMEM((2, layers, rows, breadth), jnp.float32)],
+        compiler_params=pltpu.CompilerParams(vmem_limit_bytes=48 * 1024 * 1024),
+        cost_estimate=pl.CostEstimate(flops=400 * cells, transcendentals=2 * cells, bytes_accessed=12 * cells),
+    )(tables, fields, land, river)
 
 
 def with_ghost(block, axis, dim, width):
@@ -196,15 +300,6 @@
     extent = across + 2 * GHOST
     fields = planes[: 2 * own_layers].reshape(2, own_layers, extent, breadth)
     fields = lax.all_gather(fields, "layer", axis=1, tiled=True)
-    global_row = tile * across - GHOST + lax.broadcasted_iota(jnp.int32, (1, extent, 1), 1)
-    inside = (global_row >= 0) & (global_row < tile_count * across)
-    head_old = jnp.where(inside, fields[0], 0.0)
-    classes = fields[1].astype(jnp.int32)
-    ks_here = jnp.where(inside, lookup(ks_table, classes), 1.0)
-    alpha_here = jnp.where(inside, lookup(alpha_table, classes), 0.0)
-    store_here = jnp.where(inside, lookup(store_table, classes), 1.0)
-    land_here = jnp.where(inside, planes[2 * own_layers][None], 0.0)
-
     owners = cross_owner[0]
     positions = cross_local[0]
     node_cells = node_cell[0]
@@ -235,18 +330,8 @@
         breadth,
     )
     river = with_ghost(jnp.stack([top_diag, top_rhs]), "tile", 1, GHOST)
-    layers = head_old.shape[0]
-    riv_diag = jnp.pad(river[0][None], ((0, layers - 1), (0, 0), (0, 0)))
-    riv_rhs = jnp.pad(river[1][None], ((0, layers - 1), (0, 0), (0, 0)))
-
-    head = head_old
-    for picard in range(ITERS):
-        conduct = ks_here * jnp.exp(alpha_here * jnp.minimum(head, 0.0))
-        cond_pad = jnp.pad(conduct, 1)
-        open_pad = jnp.pad(conduct * land_here, 1)
-        weights = neighbor_weights(cond_pad, open_pad)
-        for sweep in range(SWEEPS):
-            head = relax(jnp.pad(head, 1), weights, store_here, head_old, riv_diag, riv_rhs)
+    tables = jnp.stack([ks_table, alpha_table, store_table])
+    head = stencil(tables, fields, planes[2 * own_layers], river, tile_count * across)
     kept = lax.dynamic_slice_in_dim(head[:, GHOST : GHOST + across], layer * own_layers, own_layers, 0)
 
     top_head = head[0, GHOST : GHOST + across]

time: 275 us -> 208 us (0.76)
  other arithmetic: 101 us -> 14.8 us
  Pallas kernels: 50.1 us -> 73.8 us
  starting transfers between devices: 63 us -> 54.6 us
  waiting for transfers between devices: 32.4 us -> 38.8 us
    div x5 -> x0, other arithmetic: 58.7 us -> none  [relax(): return total / (diagonal_sum + riv_diag)]
    mul x3 -> x0, other arithmetic: 27.1 us -> none  [on_device(): open_pad = jnp.pad(conduct * land_here, 1)]
    pallas_call x0 -> x1, Pallas kernels: none -> 23.1 us  [stencil(): pl.pallas_call(functools.partial(stencil_kernel, total_rows), in_specs=[p...]
    ppermute x2, waiting for transfers between devices: 0.01 us -> 5.18 us  [with_ghost(): lax.ppermute(lax.slice_in_dim(block, 0, width, axis=dim), axis, backward)]
    all_to_all x1, starting transfers between devices: 14.2 us -> 10.9 us  [on_device(): arrived = lax.all_to_all(sorted_in, 'tile', 0, 0, tiled=True)]
    ppermute x2, starting transfers between devices: 7.59 us -> 4.47 us  [with_ghost(): lax.ppermute(lax.slice_in_dim(block, 0, width, axis=dim), axis, backward)]
    all_to_all x1, starting transfers between devices: 16.1 us -> 13.3 us  [on_device(): sorted_section = lax.all_to_all(reply, 'tile', 0, 0, tiled=True)]
  transfers between devices with their start and end apart: 8 -> 8, of which waited for: 4 -> 4; matrix products, arithmetic and copies ran while one was open for 6% -> 6% of each run, Pallas kernels for 15% -> 20%
where the time goes in v2:
time: 208 us; the launch traced here: 205 us
  Pallas kernels  73.8 us (35%)
  starting transfers between devices  54.6 us (26%)
  waiting for transfers between devices  38.8 us (19%)
  other arithmetic  14.8 us (7%)
  between operations  14.4 us (7%)
  local copies, waits for them, and re-layouts  8.86 us (4%)
    pallas_call x1, Pallas kernels, river_terms(): pl.pallas_call(scatter_kernel, grid=(count // CHUNK,), in_specs=[lane, la...  41.1 us
    pallas_call x1, Pallas kernels, stencil(): pl.pallas_call(functools.partial(stencil_kernel, total_rows), in_specs=[p...  23.1 us
    all_to_all x1, starting transfers between devices, on_device(): asked = lax.all_to_all(wanted, 'tile', 0, 0, tiled=True)  20.4 us
    all_to_all x1, waiting for transfers between devices, on_device(): arrived = lax.all_to_all(sorted_in, 'tile', 0, 0, tiled=True)  15.2 us
    all_to_all x1, waiting for transfers between devices, on_device(): sorted_section = lax.all_to_all(reply, 'tile', 0, 0, tiled=True)  14.6 us
    all_to_all x1, starting transfers between devices, on_device(): sorted_section = lax.all_to_all(reply, 'tile', 0, 0, tiled=True)  13.3 us
    all_to_all x1, starting transfers between devices, on_device(): arrived = lax.all_to_all(sorted_in, 'tile', 0, 0, tiled=True)  10.9 us
    pallas_call x1, Pallas kernels, node_heads(): pl.pallas_call(gather_kernel, grid=(count // CHUNK,), in_specs=[pl.BlockS...  9.54 us
  transfers between devices with their start and end apart: 8, of which 4 were waited for; matrix products, arithmetic and copies ran while one was open for 6% of the time, Pallas kernels for 20%

profile of v2, /device:TPU:1, one launch (start us, length us, event | category | flops | bytes accessed | tf_op | source)
XLA Modules:
  0.0 205.3 jit_solution(14518611491733165420)
XLA Ops:
  7.2 1.0 convert_reduce_fusion
  8.9 0.8 select_reduce_fusion.1
  9.7 0.8 all_to_all.20
  10.5 20.4 %all-to-all-start = ((s32[128,2,1]{1,2,0:T(1,128)}), s32[128,2,1]{1,2,0:T(1,128)S(1)}, u32[]{:S(2)}, u32[]{:S(2)}) async-start(s32[128,2,1]{1,2,0:T(1,128)} %bitcast.12), calls=%async_computation | async-start | bytes 131072 | tf_op jit(solution)/shard_map/all_to_all | solution.py:315
  30.9 1.0 convert_element_type.9
  31.8 0.9 convert_bitcast_fusion
  32.8 0.8 pad_maximum_fusion.4
  33.6 3.5 %collective-permute-start = (f32[5,8,512]{2,1,0:T(8,128)S(1)}, f32[5,8,512]{2,1,0:T(8,128)S(1)}, u32[]{:S(2)}, u32[]{:S(2)}) collective-permute-start(f32[5,8,512]{2,1,0:T(8,128)S(1)} %get-tuple-element.10), channel_id=1, source_target_pairs={{0,4},{4,8},{8,12},{12,16},{16,20},{20,24},{24,28},{28,32},{32,36}... | collective-permute-start | bytes 245768 | tf_op jit(solution)/shard_map/ppermute | solution.py:269
  37.1 1.9 collective-permute-start.1
  39.1 1.7 fusion.1
  41.0 0.9 compare_select_fusion.8
  41.9 3.8 %all-to-all-done = s32[128,2,1]{1,2,0:T(1,128)S(1)} async-done(((s32[128,2,1]{1,2,0:T(1,128)}), s32[128,2,1]{1,2,0:T(1,128)S(1)}, u32[]{:S(2)}, u32[]{:S(2)}) %all-to-all-start) | async-done | bytes 1056 | tf_op jit(solution)/shard_map/all_to_all | solution.py:315
  46.2 0.8 reduce.8
  47.2 0.7 gather_fusion
  48.0 0.8 broadcast_select_fusion.1
  48.8 13.3 %all-to-all-start.1 = ((f32[128,2,128]{2,1,0:T(2,128)}), f32[128,2,128]{2,1,0:T(2,128)S(1)}, u32[]{:S(2)}, u32[]{:S(2)}) async-start(f32[128,2,128]{2,1,0:T(2,128)} %broadcast_select_fusion.1), calls=%async_computation.1 | async-start | bytes 262144 | tf_op jit(solution)/shard_map/all_to_all | solution.py:317
  62.7 0.9 slice.38
  63.6 14.6 %all-to-all-done.1 = f32[128,2,128]{2,1,0:T(2,128)S(1)} async-done(((f32[128,2,128]{2,1,0:T(2,128)}), f32[128,2,128]{2,1,0:T(2,128)S(1)}, u32[]{:S(2)}, u32[]{:S(2)}) %all-to-all-start.1) | async-done | bytes 131104 | tf_op jit(solution)/shard_map/all_to_all | solution.py:317
  79.0 1.0 fusion.4
  80.0 41.1 %shard_map.122 = (f32[64,512]{1,0:T(8,128)}, f32[64,512]{1,0:T(8,128)}) custom-call(s32[1,32768]{1,0:T(1,128)} %get-tuple-element.15.rows_ref, s32[1,32768]{1,0:T(1,128)} %get-tuple-element.14.cols_ref, f32[1,32768]{1,0:T(1,128)} %get-tuple-element.9.diag_in_ref, f32[1,32768]{1,0:T(1,128)} %get-tuple-element.8.rhs_in_ref), custom_call_target="tpu_custom_call" | custom-call | flops 12884901888 | bytes 786432 | tf_op jit(solution)/shard_map/pallas_call | solution.py:109
  121.1 0.8 pad_maximum_fusion.6
  121.9 1.9 collective-permute-start.2
  123.9 2.5 %collective-permute-start.3 = (f32[2,8,512]{2,1,0:T(8,128)S(1)}, f32[2,8,512]{2,1,0:T(8,128)S(1)}, u32[]{:S(2)}, u32[]{:S(2)}) collective-permute-start(f32[2,8,512]{2,1,0:T(8,128)S(1)} %get-tuple-element.13), channel_id=1, source_target_pairs={{4,0},{8,4},{12,8},{16,12},{20,16},{24,20},{28,24},{32,28},{36,32}... | collective-permute-start | bytes 98312 | tf_op jit(solution)/shard_map/ppermute | solution.py:270
  126.4 5.2 %collective-permute-done.3 = f32[2,8,512]{2,1,0:T(8,128)S(1)} collective-permute-done((f32[2,8,512]{2,1,0:T(8,128)S(1)}, f32[2,8,512]{2,1,0:T(8,128)S(1)}, u32[]{:S(2)}, u32[]{:S(2)}) %collective-permute-start.3) | collective-permute-done | bytes 32800 | tf_op jit(solution)/shard_map/ppermute | solution.py:270
  131.7 1.7 copy-done.1
  133.4 23.1 %shard_map.123 = f32[8,80,512]{2,1,0:T(8,128)S(1)} custom-call(f32[3,12]{1,0:T(4,128)S(1)} %pad_maximum_fusion.7.tables_ref, f32[2,8,80,512]{3,2,1,0:T(8,128)S(1)} %copy-done.1, f32[80,512]{1,0:T(8,128)S(1)} %maximum_bitcast_fusion.land_ref, f32[2,80,512]{2,1,0:T(8,128)S(1)} %pad_maximum_fusion.1.river_ref), custom_call_target="tpu_custom_call" | custom-call | flops 131072000 | bytes 3932160 | tf_op jit(solution)/shard_map/pallas_call | solution.py:252
  157.2 9.5 %shard_map.124 = f32[1,8192]{1,0:T(1,128)} custom-call(f32[64,512]{1,0:T(8,128)} %slice_bitcast_fusion.top_ref, s32[1,8192]{1,0:T(1,128)} %get-tuple-element.17.rows_ref, s32[1,8192]{1,0:T(1,128)} %get-tuple-element.16.cols_ref), custom_call_target="tpu_custom_call" | custom-call | flops 1610612736 | bytes 229376 | tf_op jit(solution)/shard_map/pallas_call | solution.py:148
  167.3 1.5 reduce.9
  169.8 0.9 broadcast_select_fusion
  170.6 10.9 %all-to-all-start.2 = ((f32[128,2,32]{2,1,0:T(2,128)}), f32[128,2,32]{2,1,0:T(2,128)S(1)}, u32[]{:S(2)}, u32[]{:S(2)}) async-start(f32[128,2,32]{2,1,0:T(2,128)} %broadcast_select_fusion), calls=%async_computation.2 | async-start | bytes 262144 | tf_op jit(solution)/shard_map/all_to_all | solution.py:349
  182.3 15.2 %all-to-all-done.2 = f32[128,2,32]{2,1,0:T(2,128)S(1)} async-done(((f32[128,2,32]{2,1,0:T(2,128)}), f32[128,2,32]{2,1,0:T(2,128)S(1)}, u32[]{:S(2)}, u32[]{:S(2)}) %all-to-all-start.2) | async-done | bytes 32800 | tf_op jit(solution)/shard_map/all_to_all | solution.py:349
  197.6 0.8 select_reduce_fusion
  (57 shorter events, 6.0 us)
Async XLA Ops:
  7.2 40.1 %copy-start = (f32[16,128]{1,0:T(8,128)S(1)}, f32[16,128]{1,0:T(8,128)}, u32[]{:S(2)}) copy-start(f32[16,128]{1,0:T(8,128)} %param.17) | copy-start | bytes 24580
  7.2 31.9 %copy-start.7 = (s32[1,256]{1,0:T(1,128)S(1)}, s32[1,256]{1,0:T(1,128)}, u32[]{:S(2)}) copy-start(s32[1,256]{1,0:T(1,128)} %param.18) | copy-start | bytes 3076
  7.2 31.9 %copy-start.3 = (s32[1,256,128]{2,1,0:T(8,128)S(1)}, s32[1,256,128]{2,1,0:T(8,128)}, u32[]{:S(2)}) copy-start(s32[1,256,128]{2,1,0:T(8,128)} %param.20) | copy-start | bytes 393220
  10.5 35.2 %all-to-all-start = ((s32[128,2,1]{1,2,0:T(1,128)}), s32[128,2,1]{1,2,0:T(1,128)S(1)}, u32[]{:S(2)}, u32[]{:S(2)}) async-start(s32[128,2,1]{1,2,0:T(1,128)} %bitcast.12), calls=%async_computation | async-start | bytes 131072 | tf_op jit(solution)/shard_map/all_to_all | solution.py:315
  33.6 29.0 %collective-permute-start = (f32[5,8,512]{2,1,0:T(8,128)S(1)}, f32[5,8,512]{2,1,0:T(8,128)S(1)}, u32[]{:S(2)}, u32[]{:S(2)}) collective-permute-start(f32[5,8,512]{2,1,0:T(8,128)S(1)} %get-tuple-element.10), channel_id=1, source_target_pairs={{0,4},{4,8},{8,12},{12,16},{16,20},{20,24},{24,28},{28,32},{32,36}... | collective-permute-start | bytes 245768 | tf_op jit(solution)/shard_map/ppermute | solution.py:269
  37.1 25.5 %collective-permute-start.1 = (f32[5,8,512]{2,1,0:T(8,128)S(1)}, f32[5,8,512]{2,1,0:T(8,128)S(1)}, u32[]{:S(2)}, u32[]{:S(2)}) collective-permute-start(f32[5,8,512]{2,1,0:T(8,128)S(1)} %get-tuple-element.11), channel_id=1, source_target_pairs={{4,0},{8,4},{12,8},{16,12},{20,16},{24,20},{28,24},{32,28},{36,32}... | collective-permute-start | bytes 245768 | tf_op jit(solution)/shard_map/ppermute | solution.py:270
  40.8 21.6 %copy-start.8 = (f32[12]{0:T(128)S(1)}, f32[12]{0:T(128)}, u32[]{:S(2)}) copy-start(f32[12]{0:T(128)} %param.16) | copy-start | bytes 148
  40.8 21.6 %copy-start.9 = (f32[12]{0:T(128)S(1)}, f32[12]{0:T(128)}, u32[]{:S(2)}) copy-start(f32[12]{0:T(128)} %param.15) | copy-start | bytes 148
  40.8 21.6 %copy-start.10 = (f32[12]{0:T(128)S(1)}, f32[12]{0:T(128)}, u32[]{:S(2)}) copy-start(f32[12]{0:T(128)} %param.14) | copy-start | bytes 148
  40.9 21.7 %copy-start.2 = (f32[2,64,512]{2,1,0:T(8,128)S(1)}, f32[2,64,512]{2,1,0:T(8,128)}, u32[]{:S(2)}) copy-start(f32[2,64,512]{2,1,0:T(8,128)} %param.11) | copy-start | bytes 786436
  48.8 29.4 %all-to-all-start.1 = ((f32[128,2,128]{2,1,0:T(2,128)}), f32[128,2,128]{2,1,0:T(2,128)S(1)}, u32[]{:S(2)}, u32[]{:S(2)}) async-start(f32[128,2,128]{2,1,0:T(2,128)} %broadcast_select_fusion.1), calls=%async_computation.1 | async-start | bytes 262144 | tf_op jit(solution)/shard_map/all_to_all | solution.py:317
  62.1 69.5 %all-gather.2.cloned.1.call-start = ((), (), s32[]{:S(2)}) async-start(), calls=%async_computation.3 | async-start | bytes 3276800 | tf_op jit(solution)/shard_map/all_gather | solution.py:302
  63.5 15.5 %copy-start.6 = (f32[1,256,128]{2,1,0:T(8,128)S(1)}, f32[1,256,128]{2,1,0:T(8,128)}, u32[]{:S(2)}) copy-start(f32[1,256,128]{2,1,0:T(8,128)} %param.21) | copy-start | bytes 393220
  121.1 10.5 %copy-start.4 = (f32[64,512]{1,0:T(8,128)S(1)}, f32[64,512]{1,0:T(8,128)}, u32[]{:S(2)}) copy-start(f32[64,512]{1,0:T(8,128)} %get-tuple-element.4) | copy-start | bytes 393220
  121.1 10.5 %copy-start.5 = (f32[64,512]{1,0:T(8,128)S(1)}, f32[64,512]{1,0:T(8,128)}, u32[]{:S(2)}) copy-start(f32[64,512]{1,0:T(8,128)} %get-tuple-element.5) | copy-start | bytes 393220
  121.9 4.5 %collective-permute-start.2 = (f32[2,8,512]{2,1,0:T(8,128)S(1)}, f32[2,8,512]{2,1,0:T(8,128)S(1)}, u32[]{:S(2)}, u32[]{:S(2)}) collective-permute-start(f32[2,8,512]{2,1,0:T(8,128)S(1)} %get-tuple-element.12), channel_id=1, source_target_pairs={{0,4},{4,8},{8,12},{12,16},{16,20},{20,24},{24,28},{28,32},{32,36}... | collective-permute-start | bytes 98312 | tf_op jit(solution)/shard_map/ppermute | solution.py:269
  123.9 7.8 %collective-permute-start.3 = (f32[2,8,512]{2,1,0:T(8,128)S(1)}, f32[2,8,512]{2,1,0:T(8,128)S(1)}, u32[]{:S(2)}, u32[]{:S(2)}) collective-permute-start(f32[2,8,512]{2,1,0:T(8,128)S(1)} %get-tuple-element.13), channel_id=1, source_target_pairs={{4,0},{8,4},{12,8},{16,12},{20,16},{24,20},{28,24},{32,28},{36,32}... | collective-permute-start | bytes 98312 | tf_op jit(solution)/shard_map/ppermute | solution.py:270
  131.7 1.7 copy-start.1
  170.6 26.9 %all-to-all-start.2 = ((f32[128,2,32]{2,1,0:T(2,128)}), f32[128,2,32]{2,1,0:T(2,128)S(1)}, u32[]{:S(2)}, u32[]{:S(2)}) async-start(f32[128,2,32]{2,1,0:T(2,128)} %broadcast_select_fusion), calls=%async_computation.2 | async-start | bytes 262144 | tf_op jit(solution)/shard_map/all_to_all | solution.py:349
Sparse Core Ops, SparseCore 0:
  65.1 43.9 all-gather.1

commit v3 on v2

--- a/solution.py
+++ b/solution.py
@@ -87,12 +87,10 @@
             for piece in split3(value):
                 pieces.append(jnp.where(hit, piece, 0.0).astype(jnp.bfloat16))
         left = jnp.concatenate(pieces, axis=0)
-        cols = cols_ref[...]
-        column_hit = lax.broadcasted_iota(jnp.int32, (breadth, chunk), 0) == cols
+        cols = jnp.transpose(jnp.broadcast_to(cols_ref[...], (8, chunk)))[:, 0:1]
+        column_hit = lax.broadcasted_iota(jnp.int32, (chunk, breadth), 1) == cols
         right = jnp.where(column_hit, 1.0, 0.0).astype(jnp.bfloat16)
-        acc_ref[...] += lax.dot_general(
-            left, right, (((1,), (1,)), ((), ())), preferred_element_type=jnp.float32
-        )
+        acc_ref[...] += jnp.dot(left, right, preferred_element_type=jnp.float32)
 
     @pl.when(step == pl.num_programs(0) - 1)
     def _():

time: 208 us -> 223 us (1.072)
  starting transfers between devices: 54.6 us -> 66 us
  Pallas kernels: 73.8 us -> 82.2 us
  waiting for transfers between devices: 38.8 us -> 35.2 us
    pallas_call x1, Pallas kernels: 41.1 us -> 49.5 us  [river_terms(): pl.pallas_call(scatter_kernel, grid=(count // CHUNK,), in_specs=[lane, la...]
    ppermute x2, starting transfers between devices: 4.47 us -> 9.85 us  [with_ghost(): lax.ppermute(lax.slice_in_dim(block, 0, width, axis=dim), axis, backward)]
    all_to_all x1, starting transfers between devices: 10.9 us -> 15.9 us  [on_device(): arrived = lax.all_to_all(sorted_in, 'tile', 0, 0, tiled=True)]
    ppermute x2, waiting for transfers between devices: 5.18 us -> 1.53 us  [with_ghost(): lax.ppermute(lax.slice_in_dim(block, 0, width, axis=dim), axis, backward)]
  transfers between devices with their start and end apart: 8 -> 8, of which waited for: 4 -> 4; matrix products, arithmetic and copies ran while one was open for 6% -> 6% of each run, Pallas kernels for 20% -> 22%
where the time goes in v3:
time: 223 us; the launch traced here: 221 us
  Pallas kernels  82.2 us (37%)
  starting transfers between devices  66 us (30%)
  waiting for transfers between devices  35.2 us (16%)
  other arithmetic  14.8 us (7%)
  between operations  14.4 us (6%)
  local copies, waits for them, and re-layouts  8.87 us (4%)
    pallas_call x1, Pallas kernels, river_terms(): pl.pallas_call(scatter_kernel, grid=(count // CHUNK,), in_specs=[lane, la...  49.5 us
    pallas_call x1, Pallas kernels, stencil(): pl.pallas_call(functools.partial(stencil_kernel, total_rows), in_specs=[p...  23.1 us
    all_to_all x1, starting transfers between devices, on_device(): asked = lax.all_to_all(wanted, 'tile', 0, 0, tiled=True)  20.4 us
    all_to_all x1, starting transfers between devices, on_device(): arrived = lax.all_to_all(sorted_in, 'tile', 0, 0, tiled=True)  15.9 us
    all_to_all x1, waiting for transfers between devices, on_device(): arrived = lax.all_to_all(sorted_in, 'tile', 0, 0, tiled=True)  15.2 us
    all_to_all x1, waiting for transfers between devices, on_device(): sorted_section = lax.all_to_all(reply, 'tile', 0, 0, tiled=True)  14.6 us
    all_to_all x1, starting transfers between devices, on_device(): sorted_section = lax.all_to_all(reply, 'tile', 0, 0, tiled=True)  13.3 us
    ppermute x2, starting transfers between devices, with_ghost(): lax.ppermute(lax.slice_in_dim(block, 0, width, axis=dim), axis, backward)  9.85 us
  transfers between devices with their start and end apart: 8, of which 4 were waited for; matrix products, arithmetic and copies ran while one was open for 6% of the time, Pallas kernels for 22%

profile of v3, /device:TPU:1, one launch (start us, length us, event | category | flops | bytes accessed | tf_op | source)
XLA Modules:
  0.0 221.5 jit_solution(13948447853118939183)
XLA Ops:
  7.2 1.0 convert_reduce_fusion
  8.9 0.8 select_reduce_fusion.1
  9.7 0.8 all_to_all.20
  10.5 20.4 %all-to-all-start = ((s32[128,2,1]{1,2,0:T(1,128)}), s32[128,2,1]{1,2,0:T(1,128)S(1)}, u32[]{:S(2)}, u32[]{:S(2)}) async-start(s32[128,2,1]{1,2,0:T(1,128)} %bitcast.12), calls=%async_computation | async-start | bytes 131072 | tf_op jit(solution)/shard_map/all_to_all | solution.py:313
  30.9 1.0 convert_element_type.9
  31.8 0.9 convert_bitcast_fusion
  32.8 0.8 pad_maximum_fusion.4
  33.6 3.5 %collective-permute-start = (f32[5,8,512]{2,1,0:T(8,128)S(1)}, f32[5,8,512]{2,1,0:T(8,128)S(1)}, u32[]{:S(2)}, u32[]{:S(2)}) collective-permute-start(f32[5,8,512]{2,1,0:T(8,128)S(1)} %get-tuple-element.10), channel_id=1, source_target_pairs={{0,4},{4,8},{8,12},{12,16},{16,20},{20,24},{24,28},{28,32},{32,36}... | collective-permute-start | bytes 245768 | tf_op jit(solution)/shard_map/ppermute | solution.py:267
  37.1 1.9 collective-permute-start.1
  39.1 1.7 fusion.1
  41.0 0.9 compare_select_fusion.8
  41.9 3.8 %all-to-all-done = s32[128,2,1]{1,2,0:T(1,128)S(1)} async-done(((s32[128,2,1]{1,2,0:T(1,128)}), s32[128,2,1]{1,2,0:T(1,128)S(1)}, u32[]{:S(2)}, u32[]{:S(2)}) %all-to-all-start) | async-done | bytes 1056 | tf_op jit(solution)/shard_map/all_to_all | solution.py:313
  46.2 0.8 reduce.8
  48.0 0.8 broadcast_select_fusion.1
  48.8 13.3 %all-to-all-start.1 = ((f32[128,2,128]{2,1,0:T(2,128)}), f32[128,2,128]{2,1,0:T(2,128)S(1)}, u32[]{:S(2)}, u32[]{:S(2)}) async-start(f32[128,2,128]{2,1,0:T(2,128)} %broadcast_select_fusion.1), calls=%async_computation.1 | async-start | bytes 262144 | tf_op jit(solution)/shard_map/all_to_all | solution.py:315
  62.7 0.9 slice.38
  63.6 14.6 %all-to-all-done.1 = f32[128,2,128]{2,1,0:T(2,128)S(1)} async-done(((f32[128,2,128]{2,1,0:T(2,128)}), f32[128,2,128]{2,1,0:T(2,128)S(1)}, u32[]{:S(2)}, u32[]{:S(2)}) %all-to-all-start.1) | async-done | bytes 131104 | tf_op jit(solution)/shard_map/all_to_all | solution.py:315
  79.0 1.0 fusion.4
  80.0 49.5 %shard_map.122 = (f32[64,512]{1,0:T(8,128)}, f32[64,512]{1,0:T(8,128)}) custom-call(s32[1,32768]{1,0:T(1,128)} %get-tuple-element.15.rows_ref, s32[1,32768]{1,0:T(1,128)} %get-tuple-element.14.cols_ref, f32[1,32768]{1,0:T(1,128)} %get-tuple-element.9.diag_in_ref, f32[1,32768]{1,0:T(1,128)} %get-tuple-element.8.rhs_in_ref), custom_call_target="tpu_custom_call" | custom-call | flops 12884901888 | bytes 786432 | tf_op jit(solution)/shard_map/pallas_call | solution.py:107
  129.5 0.8 pad_maximum_fusion.6
  130.3 3.0 %collective-permute-start.2 = (f32[2,8,512]{2,1,0:T(8,128)S(1)}, f32[2,8,512]{2,1,0:T(8,128)S(1)}, u32[]{:S(2)}, u32[]{:S(2)}) collective-permute-start(f32[2,8,512]{2,1,0:T(8,128)S(1)} %get-tuple-element.12), channel_id=1, source_target_pairs={{0,4},{4,8},{8,12},{12,16},{16,20},{20,24},{24,28},{28,32},{32,36}... | collective-permute-start | bytes 98312 | tf_op jit(solution)/shard_map/ppermute | solution.py:267
  133.3 7.9 %collective-permute-start.3 = (f32[2,8,512]{2,1,0:T(8,128)S(1)}, f32[2,8,512]{2,1,0:T(8,128)S(1)}, u32[]{:S(2)}, u32[]{:S(2)}) collective-permute-start(f32[2,8,512]{2,1,0:T(8,128)S(1)} %get-tuple-element.13), channel_id=1, source_target_pairs={{4,0},{8,4},{12,8},{16,12},{20,16},{24,20},{28,24},{32,28},{36,32}... | collective-permute-start | bytes 98312 | tf_op jit(solution)/shard_map/ppermute | solution.py:268
  141.3 1.5 collective-permute-done.3
  142.9 1.7 copy-done.1
  144.6 23.1 %shard_map.123 = f32[8,80,512]{2,1,0:T(8,128)S(1)} custom-call(f32[3,12]{1,0:T(4,128)S(1)} %pad_maximum_fusion.7.tables_ref, f32[2,8,80,512]{3,2,1,0:T(8,128)S(1)} %copy-done.1, f32[80,512]{1,0:T(8,128)S(1)} %maximum_bitcast_fusion.land_ref, f32[2,80,512]{2,1,0:T(8,128)S(1)} %pad_maximum_fusion.1.river_ref), custom_call_target="tpu_custom_call" | custom-call | flops 131072000 | bytes 3932160 | tf_op jit(solution)/shard_map/pallas_call | solution.py:250
  168.5 9.5 %shard_map.124 = f32[1,8192]{1,0:T(1,128)} custom-call(f32[64,512]{1,0:T(8,128)} %slice_bitcast_fusion.top_ref, s32[1,8192]{1,0:T(1,128)} %get-tuple-element.17.rows_ref, s32[1,8192]{1,0:T(1,128)} %get-tuple-element.16.cols_ref), custom_call_target="tpu_custom_call" | custom-call | flops 1610612736 | bytes 229376 | tf_op jit(solution)/shard_map/pallas_call | solution.py:146
  178.5 1.5 reduce.9
  180.3 0.7 gather_fusion.2
  181.0 0.9 broadcast_select_fusion
  181.9 15.9 %all-to-all-start.2 = ((f32[128,2,32]{2,1,0:T(2,128)}), f32[128,2,32]{2,1,0:T(2,128)S(1)}, u32[]{:S(2)}, u32[]{:S(2)}) async-start(f32[128,2,32]{2,1,0:T(2,128)} %broadcast_select_fusion), calls=%async_computation.2 | async-start | bytes 262144 | tf_op jit(solution)/shard_map/all_to_all | solution.py:347
  198.6 15.2 %all-to-all-done.2 = f32[128,2,32]{2,1,0:T(2,128)S(1)} async-done(((f32[128,2,32]{2,1,0:T(2,128)}), f32[128,2,32]{2,1,0:T(2,128)S(1)}, u32[]{:S(2)}, u32[]{:S(2)}) %all-to-all-start.2) | async-done | bytes 32800 | tf_op jit(solution)/shard_map/all_to_all | solution.py:347
  213.9 0.8 select_reduce_fusion
  (57 shorter events, 6.0 us)
Async XLA Ops:
  7.2 40.1 %copy-start = (f32[16,128]{1,0:T(8,128)S(1)}, f32[16,128]{1,0:T(8,128)}, u32[]{:S(2)}) copy-start(f32[16,128]{1,0:T(8,128)} %param.17) | copy-start | bytes 24580
  7.2 31.9 %copy-start.7 = (s32[1,256]{1,0:T(1,128)S(1)}, s32[1,256]{1,0:T(1,128)}, u32[]{:S(2)}) copy-start(s32[1,256]{1,0:T(1,128)} %param.18) | copy-start | bytes 3076
  7.2 31.9 %copy-start.3 = (s32[1,256,128]{2,1,0:T(8,128)S(1)}, s32[1,256,128]{2,1,0:T(8,128)}, u32[]{:S(2)}) copy-start(s32[1,256,128]{2,1,0:T(8,128)} %param.20) | copy-start | bytes 393220
  10.5 35.2 %all-to-all-start = ((s32[128,2,1]{1,2,0:T(1,128)}), s32[128,2,1]{1,2,0:T(1,128)S(1)}, u32[]{:S(2)}, u32[]{:S(2)}) async-start(s32[128,2,1]{1,2,0:T(1,128)} %bitcast.12), calls=%async_computation | async-start | bytes 131072 | tf_op jit(solution)/shard_map/all_to_all | solution.py:313
  33.6 29.0 %collective-permute-start = (f32[5,8,512]{2,1,0:T(8,128)S(1)}, f32[5,8,512]{2,1,0:T(8,128)S(1)}, u32[]{:S(2)}, u32[]{:S(2)}) collective-permute-start(f32[5,8,512]{2,1,0:T(8,128)S(1)} %get-tuple-element.10), channel_id=1, source_target_pairs={{0,4},{4,8},{8,12},{12,16},{16,20},{20,24},{24,28},{28,32},{32,36}... | collective-permute-start | bytes 245768 | tf_op jit(solution)/shard_map/ppermute | solution.py:267
  37.1 25.5 %collective-permute-start.1 = (f32[5,8,512]{2,1,0:T(8,128)S(1)}, f32[5,8,512]{2,1,0:T(8,128)S(1)}, u32[]{:S(2)}, u32[]{:S(2)}) collective-permute-start(f32[5,8,512]{2,1,0:T(8,128)S(1)} %get-tuple-element.11), channel_id=1, source_target_pairs={{4,0},{8,4},{12,8},{16,12},{20,16},{24,20},{28,24},{32,28},{36,32}... | collective-permute-start | bytes 245768 | tf_op jit(solution)/shard_map/ppermute | solution.py:268
  40.8 21.6 %copy-start.8 = (f32[12]{0:T(128)S(1)}, f32[12]{0:T(128)}, u32[]{:S(2)}) copy-start(f32[12]{0:T(128)} %param.16) | copy-start | bytes 148
  40.8 21.6 %copy-start.9 = (f32[12]{0:T(128)S(1)}, f32[12]{0:T(128)}, u32[]{:S(2)}) copy-start(f32[12]{0:T(128)} %param.15) | copy-start | bytes 148
  40.8 21.6 %copy-start.10 = (f32[12]{0:T(128)S(1)}, f32[12]{0:T(128)}, u32[]{:S(2)}) copy-start(f32[12]{0:T(128)} %param.14) | copy-start | bytes 148
  40.9 21.7 %copy-start.2 = (f32[2,64,512]{2,1,0:T(8,128)S(1)}, f32[2,64,512]{2,1,0:T(8,128)}, u32[]{:S(2)}) copy-start(f32[2,64,512]{2,1,0:T(8,128)} %param.11) | copy-start | bytes 786436
  48.8 29.4 %all-to-all-start.1 = ((f32[128,2,128]{2,1,0:T(2,128)}), f32[128,2,128]{2,1,0:T(2,128)S(1)}, u32[]{:S(2)}, u32[]{:S(2)}) async-start(f32[128,2,128]{2,1,0:T(2,128)} %broadcast_select_fusion.1), calls=%async_computation.1 | async-start | bytes 262144 | tf_op jit(solution)/shard_map/all_to_all | solution.py:315
  62.1 80.8 %all-gather.2.cloned.1.call-start = ((), (), s32[]{:S(2)}) async-start(), calls=%async_computation.3 | async-start | bytes 3276800 | tf_op jit(solution)/shard_map/all_gather | solution.py:300
  63.6 15.5 %copy-start.6 = (f32[1,256,128]{2,1,0:T(8,128)S(1)}, f32[1,256,128]{2,1,0:T(8,128)}, u32[]{:S(2)}) copy-start(f32[1,256,128]{2,1,0:T(8,128)} %param.21) | copy-start | bytes 393220
  129.5 13.3 %copy-start.4 = (f32[64,512]{1,0:T(8,128)S(1)}, f32[64,512]{1,0:T(8,128)}, u32[]{:S(2)}) copy-start(f32[64,512]{1,0:T(8,128)} %get-tuple-element.4) | copy-start | bytes 393220
  129.5 13.3 %copy-start.5 = (f32[64,512]{1,0:T(8,128)S(1)}, f32[64,512]{1,0:T(8,128)}, u32[]{:S(2)}) copy-start(f32[64,512]{1,0:T(8,128)} %get-tuple-element.5) | copy-start | bytes 393220
  130.3 11.0 %collective-permute-start.2 = (f32[2,8,512]{2,1,0:T(8,128)S(1)}, f32[2,8,512]{2,1,0:T(8,128)S(1)}, u32[]{:S(2)}, u32[]{:S(2)}) collective-permute-start(f32[2,8,512]{2,1,0:T(8,128)S(1)} %get-tuple-element.12), channel_id=1, source_target_pairs={{0,4},{4,8},{8,12},{12,16},{16,20},{20,24},{24,28},{28,32},{32,36}... | collective-permute-start | bytes 98312 | tf_op jit(solution)/shard_map/ppermute | solution.py:267
  133.3 9.5 %collective-permute-start.3 = (f32[2,8,512]{2,1,0:T(8,128)S(1)}, f32[2,8,512]{2,1,0:T(8,128)S(1)}, u32[]{:S(2)}, u32[]{:S(2)}) collective-permute-start(f32[2,8,512]{2,1,0:T(8,128)S(1)} %get-tuple-element.13), channel_id=1, source_target_pairs={{4,0},{8,4},{12,8},{16,12},{20,16},{24,20},{28,24},{32,28},{36,32}... | collective-permute-start | bytes 98312 | tf_op jit(solution)/shard_map/ppermute | solution.py:268
  142.9 1.7 copy-start.1
  181.9 32.0 %all-to-all-start.2 = ((f32[128,2,32]{2,1,0:T(2,128)}), f32[128,2,32]{2,1,0:T(2,128)S(1)}, u32[]{:S(2)}, u32[]{:S(2)}) async-start(f32[128,2,32]{2,1,0:T(2,128)} %broadcast_select_fusion), calls=%async_computation.2 | async-start | bytes 262144 | tf_op jit(solution)/shard_map/all_to_all | solution.py:347
Sparse Core Ops, SparseCore 0:
  65.1 44.0 all-gather.1

commit v4 on v2

--- a/solution.py
+++ b/solution.py
@@ -259,6 +259,76 @@
         compiler_params=pltpu.CompilerParams(vmem_limit_bytes=48 * 1024 * 1024),
         cost_estimate=pl.CostEstimate(flops=400 * cells, transcendentals=2 * cells, bytes_accessed=12 * cells),
     )(tables, fields, land, river)
+
+
+def exchange_kernel(x_ref, y_ref, landed, send_sem, recv_sem, local_sem):
+    tiles = x_ref.shape[0]
+    me = lax.axis_index("tile")
+    layer = lax.axis_index("layer")
+    barrier = pltpu.get_barrier_semaphore()
+
+    def greet(i, carry):
+        peer = lax.rem(me + i, tiles)
+        pl.semaphore_signal(barrier, inc=1, device_id=(peer, layer), device_id_type=pl.DeviceIdType.MESH)
+        return carry
+
+    lax.fori_loop(1, tiles, greet, 0)
+    pl.semaphore_wait(barrier, tiles - 1)
+
+    def outgoing(peer):
+        return pltpu.make_async_remote_copy(
+            src_ref=x_ref.at[peer],
+            dst_ref=landed.at[me],
+            send_sem=send_sem.at[peer],
+            recv_sem=recv_sem.at[me],
+            device_id=(peer, layer),
+            device_id_type=pl.DeviceIdType.MESH,
+        )
+
+    def incoming(source):
+        return pltpu.make_async_remote_copy(
+            src_ref=x_ref.at[source],
+            dst_ref=landed.at[source],
+            send_sem=send_sem.at[source],
+            recv_sem=recv_sem.at[source],
+            device_id=(source, layer),
+            device_id_type=pl.DeviceIdType.MESH,
+        )
+
+    def send(i, carry):
+        outgoing(lax.rem(me + i, tiles)).start()
+        return carry
+
+    lax.fori_loop(1, tiles, send, 0)
+    own = pltpu.make_async_copy(x_ref.at[me], landed.at[me], local_sem)
+    own.start()
+    own.wait()
+
+    def finish(i, carry):
+        outgoing(lax.rem(me + i, tiles)).wait_send()
+        incoming(lax.rem(me + tiles - i, tiles)).wait_recv()
+        return carry
+
+    lax.fori_loop(1, tiles, finish, 0)
+    y_ref[...] = landed[...]
+
+
+def exchange(x, collective):
+    tiles = x.shape[0]
+    vmem = pl.BlockSpec(memory_space=pltpu.VMEM)
+    return pl.pallas_call(
+        exchange_kernel,
+        in_specs=[vmem],
+        out_specs=vmem,
+        out_shape=jax.ShapeDtypeStruct(x.shape, x.dtype),
+        scratch_shapes=[
+            pltpu.VMEM(x.shape, x.dtype),
+            pltpu.SemaphoreType.DMA((tiles,)),
+            pltpu.SemaphoreType.DMA((tiles,)),
+            pltpu.SemaphoreType.DMA,
+        ],
+        compiler_params=pltpu.CompilerParams(collective_id=collective, has_side_effects=True),
+    )(x)
 
 
 def with_ghost(block, axis, dim, width):
@@ -312,9 +382,9 @@
     place = owners * per_owner + rank
     at_place = place[None, :] == order[:, None]
     wanted = jnp.sum(jnp.where(at_place, positions[None, :], 0), axis=1)
-    asked = lax.all_to_all(wanted, "tile", 0, 0, tiled=True)
+    asked = exchange(wanted.reshape(tile_count, per_owner, 1), 0).reshape(slots)
     reply = jnp.take(section, asked, axis=0)
-    sorted_section = lax.all_to_all(reply, "tile", 0, 0, tiled=True)
+    sorted_section = exchange(reply.reshape(tile_count, per_owner, node_count), 1).reshape(slots, node_count)
     slot_section = jnp.take(sorted_section, place, axis=0)
 
     in_tile = node_cells >= 0
@@ -346,7 +416,7 @@
     ).reshape(slots, quarter)
     slot_in = jnp.where(my_inside, my_bed * (picked - my_section), 0.0)
     sorted_in = jnp.take(slot_in, jnp.sum(jnp.where(at_place, order[None, :], 0), axis=1), axis=0)
-    arrived = lax.all_to_all(sorted_in, "tile", 0, 0, tiled=True)
+    arrived = exchange(sorted_in.reshape(tile_count, per_owner, quarter), 2).reshape(slots, quarter)
     target = asked[None, :] == jnp.arange(reach_rows, dtype=jnp.int32)[:, None]
     inflow = jnp.sum(jnp.where(target[:, :, None], arrived[None], 0.0), axis=1)
     return (kept, inflow)

time: 208 us -> 220 us (1.058)
  Pallas kernels: 73.8 us -> 155 us
  waiting for transfers between devices: 38.8 us -> 1.9 us
  starting transfers between devices: 54.6 us -> 18.3 us
  local copies, waits for them, and re-layouts: 8.86 us -> 11.6 us
    pallas_call x0 -> x3, Pallas kernels: none -> 83.7 us  [exchange(): pl.pallas_call(exchange_kernel, in_specs=[vmem], out_specs=vmem, out_shap...]
    all_to_all x3 -> x0, starting transfers between devices: 44.6 us -> none  [the longest x1 20.4 us: on_device(): asked = lax.all_to_all(wanted, 'tile', 0, 0, tiled=True)]
    all_to_all x3 -> x0, waiting for transfers between devices: 33.6 us -> none  [the longest x1 15.2 us: on_device(): arrived = lax.all_to_all(sorted_in, 'tile', 0, 0, tiled=True)]
    ppermute x2, starting transfers between devices: 5.49 us -> 10.8 us  [with_ghost(): lax.ppermute(lax.slice_in_dim(block, size - width, size, axis=dim), axis,...]
    ppermute x2, waiting for transfers between devices: 5.18 us -> 1.86 us  [with_ghost(): lax.ppermute(lax.slice_in_dim(block, 0, width, axis=dim), axis, backward)]
    pallas_call x0 -> x1, other arithmetic: none -> 3.14 us  [exchange(): pl.pallas_call(exchange_kernel, in_specs=[vmem], out_specs=vmem, out_shap...]
    ppermute x2, starting transfers between devices: 4.47 us -> 7.49 us  [with_ghost(): lax.ppermute(lax.slice_in_dim(block, 0, width, axis=dim), axis, backward)]
    pallas_call x1, Pallas kernels: 41.1 us -> 38.6 us  [river_terms(): pl.pallas_call(scatter_kernel, grid=(count // CHUNK,), in_specs=[lane, la...]
  transfers between devices with their start and end apart: 8 -> 5, of which waited for: 4 -> 1; matrix products, arithmetic and copies ran while one was open for 6% -> 7% of each run, Pallas kernels for 20% -> 43%
where the time goes in v4:
time: 220 us; the launch traced here: 217 us
  Pallas kernels  155 us (70%)
  starting transfers between devices  18.3 us (8%)
  other arithmetic  15.9 us (7%)
  between operations  14.4 us (7%)
  local copies, waits for them, and re-layouts  11.6 us (5%)
    pallas_call x3, Pallas kernels, exchange(): pl.pallas_call(exchange_kernel, in_specs=[vmem], out_specs=vmem, out_shap...  83.7 us
    pallas_call x1, Pallas kernels, river_terms(): pl.pallas_call(scatter_kernel, grid=(count // CHUNK,), in_specs=[lane, la...  38.6 us
    pallas_call x1, Pallas kernels, stencil(): pl.pallas_call(functools.partial(stencil_kernel, total_rows), in_specs=[p...  23.1 us
    ppermute x2, starting transfers between devices, with_ghost(): lax.ppermute(lax.slice_in_dim(block, size - width, size, axis=dim), axis,...  10.8 us
    pallas_call x1, Pallas kernels, node_heads(): pl.pallas_call(gather_kernel, grid=(count // CHUNK,), in_specs=[pl.BlockS...  9.54 us
    ppermute x2, starting transfers between devices, with_ghost(): lax.ppermute(lax.slice_in_dim(block, 0, width, axis=dim), axis, backward)  7.49 us
  transfers between devices with their start and end apart: 5, of which 1 were waited for; matrix products, arithmetic and copies ran while one was open for 7% of the time, Pallas kernels for 43%

profile of v4, /device:TPU:1, one launch (start us, length us, event | category | flops | bytes accessed | tf_op | source)
XLA Modules:
  0.0 217.1 jit_solution(17638260738356524748)
XLA Ops:
  7.2 1.0 convert_element_type.9
  8.2 0.9 convert_bitcast_fusion
  9.1 0.8 pad_maximum_fusion.4
  9.9 4.5 %collective-permute-start = (f32[5,8,512]{2,1,0:T(8,128)S(1)}, f32[5,8,512]{2,1,0:T(8,128)S(1)}, u32[]{:S(2)}, u32[]{:S(2)}) collective-permute-start(f32[5,8,512]{2,1,0:T(8,128)S(1)} %get-tuple-element.10), channel_id=1, source_target_pairs={{0,4},{4,8},{8,12},{12,16},{16,20},{20,24},{24,28},{28,32},{32,36}... | collective-permute-start | bytes 245768 | tf_op jit(solution)/shard_map/ppermute | solution.py:339
  14.5 5.6 %collective-permute-start.1 = (f32[5,8,512]{2,1,0:T(8,128)S(1)}, f32[5,8,512]{2,1,0:T(8,128)S(1)}, u32[]{:S(2)}, u32[]{:S(2)}) collective-permute-start(f32[5,8,512]{2,1,0:T(8,128)S(1)} %get-tuple-element.11), channel_id=1, source_target_pairs={{4,0},{8,4},{12,8},{16,12},{20,16},{24,20},{28,24},{32,28},{36,32}... | collective-permute-start | bytes 245768 | tf_op jit(solution)/shard_map/ppermute | solution.py:340
  20.4 0.9 reshape.472.x_ref
  21.3 30.3 %shard_map.122 = s32[128,2,1]{2,1,0:T(2,128)} custom-call(s32[128,2,1]{2,1,0:T(2,128)} %reshape.472.x_ref), custom_call_target="tpu_custom_call" | custom-call | tf_op jit(solution)/shard_map/pallas_call | solution.py:319
  51.6 1.0 copy.21
  53.0 3.1 %reduce = s32[128,2]{1,0:T(8,128)S(1)} reduce(s32[128,2,1]{2,1,0:T(2,128)} %shard_map.122, s32[]{:T(128)} %constant.90.clone.1), dimensions={2}, to_apply=%pallas_call.22.reduce_sub_computation | reduce | bytes 2052 | tf_op jit(solution)/shard_map/pallas_call | solution.py:319
  56.3 0.7 gather_fusion
  57.1 0.9 broadcast_select_fusion.1.x_ref
  57.9 24.9 %shard_map.123 = f32[128,2,128]{2,1,0:T(2,128)} custom-call(f32[128,2,128]{2,1,0:T(2,128)} %broadcast_select_fusion.1.x_ref), custom_call_target="tpu_custom_call" | custom-call | tf_op jit(solution)/shard_map/pallas_call | solution.py:319
  82.9 1.6 gather_fusion.1
  84.6 1.0 fusion.4
  85.7 0.9 slice.38
  86.6 1.7 fusion.1
  88.3 38.6 %shard_map.124 = (f32[64,512]{1,0:T(8,128)}, f32[64,512]{1,0:T(8,128)}) custom-call(s32[1,32768]{1,0:T(1,128)} %get-tuple-element.15.rows_ref, s32[1,32768]{1,0:T(1,128)} %get-tuple-element.14.cols_ref, f32[1,32768]{1,0:T(1,128)} %get-tuple-element.9.diag_in_ref, f32[1,32768]{1,0:T(1,128)} %get-tuple-element.8.rhs_in_ref), custom_call_target="tpu_custom_call" | custom-call | flops 12884901888 | bytes 786432 | tf_op jit(solution)/shard_map/pallas_call | solution.py:109
  126.9 0.8 pad_maximum_fusion.6
  127.6 6.3 %collective-permute-start.2 = (f32[2,8,512]{2,1,0:T(8,128)S(1)}, f32[2,8,512]{2,1,0:T(8,128)S(1)}, u32[]{:S(2)}, u32[]{:S(2)}) collective-permute-start(f32[2,8,512]{2,1,0:T(8,128)S(1)} %get-tuple-element.12), channel_id=1, source_target_pairs={{0,4},{4,8},{8,12},{12,16},{16,20},{20,24},{24,28},{28,32},{32,36}... | collective-permute-start | bytes 98312 | tf_op jit(solution)/shard_map/ppermute | solution.py:339
  134.0 1.9 collective-permute-start.3
  136.3 0.9 compare_select_fusion.6
  137.3 1.9 collective-permute-done.3
  139.2 1.0 pad_maximum_fusion.1.river_ref
  140.2 1.7 copy-done.2
  142.0 23.1 %shard_map.125 = f32[8,80,512]{2,1,0:T(8,128)S(1)} custom-call(f32[3,12]{1,0:T(4,128)S(1)} %pad_maximum_fusion.7.tables_ref, f32[2,8,80,512]{3,2,1,0:T(8,128)S(1)} %copy-done.2, f32[80,512]{1,0:T(8,128)S(1)} %maximum_bitcast_fusion.land_ref, f32[2,80,512]{2,1,0:T(8,128)S(1)} %pad_maximum_fusion.1.river_ref), custom_call_target="tpu_custom_call" | custom-call | flops 131072000 | bytes 3932160 | tf_op jit(solution)/shard_map/pallas_call | solution.py:252
  165.9 9.5 %shard_map.126 = f32[1,8192]{1,0:T(1,128)} custom-call(f32[64,512]{1,0:T(8,128)} %slice_bitcast_fusion.top_ref, s32[1,8192]{1,0:T(1,128)} %get-tuple-element.17.rows_ref, s32[1,8192]{1,0:T(1,128)} %get-tuple-element.16.cols_ref), custom_call_target="tpu_custom_call" | custom-call | flops 1610612736 | bytes 229376 | tf_op jit(solution)/shard_map/pallas_call | solution.py:148
  175.9 1.5 reduce.5
  177.7 0.7 gather_fusion.2
  178.4 0.9 broadcast_select_fusion.x_ref
  179.3 28.5 %shard_map.127 = f32[128,2,32]{2,1,0:T(2,128)} custom-call(f32[128,2,32]{2,1,0:T(2,128)} %broadcast_select_fusion.x_ref), custom_call_target="tpu_custom_call" | custom-call | tf_op jit(solution)/shard_map/pallas_call | solution.py:319
  207.8 1.0 copy.27
  208.8 0.8 select_reduce_fusion
  (57 shorter events, 3.9 us)
Async XLA Ops:
  7.2 49.1 %copy-start = (f32[16,128]{1,0:T(8,128)S(1)}, f32[16,128]{1,0:T(8,128)}, u32[]{:S(2)}) copy-start(f32[16,128]{1,0:T(8,128)} %param.17) | copy-start | bytes 24580
  7.2 12.9 %copy-start.6 = (s32[1,256]{1,0:T(1,128)S(1)}, s32[1,256]{1,0:T(1,128)}, u32[]{:S(2)}) copy-start(s32[1,256]{1,0:T(1,128)} %param.18) | copy-start | bytes 3076
  7.2 13.1 %copy-start.7 = (s32[1,256]{1,0:T(1,128)S(1)}, s32[1,256]{1,0:T(1,128)}, u32[]{:S(2)}) copy-start(s32[1,256]{1,0:T(1,128)} %param.19) | copy-start | bytes 3076
  7.2 133.0 %all-gather.2.cloned.1.call-start = ((), (), s32[]{:S(2)}) async-start(), calls=%async_computation | async-start | bytes 3276800 | tf_op jit(solution)/shard_map/all_gather | solution.py:372
  9.9 75.7 %collective-permute-start = (f32[5,8,512]{2,1,0:T(8,128)S(1)}, f32[5,8,512]{2,1,0:T(8,128)S(1)}, u32[]{:S(2)}, u32[]{:S(2)}) collective-permute-start(f32[5,8,512]{2,1,0:T(8,128)S(1)} %get-tuple-element.10), channel_id=1, source_target_pairs={{0,4},{4,8},{8,12},{12,16},{16,20},{20,24},{24,28},{28,32},{32,36}... | collective-permute-start | bytes 245768 | tf_op jit(solution)/shard_map/ppermute | solution.py:339
  14.5 71.2 %collective-permute-start.1 = (f32[5,8,512]{2,1,0:T(8,128)S(1)}, f32[5,8,512]{2,1,0:T(8,128)S(1)}, u32[]{:S(2)}, u32[]{:S(2)}) collective-permute-start(f32[5,8,512]{2,1,0:T(8,128)S(1)} %get-tuple-element.11), channel_id=1, source_target_pairs={{4,0},{8,4},{12,8},{16,12},{20,16},{24,20},{28,24},{32,28},{36,32}... | collective-permute-start | bytes 245768 | tf_op jit(solution)/shard_map/ppermute | solution.py:340
  56.3 28.3 %copy-start.4 = (s32[1,256,128]{2,1,0:T(8,128)S(1)}, s32[1,256,128]{2,1,0:T(8,128)}, u32[]{:S(2)}) copy-start(s32[1,256,128]{2,1,0:T(8,128)} %param.20) | copy-start | bytes 393220
  56.3 28.3 %copy-start.5 = (f32[1,256,128]{2,1,0:T(8,128)S(1)}, f32[1,256,128]{2,1,0:T(8,128)}, u32[]{:S(2)}) copy-start(f32[1,256,128]{2,1,0:T(8,128)} %param.21) | copy-start | bytes 393220
  57.1 28.6 %copy-start.3 = (f32[2,64,512]{2,1,0:T(8,128)S(1)}, f32[2,64,512]{2,1,0:T(8,128)}, u32[]{:S(2)}) copy-start(f32[2,64,512]{2,1,0:T(8,128)} %param.11) | copy-start | bytes 786436
  88.3 48.9 %copy-start.8 = (f32[12]{0:T(128)S(1)}, f32[12]{0:T(128)}, u32[]{:S(2)}) copy-start(f32[12]{0:T(128)} %param.16) | copy-start | bytes 148
  88.3 48.9 %copy-start.9 = (f32[12]{0:T(128)S(1)}, f32[12]{0:T(128)}, u32[]{:S(2)}) copy-start(f32[12]{0:T(128)} %param.15) | copy-start | bytes 148
  88.3 48.9 %copy-start.10 = (f32[12]{0:T(128)S(1)}, f32[12]{0:T(128)}, u32[]{:S(2)}) copy-start(f32[12]{0:T(128)} %param.14) | copy-start | bytes 148
  127.6 9.7 %collective-permute-start.2 = (f32[2,8,512]{2,1,0:T(8,128)S(1)}, f32[2,8,512]{2,1,0:T(8,128)S(1)}, u32[]{:S(2)}, u32[]{:S(2)}) collective-permute-start(f32[2,8,512]{2,1,0:T(8,128)S(1)} %get-tuple-element.12), channel_id=1, source_target_pairs={{0,4},{4,8},{8,12},{12,16},{16,20},{20,24},{24,28},{28,32},{32,36}... | collective-permute-start | bytes 98312 | tf_op jit(solution)/shard_map/ppermute | solution.py:339
  134.0 5.2 %collective-permute-start.3 = (f32[2,8,512]{2,1,0:T(8,128)S(1)}, f32[2,8,512]{2,1,0:T(8,128)S(1)}, u32[]{:S(2)}, u32[]{:S(2)}) collective-permute-start(f32[2,8,512]{2,1,0:T(8,128)S(1)} %get-tuple-element.13), channel_id=1, source_target_pairs={{4,0},{8,4},{12,8},{16,12},{20,16},{24,20},{28,24},{32,28},{36,32}... | collective-permute-start | bytes 98312 | tf_op jit(solution)/shard_map/ppermute | solution.py:340
  140.2 1.7 copy-start.2
  165.1 10.3 %copy-start.1 = (f32[8,80,512]{2,1,0:T(8,128)}, f32[8,80,512]{2,1,0:T(8,128)S(1)}, u32[]{:S(2)}) copy-start(f32[8,80,512]{2,1,0:T(8,128)S(1)} %shard_map.125) | copy-start | bytes 3932164
  177.5 32.1 %slice-start = ((f32[8,80,512]{2,1,0:T(8,128)}), f32[8,64,512]{2,1,0:T(8,128)S(1)}, s32[]{:S(2)}) async-start(f32[8,80,512]{2,1,0:T(8,128)} %copy-done.1), calls=%async_computation.1 | async-start | bytes 2097152 | tf_op jit(solution)/shard_map/slice | solution.py:405
Sparse Core Ops, SparseCore 0:
  86.7 41.6 all-gather.1

commit v5 on v2

--- a/solution.py
+++ b/solution.py
@@ -24,6 +24,7 @@
     (2, 1, LATERAL),
 )
 CHUNK = 512
+INNER = 8
 
 
 def beside(padded, axis_id, step):
@@ -259,6 +260,108 @@
         compiler_params=pltpu.CompilerParams(vmem_limit_bytes=48 * 1024 * 1024),
         cost_estimate=pl.CostEstimate(flops=400 * cells, transcendentals=2 * cells, bytes_accessed=12 * cells),
     )(tables, fields, land, river)
+
+
+def exchange_kernel(x_ref, y_ref, first, second, send_a, recv_a, send_b, recv_b, local_sem):
+    outer, inner = x_ref.shape[0], x_ref.shape[1]
+    me = lax.axis_index("tile")
+    layer = lax.axis_index("layer")
+    high = me // inner
+    low = lax.rem(me, inner)
+    mesh_ids = pl.DeviceIdType.MESH
+    barrier = pltpu.get_barrier_semaphore()
+
+    def greet_inner(i, carry):
+        peer = high * inner + lax.rem(low + i, inner)
+        pl.semaphore_signal(barrier, inc=1, device_id=(peer, layer), device_id_type=mesh_ids)
+        return carry
+
+    def greet_outer(i, carry):
+        peer = lax.rem(high + i, outer) * inner + low
+        pl.semaphore_signal(barrier, inc=1, device_id=(peer, layer), device_id_type=mesh_ids)
+        return carry
+
+    lax.fori_loop(1, inner, greet_inner, 0)
+    lax.fori_loop(1, outer, greet_outer, 0)
+    pl.semaphore_wait(barrier, inner + outer - 2)
+
+    def copy_a(target, source):
+        return pltpu.make_async_remote_copy(
+            src_ref=x_ref.at[:, target],
+            dst_ref=first.at[source],
+            send_sem=send_a.at[target],
+            recv_sem=recv_a.at[source],
+            device_id=(high * inner + target, layer),
+            device_id_type=mesh_ids,
+        )
+
+    def send_first(i, carry):
+        copy_a(lax.rem(low + i, inner), low).start()
+        return carry
+
+    lax.fori_loop(1, inner, send_first, 0)
+    own = pltpu.make_async_copy(x_ref.at[:, low], first.at[low], local_sem.at[0])
+    own.start()
+    own.wait()
+
+    def finish_first(i, carry):
+        copy_a(lax.rem(low + i, inner), low).wait_send()
+        copy_a(lax.rem(low + inner - i, inner), lax.rem(low + inner - i, inner)).wait_recv()
+        return carry
+
+    lax.fori_loop(1, inner, finish_first, 0)
+
+    def copy_b(target, source):
+        return pltpu.make_async_remote_copy(
+            src_ref=first.at[:, target],
+            dst_ref=second.at[source],
+            send_sem=send_b.at[target],
+            recv_sem=recv_b.at[source],
+            device_id=(target * inner + low, layer),
+            device_id_type=mesh_ids,
+        )
+
+    def send_second(i, carry):
+        copy_b(lax.rem(high + i, outer), high).start()
+        return carry
+
+    lax.fori_loop(1, outer, send_second, 0)
+    own = pltpu.make_async_copy(first.at[:, high], second.at[high], local_sem.at[1])
+    own.start()
+    own.wait()
+
+    def finish_second(i, carry):
+        copy_b(lax.rem(high + i, outer), high).wait_send()
+        copy_b(lax.rem(high + outer - i, outer), lax.rem(high + outer - i, outer)).wait_recv()
+        return carry
+
+    lax.fori_loop(1, outer, finish_second, 0)
+    y_ref[...] = second[...]
+
+
+def exchange(x, collective):
+    tiles = x.shape[0]
+    inner = INNER if tiles % INNER == 0 else 1
+    outer = tiles // inner
+    block = x.shape[1:]
+    vmem = pl.BlockSpec(memory_space=pltpu.VMEM)
+    y = pl.pallas_call(
+        exchange_kernel,
+        in_specs=[vmem],
+        out_specs=vmem,
+        out_shape=jax.ShapeDtypeStruct((outer, inner) + block, x.dtype),
+        scratch_shapes=[
+            pltpu.VMEM((inner, outer) + block, x.dtype),
+            pltpu.VMEM((outer, inner) + block, x.dtype),
+            pltpu.SemaphoreType.DMA((inner,)),
+            pltpu.SemaphoreType.DMA((inner,)),
+            pltpu.SemaphoreType.DMA((outer,)),
+            pltpu.SemaphoreType.DMA((outer,)),
+            pltpu.SemaphoreType.DMA((2,)),
+        ],
+        compiler_params=pltpu.CompilerParams(collective_id=collective, has_side_effects=True),
+    )(x.reshape((outer, inner) + block))
+    return y.reshape(x.shape)
 
 
 def with_ghost(block, axis, dim, width):
@@ -312,9 +415,9 @@
     place = owners * per_owner + rank
     at_place = place[None, :] == order[:, None]
     wanted = jnp.sum(jnp.where(at_place, positions[None, :], 0), axis=1)
-    asked = lax.all_to_all(wanted, "tile", 0, 0, tiled=True)
+    asked = exchange(wanted.reshape(tile_count, per_owner, 1), 0).reshape(slots)
     reply = jnp.take(section, asked, axis=0)
-    sorted_section = lax.all_to_all(reply, "tile", 0, 0, tiled=True)
+    sorted_section = exchange(reply.reshape(tile_count, per_owner, node_count), 1).reshape(slots, node_count)
     slot_section = jnp.take(sorted_section, place, axis=0)
 
     in_tile = node_cells >= 0
@@ -346,7 +449,7 @@
     ).reshape(slots, quarter)
     slot_in = jnp.where(my_inside, my_bed * (picked - my_section), 0.0)
     sorted_in = jnp.take(slot_in, jnp.sum(jnp.where(at_place, order[None, :], 0), axis=1), axis=0)
-    arrived = lax.all_to_all(sorted_in, "tile", 0, 0, tiled=True)
+    arrived = exchange(sorted_in.reshape(tile_count, per_owner, quarter), 2).reshape(slots, quarter)
     target = asked[None, :] == jnp.arange(reach_rows, dtype=jnp.int32)[:, None]
     inflow = jnp.sum(jnp.where(target[:, :, None], arrived[None], 0.0), axis=1)
     return (kept, inflow)

time: 208 us -> 213 us (1.024)
  Pallas kernels: 73.8 us -> 150 us
  starting transfers between devices: 54.6 us -> 16.4 us
  waiting for transfers between devices: 38.8 us -> 1.58 us
  local copies, waits for them, and re-layouts: 8.86 us -> 11.8 us
    pallas_call x0 -> x3, Pallas kernels: none -> 75.3 us  [exchange(): pl.pallas_call(exchange_kernel, in_specs=[vmem], out_specs=vmem, out_shap...]
    all_to_all x3 -> x0, starting transfers between devices: 44.6 us -> none  [the longest x1 20.4 us: on_device(): asked = lax.all_to_all(wanted, 'tile', 0, 0, tiled=True)]
    all_to_all x3 -> x0, waiting for transfers between devices: 33.6 us -> none  [the longest x1 15.2 us: on_device(): arrived = lax.all_to_all(sorted_in, 'tile', 0, 0, tiled=True)]
    ppermute x2, waiting for transfers between devices: 5.18 us -> 1.54 us  [with_ghost(): lax.ppermute(lax.slice_in_dim(block, 0, width, axis=dim), axis, backward)]
    ppermute x2, starting transfers between devices: 5.49 us -> 8.87 us  [with_ghost(): lax.ppermute(lax.slice_in_dim(block, size - width, size, axis=dim), axis,...]
    pallas_call x0 -> x1, other arithmetic: none -> 3.13 us  [exchange(): pl.pallas_call(exchange_kernel, in_specs=[vmem], out_specs=vmem, out_shap...]
    ppermute x2, starting transfers between devices: 4.47 us -> 7.49 us  [with_ghost(): lax.ppermute(lax.slice_in_dim(block, 0, width, axis=dim), axis, backward)]
  transfers between devices with their start and end apart: 8 -> 5, of which waited for: 4 -> 1; matrix products, arithmetic and copies ran while one was open for 6% -> 7% of each run, Pallas kernels for 20% -> 44%
where the time goes in v5:
time: 213 us; the launch traced here: 210 us
  Pallas kernels  150 us (70%)
  starting transfers between devices  16.4 us (8%)
  other arithmetic  15.9 us (7%)
  between operations  14.4 us (7%)
  local copies, waits for them, and re-layouts  11.8 us (6%)
    pallas_call x3, Pallas kernels, exchange(): pl.pallas_call(exchange_kernel, in_specs=[vmem], out_specs=vmem, out_shap...  75.3 us
    pallas_call x1, Pallas kernels, river_terms(): pl.pallas_call(scatter_kernel, grid=(count // CHUNK,), in_specs=[lane, la...  42.3 us
    pallas_call x1, Pallas kernels, stencil(): pl.pallas_call(functools.partial(stencil_kernel, total_rows), in_specs=[p...  23.1 us
    pallas_call x1, Pallas kernels, node_heads(): pl.pallas_call(gather_kernel, grid=(count // CHUNK,), in_specs=[pl.BlockS...  9.51 us
    ppermute x2, starting transfers between devices, with_ghost(): lax.ppermute(lax.slice_in_dim(block, size - width, size, axis=dim), axis,...  8.87 us
    ppermute x2, starting transfers between devices, with_ghost(): lax.ppermute(lax.slice_in_dim(block, 0, width, axis=dim), axis, backward)  7.49 us
  transfers between devices with their start and end apart: 5, of which 1 were waited for; matrix products, arithmetic and copies ran while one was open for 7% of the time, Pallas kernels for 44%

profile of v5, /device:TPU:1, one launch (start us, length us, event | category | flops | bytes accessed | tf_op | source)
XLA Modules:
  0.0 210.4 jit_solution(9356354884188334116)
XLA Ops:
  7.2 1.0 convert_element_type.9
  8.2 0.9 convert_bitcast_fusion
  9.1 0.8 pad_maximum_fusion.4
  9.9 4.5 %collective-permute-start = (f32[5,8,512]{2,1,0:T(8,128)S(1)}, f32[5,8,512]{2,1,0:T(8,128)S(1)}, u32[]{:S(2)}, u32[]{:S(2)}) collective-permute-start(f32[5,8,512]{2,1,0:T(8,128)S(1)} %get-tuple-element.10), channel_id=1, source_target_pairs={{0,4},{4,8},{8,12},{12,16},{16,20},{20,24},{24,28},{28,32},{32,36}... | collective-permute-start | bytes 245768 | tf_op jit(solution)/shard_map/ppermute | solution.py:372
  14.5 5.6 %collective-permute-start.1 = (f32[5,8,512]{2,1,0:T(8,128)S(1)}, f32[5,8,512]{2,1,0:T(8,128)S(1)}, u32[]{:S(2)}, u32[]{:S(2)}) collective-permute-start(f32[5,8,512]{2,1,0:T(8,128)S(1)} %get-tuple-element.11), channel_id=1, source_target_pairs={{4,0},{8,4},{12,8},{16,12},{20,16},{24,20},{28,24},{32,28},{36,32}... | collective-permute-start | bytes 245768 | tf_op jit(solution)/shard_map/ppermute | solution.py:373
  20.4 0.9 reshape_reshape.17.x_ref
  21.3 24.5 %shard_map.122 = s32[16,8,2,1]{3,2,1,0:T(2,128)} custom-call(s32[16,8,2,1]{3,2,1,0:T(2,128)} %reshape_reshape.17.x_ref), custom_call_target="tpu_custom_call" | custom-call | tf_op jit(solution)/shard_map/pallas_call | solution.py:348
  45.9 1.1 copy.21
  47.0 3.1 %reduce = s32[16,8,2]{2,1,0:T(8,128)S(1)} reduce(s32[16,8,2,1]{3,2,1,0:T(2,128)} %shard_map.122, s32[]{:T(128)} %constant.90.clone.1), dimensions={3}, to_apply=%pallas_call.22.reduce_sub_computation | reduce | bytes 2052 | tf_op jit(solution)/shard_map/pallas_call | solution.py:348
  50.5 0.7 gather_fusion
  51.2 0.9 broadcast_select_fusion.1.x_ref
  52.1 25.7 %shard_map.123 = f32[16,8,2,128]{3,2,1,0:T(2,128)} custom-call(f32[16,8,2,128]{3,2,1,0:T(2,128)} %broadcast_select_fusion.1.x_ref), custom_call_target="tpu_custom_call" | custom-call | tf_op jit(solution)/shard_map/pallas_call | solution.py:348
  77.8 1.7 gather_fusion.1
  79.6 1.0 fusion.4
  80.6 1.7 fusion.1
  82.3 0.9 slice.38
  83.3 42.3 %shard_map.124 = (f32[64,512]{1,0:T(8,128)}, f32[64,512]{1,0:T(8,128)}) custom-call(s32[1,32768]{1,0:T(1,128)} %get-tuple-element.15.rows_ref, s32[1,32768]{1,0:T(1,128)} %get-tuple-element.14.cols_ref, f32[1,32768]{1,0:T(1,128)} %get-tuple-element.9.diag_in_ref, f32[1,32768]{1,0:T(1,128)} %get-tuple-element.8.rhs_in_ref), custom_call_target="tpu_custom_call" | custom-call | flops 12884901888 | bytes 786432 | tf_op jit(solution)/shard_map/pallas_call | solution.py:110
  125.6 0.8 pad_maximum_fusion.6
  126.3 4.4 %collective-permute-start.2 = (f32[2,8,512]{2,1,0:T(8,128)S(1)}, f32[2,8,512]{2,1,0:T(8,128)S(1)}, u32[]{:S(2)}, u32[]{:S(2)}) collective-permute-start(f32[2,8,512]{2,1,0:T(8,128)S(1)} %get-tuple-element.12), channel_id=1, source_target_pairs={{0,4},{4,8},{8,12},{12,16},{16,20},{20,24},{24,28},{28,32},{32,36}... | collective-permute-start | bytes 98312 | tf_op jit(solution)/shard_map/ppermute | solution.py:372
  130.7 1.9 collective-permute-start.3
  133.3 0.9 compare_select_fusion.6
  134.4 1.5 collective-permute-done.3
  135.9 1.0 pad_maximum_fusion.1.river_ref
  137.0 1.7 copy-done.2
  138.7 23.1 %shard_map.125 = f32[8,80,512]{2,1,0:T(8,128)S(1)} custom-call(f32[3,12]{1,0:T(4,128)S(1)} %pad_maximum_fusion.7.tables_ref, f32[2,8,80,512]{3,2,1,0:T(8,128)S(1)} %copy-done.2, f32[80,512]{1,0:T(8,128)S(1)} %maximum_bitcast_fusion.land_ref, f32[2,80,512]{2,1,0:T(8,128)S(1)} %pad_maximum_fusion.1.river_ref), custom_call_target="tpu_custom_call" | custom-call | flops 131072000 | bytes 3932160 | tf_op jit(solution)/shard_map/pallas_call | solution.py:253
  162.6 9.5 %shard_map.126 = f32[1,8192]{1,0:T(1,128)} custom-call(f32[64,512]{1,0:T(8,128)} %slice_bitcast_fusion.top_ref, s32[1,8192]{1,0:T(1,128)} %get-tuple-element.17.rows_ref, s32[1,8192]{1,0:T(1,128)} %get-tuple-element.16.cols_ref), custom_call_target="tpu_custom_call" | custom-call | flops 1610612736 | bytes 229376 | tf_op jit(solution)/shard_map/pallas_call | solution.py:149
  172.6 1.5 reduce.5
  174.4 0.7 gather_fusion.2
  175.1 0.9 broadcast_select_fusion.x_ref
  176.0 25.1 %shard_map.127 = f32[16,8,2,32]{3,2,1,0:T(2,128)} custom-call(f32[16,8,2,32]{3,2,1,0:T(2,128)} %broadcast_select_fusion.x_ref), custom_call_target="tpu_custom_call" | custom-call | tf_op jit(solution)/shard_map/pallas_call | solution.py:348
  201.1 1.0 copy.27
  202.1 0.8 select_reduce_fusion
  (58 shorter events, 4.0 us)
Async XLA Ops:
  7.2 43.3 %copy-start = (f32[16,128]{1,0:T(8,128)S(1)}, f32[16,128]{1,0:T(8,128)}, u32[]{:S(2)}) copy-start(f32[16,128]{1,0:T(8,128)} %param.17) | copy-start | bytes 24580
  7.2 12.9 %copy-start.6 = (s32[1,256]{1,0:T(1,128)S(1)}, s32[1,256]{1,0:T(1,128)}, u32[]{:S(2)}) copy-start(s32[1,256]{1,0:T(1,128)} %param.18) | copy-start | bytes 3076
  7.2 13.1 %copy-start.7 = (s32[1,256]{1,0:T(1,128)S(1)}, s32[1,256]{1,0:T(1,128)}, u32[]{:S(2)}) copy-start(s32[1,256]{1,0:T(1,128)} %param.19) | copy-start | bytes 3076
  7.2 129.8 %all-gather.2.cloned.1.call-start = ((), (), s32[]{:S(2)}) async-start(), calls=%async_computation | async-start | bytes 3276800 | tf_op jit(solution)/shard_map/all_gather | solution.py:405
  9.9 72.3 %collective-permute-start = (f32[5,8,512]{2,1,0:T(8,128)S(1)}, f32[5,8,512]{2,1,0:T(8,128)S(1)}, u32[]{:S(2)}, u32[]{:S(2)}) collective-permute-start(f32[5,8,512]{2,1,0:T(8,128)S(1)} %get-tuple-element.10), channel_id=1, source_target_pairs={{0,4},{4,8},{8,12},{12,16},{16,20},{20,24},{24,28},{28,32},{32,36}... | collective-permute-start | bytes 245768 | tf_op jit(solution)/shard_map/ppermute | solution.py:372
  14.5 67.8 %collective-permute-start.1 = (f32[5,8,512]{2,1,0:T(8,128)S(1)}, f32[5,8,512]{2,1,0:T(8,128)S(1)}, u32[]{:S(2)}, u32[]{:S(2)}) collective-permute-start(f32[5,8,512]{2,1,0:T(8,128)S(1)} %get-tuple-element.11), channel_id=1, source_target_pairs={{4,0},{8,4},{12,8},{16,12},{20,16},{24,20},{28,24},{32,28},{36,32}... | collective-permute-start | bytes 245768 | tf_op jit(solution)/shard_map/ppermute | solution.py:373
  50.4 29.1 %copy-start.4 = (s32[1,256,128]{2,1,0:T(8,128)S(1)}, s32[1,256,128]{2,1,0:T(8,128)}, u32[]{:S(2)}) copy-start(s32[1,256,128]{2,1,0:T(8,128)} %param.20) | copy-start | bytes 393220
  50.5 29.1 %copy-start.5 = (f32[1,256,128]{2,1,0:T(8,128)S(1)}, f32[1,256,128]{2,1,0:T(8,128)}, u32[]{:S(2)}) copy-start(f32[1,256,128]{2,1,0:T(8,128)} %param.21) | copy-start | bytes 393220
  77.7 4.6 %copy-start.3 = (f32[2,64,512]{2,1,0:T(8,128)S(1)}, f32[2,64,512]{2,1,0:T(8,128)}, u32[]{:S(2)}) copy-start(f32[2,64,512]{2,1,0:T(8,128)} %param.11) | copy-start | bytes 786436
  83.3 51.0 %copy-start.8 = (f32[12]{0:T(128)S(1)}, f32[12]{0:T(128)}, u32[]{:S(2)}) copy-start(f32[12]{0:T(128)} %param.16) | copy-start | bytes 148
  83.3 51.0 %copy-start.9 = (f32[12]{0:T(128)S(1)}, f32[12]{0:T(128)}, u32[]{:S(2)}) copy-start(f32[12]{0:T(128)} %param.15) | copy-start | bytes 148
  83.3 50.9 %copy-start.10 = (f32[12]{0:T(128)S(1)}, f32[12]{0:T(128)}, u32[]{:S(2)}) copy-start(f32[12]{0:T(128)} %param.14) | copy-start | bytes 148
  126.3 8.1 %collective-permute-start.2 = (f32[2,8,512]{2,1,0:T(8,128)S(1)}, f32[2,8,512]{2,1,0:T(8,128)S(1)}, u32[]{:S(2)}, u32[]{:S(2)}) collective-permute-start(f32[2,8,512]{2,1,0:T(8,128)S(1)} %get-tuple-element.12), channel_id=1, source_target_pairs={{0,4},{4,8},{8,12},{12,16},{16,20},{20,24},{24,28},{28,32},{32,36}... | collective-permute-start | bytes 98312 | tf_op jit(solution)/shard_map/ppermute | solution.py:372
  130.7 5.2 %collective-permute-start.3 = (f32[2,8,512]{2,1,0:T(8,128)S(1)}, f32[2,8,512]{2,1,0:T(8,128)S(1)}, u32[]{:S(2)}, u32[]{:S(2)}) collective-permute-start(f32[2,8,512]{2,1,0:T(8,128)S(1)} %get-tuple-element.13), channel_id=1, source_target_pairs={{4,0},{8,4},{12,8},{16,12},{20,16},{24,20},{28,24},{32,28},{36,32}... | collective-permute-start | bytes 98312 | tf_op jit(solution)/shard_map/ppermute | solution.py:373
  137.0 1.7 copy-start.2
  161.9 10.2 %copy-start.1 = (f32[8,80,512]{2,1,0:T(8,128)}, f32[8,80,512]{2,1,0:T(8,128)S(1)}, u32[]{:S(2)}) copy-start(f32[8,80,512]{2,1,0:T(8,128)S(1)} %shard_map.125) | copy-start | bytes 3932164
  174.2 28.6 %slice-start = ((f32[8,80,512]{2,1,0:T(8,128)}), f32[8,64,512]{2,1,0:T(8,128)S(1)}, s32[]{:S(2)}) async-start(f32[8,80,512]{2,1,0:T(8,128)} %copy-done.1), calls=%async_computation.1 | async-start | bytes 2097152 | tf_op jit(solution)/shard_map/slice | solution.py:438
Sparse Core Ops, SparseCore 0:
  83.4 39.4 all-gather.1

commit v6 on v5

--- a/solution.py
+++ b/solution.py
@@ -364,6 +364,59 @@
     return y.reshape(x.shape)
 
 
+def combine_kernel(x_ref, y_ref, landed, send_sem, recv_sem, local_sem):
+    groups = landed.shape[0]
+    me = lax.axis_index("layer")
+    tile = lax.axis_index("tile")
+    mesh_ids = pl.DeviceIdType.MESH
+    barrier = pltpu.get_barrier_semaphore()
+    for i in range(1, groups):
+        pl.semaphore_signal(barrier, inc=1, device_id=(tile, lax.rem(me + i, groups)), device_id_type=mesh_ids)
+    pl.semaphore_wait(barrier, groups - 1)
+
+    def copy(target, source):
+        return pltpu.make_async_remote_copy(
+            src_ref=x_ref,
+            dst_ref=landed.at[source],
+            send_sem=send_sem.at[target],
+            recv_sem=recv_sem.at[source],
+            device_id=(tile, target),
+            device_id_type=mesh_ids,
+        )
+
+    for i in range(1, groups):
+        copy(lax.rem(me + i, groups), me).start()
+    own = pltpu.make_async_copy(x_ref, landed.at[me], local_sem)
+    own.start()
+    own.wait()
+    for i in range(1, groups):
+        copy(lax.rem(me + i, groups), me).wait_send()
+        source = lax.rem(me + groups - i, groups)
+        copy(source, source).wait_recv()
+    total = landed[0]
+    for g in range(1, groups):
+        total = total + landed[g]
+    y_ref[...] = total
+
+
+def combine(x, collective):
+    groups = lax.axis_size("layer")
+    vmem = pl.BlockSpec(memory_space=pltpu.VMEM)
+    return pl.pallas_call(
+        combine_kernel,
+        in_specs=[vmem],
+        out_specs=vmem,
+        out_shape=jax.ShapeDtypeStruct(x.shape, x.dtype),
+        scratch_shapes=[
+            pltpu.VMEM((groups,) + x.shape, x.dtype),
+            pltpu.SemaphoreType.DMA((groups,)),
+            pltpu.SemaphoreType.DMA((groups,)),
+            pltpu.SemaphoreType.DMA,
+        ],
+        compiler_params=pltpu.CompilerParams(collective_id=collective, has_side_effects=True),
+    )(x)
+
+
 def with_ghost(block, axis, dim, width):
     count = lax.axis_size(axis)
     forward = [(i, i + 1) for i in range(count - 1)]
@@ -420,19 +473,24 @@
     sorted_section = exchange(reply.reshape(tile_count, per_owner, node_count), 1).reshape(slots, node_count)
     slot_section = jnp.take(sorted_section, place, axis=0)
 
-    in_tile = node_cells >= 0
-    bed_terms = jnp.where(in_tile, bed_given, 0.0)
-    cell_rows = jnp.where(in_tile, node_cells // breadth, -1)
-    cell_cols = jnp.where(in_tile, node_cells % breadth, 0)
+    share = slots // layer_count
+    share_cells = lax.dynamic_slice_in_dim(node_cells, layer * share, share, 0)
+    share_bed = lax.dynamic_slice_in_dim(bed_given, layer * share, share, 0)
+    share_section = lax.dynamic_slice_in_dim(slot_section, layer * share, share, 0)
+    in_tile = share_cells >= 0
+    bed_terms = jnp.where(in_tile, share_bed, 0.0)
+    cell_rows = jnp.where(in_tile, share_cells // breadth, -1)
+    cell_cols = jnp.where(in_tile, share_cells % breadth, 0)
     top_diag, top_rhs = river_terms(
         cell_rows.reshape(1, -1),
         cell_cols.reshape(1, -1),
         bed_terms.reshape(1, -1),
-        (bed_terms * slot_section).reshape(1, -1),
+        (bed_terms * share_section).reshape(1, -1),
         across,
         breadth,
     )
-    river = with_ghost(jnp.stack([top_diag, top_rhs]), "tile", 1, GHOST)
+    river = combine(jnp.stack([top_diag, top_rhs]), 3)
+    river = with_ghost(river, "tile", 1, GHOST)
     tables = jnp.stack([ks_table, alpha_table, store_table])
     head = stencil(tables, fields, planes[2 * own_layers], river, tile_count * across)
     kept = lax.dynamic_slice_in_dim(head[:, GHOST : GHOST + across], layer * own_layers, own_layers, 0)

time: 213 us -> 215 us (level)
  Pallas kernels: 150 us -> 153 us
    pallas_call x1, Pallas kernels: 42.3 us -> 12.1 us  [river_terms(): pl.pallas_call(scatter_kernel, grid=(count // CHUNK,), in_specs=[lane, la...]
    pallas_call x0 -> x1, Pallas kernels: none -> 28.7 us  [combine(): pl.pallas_call(combine_kernel, in_specs=[vmem], out_specs=vmem, out_shape...]
    pallas_call x3, Pallas kernels: 75.3 us -> 79.7 us  [exchange(): pl.pallas_call(exchange_kernel, in_specs=[vmem], out_specs=vmem, out_shap...]
  transfers between devices with their start and end apart: 5 -> 5, of which waited for: 1 -> 1; matrix products, arithmetic and copies ran while one was open for 7% -> 8% of each run, Pallas kernels for 44% -> 43%
where the time goes in v6:
time: 215 us; the launch traced here: 214 us
  Pallas kernels  153 us (71%)
  other arithmetic  16.3 us (8%)
  starting transfers between devices  15.5 us (7%)
  between operations  14.4 us (7%)
  local copies, waits for them, and re-layouts  12.6 us (6%)
    pallas_call x3, Pallas kernels, exchange(): pl.pallas_call(exchange_kernel, in_specs=[vmem], out_specs=vmem, out_shap...  79.7 us
    pallas_call x1, Pallas kernels, combine(): pl.pallas_call(combine_kernel, in_specs=[vmem], out_specs=vmem, out_shape...  28.7 us
    pallas_call x1, Pallas kernels, stencil(): pl.pallas_call(functools.partial(stencil_kernel, total_rows), in_specs=[p...  23.1 us
    pallas_call x1, Pallas kernels, river_terms(): pl.pallas_call(scatter_kernel, grid=(count // CHUNK,), in_specs=[lane, la...  12.1 us
    pallas_call x1, Pallas kernels, node_heads(): pl.pallas_call(gather_kernel, grid=(count // CHUNK,), in_specs=[pl.BlockS...  9.55 us
    ppermute x2, starting transfers between devices, with_ghost(): lax.ppermute(lax.slice_in_dim(block, size - width, size, axis=dim), axis,...  8.02 us
    ppermute x2, starting transfers between devices, with_ghost(): lax.ppermute(lax.slice_in_dim(block, 0, width, axis=dim), axis, backward)  7.49 us
  transfers between devices with their start and end apart: 5, of which 1 were waited for; matrix products, arithmetic and copies ran while one was open for 8% of the time, Pallas kernels for 43%

profile of v6, /device:TPU:1, one launch (start us, length us, event | category | flops | bytes accessed | tf_op | source)
XLA Modules:
  0.0 213.6 jit_solution(9787786085516342646)
XLA Ops:
  7.2 1.0 convert_element_type.9
  8.2 0.9 convert_bitcast_fusion
  9.1 0.8 pad_maximum_fusion.5
  9.9 4.6 %collective-permute-start = (f32[5,8,512]{2,1,0:T(8,128)S(1)}, f32[5,8,512]{2,1,0:T(8,128)S(1)}, u32[]{:S(2)}, u32[]{:S(2)}) collective-permute-start(f32[5,8,512]{2,1,0:T(8,128)S(1)} %get-tuple-element.8), channel_id=1, source_target_pairs={{0,4},{4,8},{8,12},{12,16},{16,20},{20,24},{24,28},{28,32},{32,36}... | collective-permute-start | bytes 245768 | tf_op jit(solution)/shard_map/ppermute | solution.py:425
  14.6 5.6 %collective-permute-start.1 = (f32[5,8,512]{2,1,0:T(8,128)S(1)}, f32[5,8,512]{2,1,0:T(8,128)S(1)}, u32[]{:S(2)}, u32[]{:S(2)}) collective-permute-start(f32[5,8,512]{2,1,0:T(8,128)S(1)} %get-tuple-element.9), channel_id=1, source_target_pairs={{4,0},{8,4},{12,8},{16,12},{20,16},{24,20},{28,24},{32,28},{36,32}... | collective-permute-start | bytes 245768 | tf_op jit(solution)/shard_map/ppermute | solution.py:426
  20.6 0.9 reshape_reshape.17.x_ref
  21.5 24.5 %shard_map.122 = s32[16,8,2,1]{3,2,1,0:T(2,128)} custom-call(s32[16,8,2,1]{3,2,1,0:T(2,128)} %reshape_reshape.17.x_ref), custom_call_target="tpu_custom_call" | custom-call | tf_op jit(solution)/shard_map/pallas_call | solution.py:348
  46.0 1.1 copy.21
  47.1 3.1 %reduce = s32[16,8,2]{2,1,0:T(8,128)S(1)} reduce(s32[16,8,2,1]{3,2,1,0:T(2,128)} %shard_map.122, s32[]{:T(128)} %constant.94.clone.1), dimensions={3}, to_apply=%pallas_call.25.reduce_sub_computation | reduce | bytes 2052 | tf_op jit(solution)/shard_map/pallas_call | solution.py:348
  51.3 0.9 broadcast_select_fusion.1.x_ref
  52.2 25.7 %shard_map.123 = f32[16,8,2,128]{3,2,1,0:T(2,128)} custom-call(f32[16,8,2,128]{3,2,1,0:T(2,128)} %broadcast_select_fusion.1.x_ref), custom_call_target="tpu_custom_call" | custom-call | tf_op jit(solution)/shard_map/pallas_call | solution.py:348
  77.9 0.9 fusion.2
  79.4 1.6 gather_fusion.1
  81.2 0.9 slice.38
  82.8 12.1 %shard_map.124 = (f32[64,512]{1,0:T(8,128)}, f32[64,512]{1,0:T(8,128)}) custom-call(s32[1,8192]{1,0:T(1,128)} %get-tuple-element.15.rows_ref, s32[1,8192]{1,0:T(1,128)} %get-tuple-element.14.cols_ref, f32[1,8192]{1,0:T(1,128)} %broadcast_select_fusion.3.diag_in_ref, f32[1,8192]{1,0:T(1,128)} %bitcast.54), custom_call_target="tpu_custom_call" | custom-call | flops 3221225472 | bytes 393216 | tf_op jit(solution)/shard_map/pallas_call | solution.py:110
  94.9 1.8 pad_maximum_fusion.2.x_ref
  96.7 28.7 %shard_map.125 = f32[2,64,512]{2,1,0:T(8,128)} custom-call(f32[2,64,512]{2,1,0:T(8,128)} %pad_maximum_fusion.2.x_ref), custom_call_target="tpu_custom_call" | custom-call | tf_op jit(solution)/shard_map/pallas_call | solution.py:405
  125.4 0.8 fusion.4
  126.2 3.4 %collective-permute-start.2 = (f32[2,8,512]{2,1,0:T(8,128)S(1)}, f32[2,8,512]{2,1,0:T(8,128)S(1)}, u32[]{:S(2)}, u32[]{:S(2)}) collective-permute-start(f32[2,8,512]{2,1,0:T(8,128)S(1)} %get-tuple-element.10), channel_id=1, source_target_pairs={{0,4},{4,8},{8,12},{12,16},{16,20},{20,24},{24,28},{28,32},{32,36}... | collective-permute-start | bytes 98312 | tf_op jit(solution)/shard_map/ppermute | solution.py:425
  129.6 1.9 collective-permute-start.3
  132.2 0.9 compare_select_fusion.6
  133.3 1.6 collective-permute-done.3
  134.8 1.0 pad_maximum_fusion.1.river_ref
  135.9 1.7 copy-done.2
  137.6 23.1 %shard_map.126 = f32[8,80,512]{2,1,0:T(8,128)S(1)} custom-call(f32[3,12]{1,0:T(4,128)S(1)} %pad_maximum_fusion.6.tables_ref, f32[2,8,80,512]{3,2,1,0:T(8,128)S(1)} %copy-done.2, f32[80,512]{1,0:T(8,128)S(1)} %maximum_bitcast_fusion.land_ref, f32[2,80,512]{2,1,0:T(8,128)S(1)} %pad_maximum_fusion.1.river_ref), custom_call_target="tpu_custom_call" | custom-call | flops 131072000 | bytes 3932160 | tf_op jit(solution)/shard_map/pallas_call | solution.py:253
  161.5 9.5 %shard_map.127 = f32[1,8192]{1,0:T(1,128)} custom-call(f32[64,512]{1,0:T(8,128)} %slice_bitcast_fusion.top_ref, s32[1,8192]{1,0:T(1,128)} %get-tuple-element.13.rows_ref, s32[1,8192]{1,0:T(1,128)} %get-tuple-element.12.cols_ref), custom_call_target="tpu_custom_call" | custom-call | flops 1610612736 | bytes 229376 | tf_op jit(solution)/shard_map/pallas_call | solution.py:149
  171.5 1.5 reduce.5
  173.3 0.7 gather_fusion.2
  174.0 0.9 broadcast_select_fusion.x_ref
  174.9 29.5 %shard_map.128 = f32[16,8,2,32]{3,2,1,0:T(2,128)} custom-call(f32[16,8,2,32]{3,2,1,0:T(2,128)} %broadcast_select_fusion.x_ref), custom_call_target="tpu_custom_call" | custom-call | tf_op jit(solution)/shard_map/pallas_call | solution.py:348
  204.3 1.0 copy.27
  205.3 0.8 select_reduce_fusion
  (63 shorter events, 6.0 us)
Async XLA Ops:
  7.2 43.4 %copy-start = (f32[16,128]{1,0:T(8,128)S(1)}, f32[16,128]{1,0:T(8,128)}, u32[]{:S(2)}) copy-start(f32[16,128]{1,0:T(8,128)} %param.17) | copy-start | bytes 24580
  7.2 13.0 %copy-start.6 = (s32[1,256]{1,0:T(1,128)S(1)}, s32[1,256]{1,0:T(1,128)}, u32[]{:S(2)}) copy-start(s32[1,256]{1,0:T(1,128)} %param.18) | copy-start | bytes 3076
  7.2 13.2 %copy-start.7 = (s32[1,256]{1,0:T(1,128)S(1)}, s32[1,256]{1,0:T(1,128)}, u32[]{:S(2)}) copy-start(s32[1,256]{1,0:T(1,128)} %param.19) | copy-start | bytes 3076
  7.2 128.6 %all-gather.2.cloned.1.call-start = ((), (), s32[]{:S(2)}) async-start(), calls=%async_computation | async-start | bytes 3276800 | tf_op jit(solution)/shard_map/all_gather | solution.py:458
  9.9 67.9 %copy-start.4 = (s32[1,256,128]{2,1,0:T(8,128)S(1)}, s32[1,256,128]{2,1,0:T(8,128)}, u32[]{:S(2)}) copy-start(s32[1,256,128]{2,1,0:T(8,128)} %param.20) | copy-start | bytes 393220
  9.9 71.1 %collective-permute-start = (f32[5,8,512]{2,1,0:T(8,128)S(1)}, f32[5,8,512]{2,1,0:T(8,128)S(1)}, u32[]{:S(2)}, u32[]{:S(2)}) collective-permute-start(f32[5,8,512]{2,1,0:T(8,128)S(1)} %get-tuple-element.8), channel_id=1, source_target_pairs={{0,4},{4,8},{8,12},{12,16},{16,20},{20,24},{24,28},{28,32},{32,36}... | collective-permute-start | bytes 245768 | tf_op jit(solution)/shard_map/ppermute | solution.py:425
  14.6 66.5 %collective-permute-start.1 = (f32[5,8,512]{2,1,0:T(8,128)S(1)}, f32[5,8,512]{2,1,0:T(8,128)S(1)}, u32[]{:S(2)}, u32[]{:S(2)}) collective-permute-start(f32[5,8,512]{2,1,0:T(8,128)S(1)} %get-tuple-element.9), channel_id=1, source_target_pairs={{4,0},{8,4},{12,8},{16,12},{20,16},{24,20},{28,24},{32,28},{36,32}... | collective-permute-start | bytes 245768 | tf_op jit(solution)/shard_map/ppermute | solution.py:426
  20.5 57.3 %copy-start.5 = (f32[1,256,128]{2,1,0:T(8,128)S(1)}, f32[1,256,128]{2,1,0:T(8,128)}, u32[]{:S(2)}) copy-start(f32[1,256,128]{2,1,0:T(8,128)} %param.21) | copy-start | bytes 393220
  51.3 29.8 %copy-start.3 = (f32[2,64,512]{2,1,0:T(8,128)S(1)}, f32[2,64,512]{2,1,0:T(8,128)}, u32[]{:S(2)}) copy-start(f32[2,64,512]{2,1,0:T(8,128)} %param.11) | copy-start | bytes 786436
  94.9 38.1 %copy-start.8 = (f32[12]{0:T(128)S(1)}, f32[12]{0:T(128)}, u32[]{:S(2)}) copy-start(f32[12]{0:T(128)} %param.16) | copy-start | bytes 148
  94.9 38.1 %copy-start.9 = (f32[12]{0:T(128)S(1)}, f32[12]{0:T(128)}, u32[]{:S(2)}) copy-start(f32[12]{0:T(128)} %param.15) | copy-start | bytes 148
  94.9 38.1 %copy-start.10 = (f32[12]{0:T(128)S(1)}, f32[12]{0:T(128)}, u32[]{:S(2)}) copy-start(f32[12]{0:T(128)} %param.14) | copy-start | bytes 148
  126.2 7.0 %collective-permute-start.2 = (f32[2,8,512]{2,1,0:T(8,128)S(1)}, f32[2,8,512]{2,1,0:T(8,128)S(1)}, u32[]{:S(2)}, u32[]{:S(2)}) collective-permute-start(f32[2,8,512]{2,1,0:T(8,128)S(1)} %get-tuple-element.10), channel_id=1, source_target_pairs={{0,4},{4,8},{8,12},{12,16},{16,20},{20,24},{24,28},{28,32},{32,36}... | collective-permute-start | bytes 98312 | tf_op jit(solution)/shard_map/ppermute | solution.py:425
  129.6 5.2 %collective-permute-start.3 = (f32[2,8,512]{2,1,0:T(8,128)S(1)}, f32[2,8,512]{2,1,0:T(8,128)S(1)}, u32[]{:S(2)}, u32[]{:S(2)}) collective-permute-start(f32[2,8,512]{2,1,0:T(8,128)S(1)} %get-tuple-element.11), channel_id=1, source_target_pairs={{4,0},{8,4},{12,8},{16,12},{20,16},{24,20},{28,24},{32,28},{36,32}... | collective-permute-start | bytes 98312 | tf_op jit(solution)/shard_map/ppermute | solution.py:426
  135.9 1.7 copy-start.2
  160.7 10.3 %copy-start.1 = (f32[8,80,512]{2,1,0:T(8,128)}, f32[8,80,512]{2,1,0:T(8,128)S(1)}, u32[]{:S(2)}) copy-start(f32[8,80,512]{2,1,0:T(8,128)S(1)} %shard_map.126) | copy-start | bytes 3932164
  173.1 33.0 %slice-start = ((f32[8,80,512]{2,1,0:T(8,128)}), f32[8,64,512]{2,1,0:T(8,128)S(1)}, s32[]{:S(2)}) async-start(f32[8,80,512]{2,1,0:T(8,128)} %copy-done.1), calls=%async_computation.1 | async-start | bytes 2097152 | tf_op jit(solution)/shard_map/slice | solution.py:496
Sparse Core Ops, SparseCore 0:
  82.2 50.6 all-gather.1

commit v7 on v2

--- a/solution.py
+++ b/solution.py
@@ -68,9 +68,14 @@
     return high, middle, low
 
 
-def scatter_kernel(rows_ref, cols_ref, diag_in_ref, rhs_in_ref, diag_ref, rhs_ref, acc_ref):
+def split2(value):
+    high = value.astype(jnp.bfloat16).astype(jnp.float32)
+    return high, value - high
+
+
+def scatter_kernel(rows_ref, cols_ref, values_ref, out_ref, acc_ref):
     step = pl.program_id(0)
-    grid_rows, breadth = diag_ref.shape
+    grid_rows, breadth = out_ref.shape
     chunk = rows_ref.shape[1]
 
     @pl.when(step == 0)
@@ -82,11 +87,9 @@
     @pl.when(jnp.max(rows) >= 0)
     def _():
         hit = lax.broadcasted_iota(jnp.int32, (grid_rows, chunk), 0) == rows
-        pieces = []
-        for value in (diag_in_ref[...], rhs_in_ref[...]):
-            for piece in split3(value):
-                pieces.append(jnp.where(hit, piece, 0.0).astype(jnp.bfloat16))
-        left = jnp.concatenate(pieces, axis=0)
+        left = jnp.concatenate(
+            [jnp.where(hit, piece, 0.0).astype(jnp.bfloat16) for piece in split2(values_ref[...])], axis=0
+        )
         cols = cols_ref[...]
         column_hit = lax.broadcasted_iota(jnp.int32, (breadth, chunk), 0) == cols
         right = jnp.where(column_hit, 1.0, 0.0).astype(jnp.bfloat16)
@@ -97,31 +100,25 @@
     @pl.when(step == pl.num_programs(0) - 1)
     def _():
         acc = acc_ref[...]
-        g = grid_rows
-        diag_ref[...] = acc[0:g] + acc[g : 2 * g] + acc[2 * g : 3 * g]
-        rhs_ref[...] = acc[3 * g : 4 * g] + acc[4 * g : 5 * g] + acc[5 * g : 6 * g]
-
-
-def river_terms(rows, cols, diag_values, rhs_values, grid_rows, breadth):
+        out_ref[...] = acc[0:grid_rows] + acc[grid_rows : 2 * grid_rows]
+
+
+def river_terms(rows, cols, values, grid_rows, breadth):
     count = rows.shape[1]
     lane = pl.BlockSpec((1, CHUNK), lambda i: (0, i))
-    whole = pl.BlockSpec((grid_rows, breadth), lambda i: (0, 0))
     return pl.pallas_call(
         scatter_kernel,
         grid=(count // CHUNK,),
-        in_specs=[lane, lane, lane, lane],
-        out_specs=[whole, whole],
-        out_shape=[
-            jax.ShapeDtypeStruct((grid_rows, breadth), jnp.float32),
-            jax.ShapeDtypeStruct((grid_rows, breadth), jnp.float32),
-        ],
-        scratch_shapes=[pltpu.VMEM((6 * grid_rows, breadth), jnp.float32)],
+        in_specs=[lane, lane, lane],
+        out_specs=pl.BlockSpec((grid_rows, breadth), lambda i: (0, 0)),
+        out_shape=jax.ShapeDtypeStruct((grid_rows, breadth), jnp.float32),
+        scratch_shapes=[pltpu.VMEM((2 * grid_rows, breadth), jnp.float32)],
         cost_estimate=pl.CostEstimate(
-            flops=2 * 6 * grid_rows * breadth * count,
+            flops=2 * 2 * grid_rows * breadth * count,
             transcendentals=0,
-            bytes_accessed=16 * count + 8 * grid_rows * breadth,
+            bytes_accessed=12 * count + 4 * grid_rows * breadth,
         ),
-    )(rows, cols, diag_values, rhs_values)
+    )(rows, cols, values)
 
 
 def gather_kernel(top_ref, rows_ref, cols_ref, out_ref):
@@ -312,23 +309,17 @@
     place = owners * per_owner + rank
     at_place = place[None, :] == order[:, None]
     wanted = jnp.sum(jnp.where(at_place, positions[None, :], 0), axis=1)
+    in_tile = node_cells >= 0
+    bed_terms = jnp.where(in_tile, bed_given, 0.0)
+    cell_rows = jnp.where(in_tile, node_cells // breadth, -1).reshape(1, -1)
+    cell_cols = jnp.where(in_tile, node_cells % breadth, 0).reshape(1, -1)
+    top_diag = river_terms(cell_rows, cell_cols, bed_terms.reshape(1, -1), across, breadth)
     asked = lax.all_to_all(wanted, "tile", 0, 0, tiled=True)
     reply = jnp.take(section, asked, axis=0)
     sorted_section = lax.all_to_all(reply, "tile", 0, 0, tiled=True)
     slot_section = jnp.take(sorted_section, place, axis=0)
 
-    in_tile = node_cells >= 0
-    bed_terms = jnp.where(in_tile, bed_given, 0.0)
-    cell_rows = jnp.where(in_tile, node_cells // breadth, -1)
-    cell_cols = jnp.where(in_tile, node_cells % breadth, 0)
-    top_diag, top_rhs = river_terms(
-        cell_rows.reshape(1, -1),
-        cell_cols.reshape(1, -1),
-        bed_terms.reshape(1, -1),
-        (bed_terms * slot_section).reshape(1, -1),
-        across,
-        breadth,
-    )
+    top_rhs = river_terms(cell_rows, cell_cols, (bed_terms * slot_section).reshape(1, -1), across, breadth)
     river = with_ghost(jnp.stack([top_diag, top_rhs]), "tile", 1, GHOST)
     tables = jnp.stack([ks_table, alpha_table, store_table])
     head = stencil(tables, fields, planes[2 * own_layers], river, tile_count * across)

time: 208 us -> 247 us (1.19)
  Pallas kernels: 73.8 us -> 112 us
  starting transfers between devices: 54.6 us -> 57.6 us
  waiting for transfers between devices: 38.8 us -> 36.3 us
    pallas_call x1 -> x2, Pallas kernels: 41.1 us -> 79 us  [river_terms(): pl.pallas_call(scatter_kernel, grid=(count // CHUNK,), in_specs=[lane, la...]
    all_to_all x1, starting transfers between devices: 10.9 us -> 14 us  [on_device(): arrived = lax.all_to_all(sorted_in, 'tile', 0, 0, tiled=True)]
    ppermute x2, waiting for transfers between devices: 5.18 us -> 2.61 us  [with_ghost(): lax.ppermute(lax.slice_in_dim(block, 0, width, axis=dim), axis, backward)]
  transfers between devices with their start and end apart: 8 -> 8, of which waited for: 4 -> 4; matrix products, arithmetic and copies ran while one was open for 6% -> 5% of each run, Pallas kernels for 20% -> 32%
where the time goes in v7:
time: 247 us; the launch traced here: 244 us
  Pallas kernels  112 us (45%)
  starting transfers between devices  57.6 us (23%)
  waiting for transfers between devices  36.3 us (15%)
  other arithmetic  14.7 us (6%)
  between operations  14.4 us (6%)
  local copies, waits for them, and re-layouts  8.86 us (4%)
    pallas_call x2, Pallas kernels, river_terms(): pl.pallas_call(scatter_kernel, grid=(count // CHUNK,), in_specs=[lane, la...  79 us
    pallas_call x1, Pallas kernels, stencil(): pl.pallas_call(functools.partial(stencil_kernel, total_rows), in_specs=[p...  23.1 us
    all_to_all x1, starting transfers between devices, on_device(): asked = lax.all_to_all(wanted, 'tile', 0, 0, tiled=True)  20.4 us
    all_to_all x1, waiting for transfers between devices, on_device(): arrived = lax.all_to_all(sorted_in, 'tile', 0, 0, tiled=True)  15.2 us
    all_to_all x1, waiting for transfers between devices, on_device(): sorted_section = lax.all_to_all(reply, 'tile', 0, 0, tiled=True)  14.6 us
    all_to_all x1, starting transfers between devices, on_device(): arrived = lax.all_to_all(sorted_in, 'tile', 0, 0, tiled=True)  14 us
    all_to_all x1, starting transfers between devices, on_device(): sorted_section = lax.all_to_all(reply, 'tile', 0, 0, tiled=True)  13.2 us
    pallas_call x1, Pallas kernels, node_heads(): pl.pallas_call(gather_kernel, grid=(count // CHUNK,), in_specs=[pl.BlockS...  9.54 us
  transfers between devices with their start and end apart: 8, of which 4 were waited for; matrix products, arithmetic and copies ran while one was open for 5% of the time, Pallas kernels for 32%

profile of v7, /device:TPU:1, one launch (start us, length us, event | category | flops | bytes accessed | tf_op | source)
XLA Modules:
  0.0 243.6 jit_solution(18185810941905021726)
XLA Ops:
  7.2 1.0 convert_reduce_fusion
  8.9 0.8 select_reduce_fusion.1
  9.7 0.8 all_to_all.20
  10.5 20.4 %all-to-all-start = ((s32[128,2,1]{1,2,0:T(1,128)}), s32[128,2,1]{1,2,0:T(1,128)S(1)}, u32[]{:S(2)}, u32[]{:S(2)}) async-start(s32[128,2,1]{1,2,0:T(1,128)} %bitcast.13), calls=%async_computation | async-start | bytes 131072 | tf_op jit(solution)/shard_map/all_to_all | solution.py:317
  30.9 1.0 convert_element_type.9
  31.9 0.9 convert_bitcast_fusion
  32.8 0.8 pad_maximum_fusion.4
  33.6 3.5 %collective-permute-start = (f32[5,8,512]{2,1,0:T(8,128)S(1)}, f32[5,8,512]{2,1,0:T(8,128)S(1)}, u32[]{:S(2)}, u32[]{:S(2)}) collective-permute-start(f32[5,8,512]{2,1,0:T(8,128)S(1)} %get-tuple-element.6), channel_id=1, source_target_pairs={{0,4},{4,8},{8,12},{12,16},{16,20},{20,24},{24,28},{28,32},{32,36}... | collective-permute-start | bytes 245768 | tf_op jit(solution)/shard_map/ppermute | solution.py:266
  37.1 1.9 collective-permute-start.1
  39.1 1.7 fusion.1
  41.0 0.9 compare_select_fusion.8
  41.9 3.9 %all-to-all-done = s32[128,2,1]{1,2,0:T(1,128)S(1)} async-done(((s32[128,2,1]{1,2,0:T(1,128)}), s32[128,2,1]{1,2,0:T(1,128)S(1)}, u32[]{:S(2)}, u32[]{:S(2)}) %all-to-all-start) | async-done | bytes 1056 | tf_op jit(solution)/shard_map/all_to_all | solution.py:317
  46.3 0.8 reduce.8
  48.0 0.8 broadcast_select_fusion.1
  48.9 13.2 %all-to-all-start.1 = ((f32[128,2,128]{2,1,0:T(2,128)}), f32[128,2,128]{2,1,0:T(2,128)S(1)}, u32[]{:S(2)}, u32[]{:S(2)}) async-start(f32[128,2,128]{2,1,0:T(2,128)} %broadcast_select_fusion.1), calls=%async_computation.1 | async-start | bytes 262144 | tf_op jit(solution)/shard_map/all_to_all | solution.py:319
  62.6 0.9 slice.38
  63.5 14.6 %all-to-all-done.1 = f32[128,2,128]{2,1,0:T(2,128)S(1)} async-done(((f32[128,2,128]{2,1,0:T(2,128)}), f32[128,2,128]{2,1,0:T(2,128)S(1)}, u32[]{:S(2)}, u32[]{:S(2)}) %all-to-all-start.1) | async-done | bytes 131104 | tf_op jit(solution)/shard_map/all_to_all | solution.py:319
  79.0 1.0 fusion.4
  80.0 39.5 %shard_map.123 = f32[64,512]{1,0:T(8,128)} custom-call(s32[1,32768]{1,0:T(1,128)} %get-tuple-element.11.rows_ref, s32[1,32768]{1,0:T(1,128)} %get-tuple-element.10.cols_ref, f32[1,32768]{1,0:T(1,128)} %get-tuple-element.4.values_ref), custom_call_target="tpu_custom_call" | custom-call | flops 4294967296 | bytes 524288 | tf_op jit(solution)/shard_map/pallas_call | solution.py:109
  119.4 39.5 %shard_map.122 = f32[64,512]{1,0:T(8,128)} custom-call(s32[1,32768]{1,0:T(1,128)} %get-tuple-element.11.rows_ref, s32[1,32768]{1,0:T(1,128)} %get-tuple-element.10.cols_ref, f32[1,32768]{1,0:T(1,128)} %get-tuple-element.5.values_ref), custom_call_target="tpu_custom_call" | custom-call | flops 4294967296 | bytes 524288 | tf_op jit(solution)/shard_map/pallas_call | solution.py:109
  159.0 0.8 pad_maximum_fusion.6
  159.8 1.9 collective-permute-start.2
  161.7 2.6 %collective-permute-start.3 = (f32[2,8,512]{2,1,0:T(8,128)S(1)}, f32[2,8,512]{2,1,0:T(8,128)S(1)}, u32[]{:S(2)}, u32[]{:S(2)}) collective-permute-start(f32[2,8,512]{2,1,0:T(8,128)S(1)} %get-tuple-element.9), channel_id=1, source_target_pairs={{4,0},{8,4},{12,8},{16,12},{20,16},{24,20},{28,24},{32,28},{36,32}... | collective-permute-start | bytes 98312 | tf_op jit(solution)/shard_map/ppermute | solution.py:267
  164.3 2.6 %collective-permute-done.3 = f32[2,8,512]{2,1,0:T(8,128)S(1)} collective-permute-done((f32[2,8,512]{2,1,0:T(8,128)S(1)}, f32[2,8,512]{2,1,0:T(8,128)S(1)}, u32[]{:S(2)}, u32[]{:S(2)}) %collective-permute-start.3) | collective-permute-done | bytes 32800 | tf_op jit(solution)/shard_map/ppermute | solution.py:267
  167.0 1.7 copy-done.1
  168.7 23.1 %shard_map.124 = f32[8,80,512]{2,1,0:T(8,128)S(1)} custom-call(f32[3,12]{1,0:T(4,128)S(1)} %pad_maximum_fusion.7.tables_ref, f32[2,8,80,512]{3,2,1,0:T(8,128)S(1)} %copy-done.1, f32[80,512]{1,0:T(8,128)S(1)} %maximum_bitcast_fusion.land_ref, f32[2,80,512]{2,1,0:T(8,128)S(1)} %pad_maximum_fusion.1.river_ref), custom_call_target="tpu_custom_call" | custom-call | flops 131072000 | bytes 3932160 | tf_op jit(solution)/shard_map/pallas_call | solution.py:249
  192.5 9.5 %shard_map.125 = f32[1,8192]{1,0:T(1,128)} custom-call(f32[64,512]{1,0:T(8,128)} %slice_bitcast_fusion.top_ref, s32[1,8192]{1,0:T(1,128)} %get-tuple-element.13.rows_ref, s32[1,8192]{1,0:T(1,128)} %get-tuple-element.12.cols_ref), custom_call_target="tpu_custom_call" | custom-call | flops 1610612736 | bytes 229376 | tf_op jit(solution)/shard_map/pallas_call | solution.py:145
  202.6 1.5 reduce.9
  205.1 0.9 broadcast_select_fusion
  205.9 14.0 %all-to-all-start.2 = ((f32[128,2,32]{2,1,0:T(2,128)}), f32[128,2,32]{2,1,0:T(2,128)S(1)}, u32[]{:S(2)}, u32[]{:S(2)}) async-start(f32[128,2,32]{2,1,0:T(2,128)} %broadcast_select_fusion), calls=%async_computation.2 | async-start | bytes 262144 | tf_op jit(solution)/shard_map/all_to_all | solution.py:340
  220.7 15.2 %all-to-all-done.2 = f32[128,2,32]{2,1,0:T(2,128)S(1)} async-done(((f32[128,2,32]{2,1,0:T(2,128)}), f32[128,2,32]{2,1,0:T(2,128)S(1)}, u32[]{:S(2)}, u32[]{:S(2)}) %all-to-all-start.2) | async-done | bytes 32800 | tf_op jit(solution)/shard_map/all_to_all | solution.py:340
  236.0 0.8 select_reduce_fusion
  (58 shorter events, 6.7 us)
Async XLA Ops:
  7.2 40.1 %copy-start = (f32[16,128]{1,0:T(8,128)S(1)}, f32[16,128]{1,0:T(8,128)}, u32[]{:S(2)}) copy-start(f32[16,128]{1,0:T(8,128)} %param.17) | copy-start | bytes 24580
  7.2 31.9 %copy-start.7 = (s32[1,256]{1,0:T(1,128)S(1)}, s32[1,256]{1,0:T(1,128)}, u32[]{:S(2)}) copy-start(s32[1,256]{1,0:T(1,128)} %param.18) | copy-start | bytes 3076
  7.2 31.9 %copy-start.3 = (s32[1,256,128]{2,1,0:T(8,128)S(1)}, s32[1,256,128]{2,1,0:T(8,128)}, u32[]{:S(2)}) copy-start(s32[1,256,128]{2,1,0:T(8,128)} %param.20) | copy-start | bytes 393220
  10.5 35.3 %all-to-all-start = ((s32[128,2,1]{1,2,0:T(1,128)}), s32[128,2,1]{1,2,0:T(1,128)S(1)}, u32[]{:S(2)}, u32[]{:S(2)}) async-start(s32[128,2,1]{1,2,0:T(1,128)} %bitcast.13), calls=%async_computation | async-start | bytes 131072 | tf_op jit(solution)/shard_map/all_to_all | solution.py:317
  33.6 29.0 %collective-permute-start = (f32[5,8,512]{2,1,0:T(8,128)S(1)}, f32[5,8,512]{2,1,0:T(8,128)S(1)}, u32[]{:S(2)}, u32[]{:S(2)}) collective-permute-start(f32[5,8,512]{2,1,0:T(8,128)S(1)} %get-tuple-element.6), channel_id=1, source_target_pairs={{0,4},{4,8},{8,12},{12,16},{16,20},{20,24},{24,28},{28,32},{32,36}... | collective-permute-start | bytes 245768 | tf_op jit(solution)/shard_map/ppermute | solution.py:266
  37.1 25.4 %collective-permute-start.1 = (f32[5,8,512]{2,1,0:T(8,128)S(1)}, f32[5,8,512]{2,1,0:T(8,128)S(1)}, u32[]{:S(2)}, u32[]{:S(2)}) collective-permute-start(f32[5,8,512]{2,1,0:T(8,128)S(1)} %get-tuple-element.7), channel_id=1, source_target_pairs={{4,0},{8,4},{12,8},{16,12},{20,16},{24,20},{28,24},{32,28},{36,32}... | collective-permute-start | bytes 245768 | tf_op jit(solution)/shard_map/ppermute | solution.py:267
  40.8 21.6 %copy-start.8 = (f32[12]{0:T(128)S(1)}, f32[12]{0:T(128)}, u32[]{:S(2)}) copy-start(f32[12]{0:T(128)} %param.16) | copy-start | bytes 148
  40.8 21.6 %copy-start.9 = (f32[12]{0:T(128)S(1)}, f32[12]{0:T(128)}, u32[]{:S(2)}) copy-start(f32[12]{0:T(128)} %param.15) | copy-start | bytes 148
  40.8 21.6 %copy-start.10 = (f32[12]{0:T(128)S(1)}, f32[12]{0:T(128)}, u32[]{:S(2)}) copy-start(f32[12]{0:T(128)} %param.14) | copy-start | bytes 148
  40.9 21.7 %copy-start.2 = (f32[2,64,512]{2,1,0:T(8,128)S(1)}, f32[2,64,512]{2,1,0:T(8,128)}, u32[]{:S(2)}) copy-start(f32[2,64,512]{2,1,0:T(8,128)} %param.11) | copy-start | bytes 786436
  48.9 29.3 %all-to-all-start.1 = ((f32[128,2,128]{2,1,0:T(2,128)}), f32[128,2,128]{2,1,0:T(2,128)S(1)}, u32[]{:S(2)}, u32[]{:S(2)}) async-start(f32[128,2,128]{2,1,0:T(2,128)} %broadcast_select_fusion.1), calls=%async_computation.1 | async-start | bytes 262144 | tf_op jit(solution)/shard_map/all_to_all | solution.py:319
  62.1 104.9 %all-gather.2.cloned.1.call-start = ((), (), s32[]{:S(2)}) async-start(), calls=%async_computation.3 | async-start | bytes 3276800 | tf_op jit(solution)/shard_map/all_gather | solution.py:299
  63.5 15.5 %copy-start.6 = (f32[1,256,128]{2,1,0:T(8,128)S(1)}, f32[1,256,128]{2,1,0:T(8,128)}, u32[]{:S(2)}) copy-start(f32[1,256,128]{2,1,0:T(8,128)} %param.21) | copy-start | bytes 393220
  119.4 39.5 %copy-start.4 = (f32[64,512]{1,0:T(8,128)S(1)}, f32[64,512]{1,0:T(8,128)}, u32[]{:S(2)}) copy-start(f32[64,512]{1,0:T(8,128)} %shard_map.123) | copy-start | bytes 393220
  159.0 8.0 %copy-start.5 = (f32[64,512]{1,0:T(8,128)S(1)}, f32[64,512]{1,0:T(8,128)}, u32[]{:S(2)}) copy-start(f32[64,512]{1,0:T(8,128)} %shard_map.122) | copy-start | bytes 393220
  159.8 4.5 %collective-permute-start.2 = (f32[2,8,512]{2,1,0:T(8,128)S(1)}, f32[2,8,512]{2,1,0:T(8,128)S(1)}, u32[]{:S(2)}, u32[]{:S(2)}) collective-permute-start(f32[2,8,512]{2,1,0:T(8,128)S(1)} %get-tuple-element.8), channel_id=1, source_target_pairs={{0,4},{4,8},{8,12},{12,16},{16,20},{20,24},{24,28},{28,32},{32,36}... | collective-permute-start | bytes 98312 | tf_op jit(solution)/shard_map/ppermute | solution.py:266
  161.7 5.2 %collective-permute-start.3 = (f32[2,8,512]{2,1,0:T(8,128)S(1)}, f32[2,8,512]{2,1,0:T(8,128)S(1)}, u32[]{:S(2)}, u32[]{:S(2)}) collective-permute-start(f32[2,8,512]{2,1,0:T(8,128)S(1)} %get-tuple-element.9), channel_id=1, source_target_pairs={{4,0},{8,4},{12,8},{16,12},{20,16},{24,20},{28,24},{32,28},{36,32}... | collective-permute-start | bytes 98312 | tf_op jit(solution)/shard_map/ppermute | solution.py:267
  167.0 1.7 copy-start.1
  205.9 30.0 %all-to-all-start.2 = ((f32[128,2,32]{2,1,0:T(2,128)}), f32[128,2,32]{2,1,0:T(2,128)S(1)}, u32[]{:S(2)}, u32[]{:S(2)}) async-start(f32[128,2,32]{2,1,0:T(2,128)} %broadcast_select_fusion), calls=%async_computation.2 | async-start | bytes 262144 | tf_op jit(solution)/shard_map/all_to_all | solution.py:340
Sparse Core Ops, SparseCore 0:
  65.0 43.9 all-gather.1

commit v8 on v2

--- a/solution.py
+++ b/solution.py
@@ -23,7 +23,7 @@
     (2, -1, LATERAL),
     (2, 1, LATERAL),
 )
-CHUNK = 512
+CHUNK = 2048
 
 
 def beside(padded, axis_id, step):
@@ -104,11 +104,12 @@
 
 def river_terms(rows, cols, diag_values, rhs_values, grid_rows, breadth):
     count = rows.shape[1]
-    lane = pl.BlockSpec((1, CHUNK), lambda i: (0, i))
+    chunk = min(CHUNK, count)
+    lane = pl.BlockSpec((1, chunk), lambda i: (0, i))
     whole = pl.BlockSpec((grid_rows, breadth), lambda i: (0, 0))
     return pl.pallas_call(
         scatter_kernel,
-        grid=(count // CHUNK,),
+        grid=(count // chunk,),
         in_specs=[lane, lane, lane, lane],
         out_specs=[whole, whole],
         out_shape=[
@@ -116,6 +117,7 @@
             jax.ShapeDtypeStruct((grid_rows, breadth), jnp.float32),
         ],
         scratch_shapes=[pltpu.VMEM((6 * grid_rows, breadth), jnp.float32)],
+        compiler_params=pltpu.CompilerParams(vmem_limit_bytes=48 * 1024 * 1024),
         cost_estimate=pl.CostEstimate(
             flops=2 * 6 * grid_rows * breadth * count,
             transcendentals=0,
@@ -144,10 +146,12 @@
 def node_heads(top, rows, cols):
     grid_rows, breadth = top.shape
     count = rows.shape[1]
-    lane = pl.BlockSpec((1, CHUNK), lambda i: (0, i))
+    chunk = min(CHUNK, count)
+    lane = pl.BlockSpec((1, chunk), lambda i: (0, i))
     return pl.pallas_call(
         gather_kernel,
-        grid=(count // CHUNK,),
+        grid=(count // chunk,),
+        compiler_params=pltpu.CompilerParams(vmem_limit_bytes=48 * 1024 * 1024),
         in_specs=[pl.BlockSpec((grid_rows, breadth), lambda i: (0, 0)), lane, lane],
         out_specs=lane,
         out_shape=jax.ShapeDtypeStruct((1, count), jnp.float32),

time: 208 us -> 180 us (0.87)
  Pallas kernels: 73.8 us -> 41.8 us
  starting transfers between devices: 54.6 us -> 64.4 us
  other arithmetic: 14.8 us -> 11.2 us
    pallas_call x2, Pallas kernels: 50.6 us -> 18.7 us  [the longest x1 15.9 us: river_terms(): pl.pallas_call(scatter_kernel, grid=(count // chunk,), in_specs=[lane, la...]
    all_to_all x1, starting transfers between devices: 10.9 us -> 16.7 us  [on_device(): arrived = lax.all_to_all(sorted_in, 'tile', 0, 0, tiled=True)]
    ppermute x2, starting transfers between devices: 5.49 us -> 11.2 us  [with_ghost(): lax.ppermute(lax.slice_in_dim(block, size - width, size, axis=dim), axis,...]
  transfers between devices with their start and end apart: 8 -> 8, of which waited for: 4 -> 5; matrix products, arithmetic and copies ran while one was open for 6% -> 6% of each run, Pallas kernels for 20% -> 9%
where the time goes in v8:
time: 180 us; the launch traced here: 179 us
  starting transfers between devices  64.4 us (36%)
  Pallas kernels  41.8 us (23%)
  waiting for transfers between devices  38.9 us (22%)
  between operations  14.5 us (8%)
  other arithmetic  11.2 us (6%)
  local copies, waits for them, and re-layouts  8.23 us (5%)
    pallas_call x1, Pallas kernels, stencil(): pl.pallas_call(functools.partial(stencil_kernel, total_rows), in_specs=[p...  23.1 us
    all_to_all x1, starting transfers between devices, on_device(): asked = lax.all_to_all(wanted, 'tile', 0, 0, tiled=True)  20.4 us
    all_to_all x1, starting transfers between devices, on_device(): arrived = lax.all_to_all(sorted_in, 'tile', 0, 0, tiled=True)  16.7 us
    pallas_call x1, Pallas kernels, river_terms(): pl.pallas_call(scatter_kernel, grid=(count // chunk,), in_specs=[lane, la...  15.9 us
    all_to_all x1, waiting for transfers between devices, on_device(): arrived = lax.all_to_all(sorted_in, 'tile', 0, 0, tiled=True)  15.3 us
    all_to_all x1, waiting for transfers between devices, on_device(): sorted_section = lax.all_to_all(reply, 'tile', 0, 0, tiled=True)  14.6 us
    all_to_all x1, starting transfers between devices, on_device(): sorted_section = lax.all_to_all(reply, 'tile', 0, 0, tiled=True)  12.1 us
    ppermute x2, starting transfers between devices, with_ghost(): lax.ppermute(lax.slice_in_dim(block, size - width, size, axis=dim), axis,...  11.2 us
  transfers between devices with their start and end apart: 8, of which 5 were waited for; matrix products, arithmetic and copies ran while one was open for 6% of the time, Pallas kernels for 9%

profile of v8, /device:TPU:1, one launch (start us, length us, event | category | flops | bytes accessed | tf_op | source)
XLA Modules:
  0.0 179.0 jit_solution(13566638124954926277)
XLA Ops:
  7.2 1.0 convert_reduce_fusion
  8.9 0.8 select_reduce_fusion.1
  9.7 0.8 all_to_all.20
  10.5 20.4 %all-to-all-start = ((s32[128,2,1]{1,2,0:T(1,128)}), s32[128,2,1]{1,2,0:T(1,128)S(1)}, u32[]{:S(2)}, u32[]{:S(2)}) async-start(s32[128,2,1]{1,2,0:T(1,128)} %bitcast.12), calls=%async_computation | async-start | bytes 131072 | tf_op jit(solution)/shard_map/all_to_all | solution.py:319
  30.9 1.0 convert_element_type.9
  31.9 0.9 convert_bitcast_fusion
  32.8 0.8 pad_maximum_fusion.4
  33.6 3.5 %collective-permute-start = (f32[5,8,512]{2,1,0:T(8,128)S(1)}, f32[5,8,512]{2,1,0:T(8,128)S(1)}, u32[]{:S(2)}, u32[]{:S(2)}) collective-permute-start(f32[5,8,512]{2,1,0:T(8,128)S(1)} %get-tuple-element.10), channel_id=1, source_target_pairs={{0,4},{4,8},{8,12},{12,16},{16,20},{20,24},{24,28},{28,32},{32,36}... | collective-permute-start | bytes 245768 | tf_op jit(solution)/shard_map/ppermute | solution.py:273
  37.1 1.9 %collective-permute-start.1 = (f32[5,8,512]{2,1,0:T(8,128)S(1)}, f32[5,8,512]{2,1,0:T(8,128)S(1)}, u32[]{:S(2)}, u32[]{:S(2)}) collective-permute-start(f32[5,8,512]{2,1,0:T(8,128)S(1)} %get-tuple-element.11), channel_id=1, source_target_pairs={{4,0},{8,4},{12,8},{16,12},{20,16},{24,20},{28,24},{32,28},{36,32}... | collective-permute-start | bytes 245768 | tf_op jit(solution)/shard_map/ppermute | solution.py:274
  39.1 1.0 fusion.1
  40.7 5.0 %all-to-all-done = s32[128,2,1]{1,2,0:T(1,128)S(1)} async-done(((s32[128,2,1]{1,2,0:T(1,128)}), s32[128,2,1]{1,2,0:T(1,128)S(1)}, u32[]{:S(2)}, u32[]{:S(2)}) %all-to-all-start) | async-done | bytes 1056 | tf_op jit(solution)/shard_map/all_to_all | solution.py:319
  46.2 0.8 reduce.8
  47.2 0.7 gather_fusion
  48.0 0.9 broadcast_select_fusion.1
  48.8 12.1 %all-to-all-start.1 = ((f32[128,2,128]{2,1,0:T(2,128)}), f32[128,2,128]{2,1,0:T(2,128)S(1)}, u32[]{:S(2)}, u32[]{:S(2)}) async-start(f32[128,2,128]{2,1,0:T(2,128)} %broadcast_select_fusion.1), calls=%async_computation.1 | async-start | bytes 262144 | tf_op jit(solution)/shard_map/all_to_all | solution.py:321
  61.4 0.9 slice.38
  62.3 14.6 %all-to-all-done.1 = f32[128,2,128]{2,1,0:T(2,128)S(1)} async-done(((f32[128,2,128]{2,1,0:T(2,128)}), f32[128,2,128]{2,1,0:T(2,128)S(1)}, u32[]{:S(2)}, u32[]{:S(2)}) %all-to-all-start.1) | async-done | bytes 131104 | tf_op jit(solution)/shard_map/all_to_all | solution.py:321
  77.0 0.7 gather_fusion.1
  78.1 15.9 %shard_map.122 = (f32[64,512]{1,0:T(8,128)S(1)}, f32[64,512]{1,0:T(8,128)S(1)}) custom-call(s32[1,32768]{1,0:T(1,128)S(1)} %get-tuple-element.15.rows_ref, s32[1,32768]{1,0:T(1,128)S(1)} %get-tuple-element.14.cols_ref, f32[1,32768]{1,0:T(1,128)S(1)} %get-tuple-element.9.diag_in_ref, f32[1,32768]{1,0:T(1,128)S(1)} %get-tuple-element.8.rhs_in_ref), custom_call_target="tpu_custom_call" | custom-call | flops 12884901888 | bytes 786432 | tf_op jit(solution)/shard_map/pallas_call | solution.py:110
  94.0 7.6 %collective-permute-start.2 = (f32[2,8,512]{2,1,0:T(8,128)S(1)}, f32[2,8,512]{2,1,0:T(8,128)S(1)}, u32[]{:S(2)}, u32[]{:S(2)}) collective-permute-start(f32[2,8,512]{2,1,0:T(8,128)S(1)} %get-tuple-element.12), channel_id=1, source_target_pairs={{0,4},{4,8},{8,12},{12,16},{16,20},{20,24},{24,28},{28,32},{32,36}... | collective-permute-start | bytes 98312 | tf_op jit(solution)/shard_map/ppermute | solution.py:273
  101.6 2.1 %collective-permute-start.3 = (f32[2,8,512]{2,1,0:T(8,128)S(1)}, f32[2,8,512]{2,1,0:T(8,128)S(1)}, u32[]{:S(2)}, u32[]{:S(2)}) collective-permute-start(f32[2,8,512]{2,1,0:T(8,128)S(1)} %get-tuple-element.13), channel_id=1, source_target_pairs={{4,0},{8,4},{12,8},{16,12},{20,16},{24,20},{28,24},{32,28},{36,32}... | collective-permute-start | bytes 98312 | tf_op jit(solution)/shard_map/ppermute | solution.py:274
  103.8 3.5 %collective-permute-done.3 = f32[2,8,512]{2,1,0:T(8,128)S(1)} collective-permute-done((f32[2,8,512]{2,1,0:T(8,128)S(1)}, f32[2,8,512]{2,1,0:T(8,128)S(1)}, u32[]{:S(2)}, u32[]{:S(2)}) %collective-permute-start.3) | collective-permute-done | bytes 32800 | tf_op jit(solution)/shard_map/ppermute | solution.py:274
  107.8 1.7 copy-done.1
  109.5 23.1 %shard_map.123 = f32[8,80,512]{2,1,0:T(8,128)S(1)} custom-call(f32[3,12]{1,0:T(4,128)S(1)} %pad_maximum_fusion.7.tables_ref, f32[2,8,80,512]{3,2,1,0:T(8,128)S(1)} %copy-done.1, f32[80,512]{1,0:T(8,128)S(1)} %maximum_bitcast_fusion.land_ref, f32[2,80,512]{2,1,0:T(8,128)S(1)} %pad_maximum_fusion.1.river_ref), custom_call_target="tpu_custom_call" | custom-call | flops 131072000 | bytes 3932160 | tf_op jit(solution)/shard_map/pallas_call | solution.py:256
  132.7 2.8 %shard_map.124 = f32[1,8192]{1,0:T(1,128)S(1)} custom-call(f32[64,512]{1,0:T(8,128)S(1)} %slice_bitcast_fusion.top_ref, s32[1,8192]{1,0:T(1,128)S(1)} %get-tuple-element.17.rows_ref, s32[1,8192]{1,0:T(1,128)S(1)} %get-tuple-element.16.cols_ref), custom_call_target="tpu_custom_call" | custom-call | flops 1610612736 | bytes 229376 | tf_op jit(solution)/shard_map/pallas_call | solution.py:151
  136.0 0.7 reduce.9
  137.0 0.7 gather_fusion.2
  137.7 0.9 broadcast_select_fusion
  138.6 16.7 %all-to-all-start.2 = ((f32[128,2,32]{2,1,0:T(2,128)}), f32[128,2,32]{2,1,0:T(2,128)S(1)}, u32[]{:S(2)}, u32[]{:S(2)}) async-start(f32[128,2,32]{2,1,0:T(2,128)} %broadcast_select_fusion), calls=%async_computation.2 | async-start | bytes 262144 | tf_op jit(solution)/shard_map/all_to_all | solution.py:353
  155.4 0.7 constant_dynamic-slice_fusion.1
  156.1 15.3 %all-to-all-done.2 = f32[128,2,32]{2,1,0:T(2,128)S(1)} async-done(((f32[128,2,32]{2,1,0:T(2,128)}), f32[128,2,32]{2,1,0:T(2,128)S(1)}, u32[]{:S(2)}, u32[]{:S(2)}) %all-to-all-start.2) | async-done | bytes 32800 | tf_op jit(solution)/shard_map/all_to_all | solution.py:353
  171.4 0.8 select_reduce_fusion
  (53 shorter events, 4.2 us)
Async XLA Ops:
  7.2 40.1 %copy-start = (f32[16,128]{1,0:T(8,128)S(1)}, f32[16,128]{1,0:T(8,128)}, u32[]{:S(2)}) copy-start(f32[16,128]{1,0:T(8,128)} %param.17) | copy-start | bytes 24580
  7.2 31.9 %copy-start.5 = (s32[1,256]{1,0:T(1,128)S(1)}, s32[1,256]{1,0:T(1,128)}, u32[]{:S(2)}) copy-start(s32[1,256]{1,0:T(1,128)} %param.18) | copy-start | bytes 3076
  7.2 31.9 %copy-start.3 = (s32[1,256,128]{2,1,0:T(8,128)S(1)}, s32[1,256,128]{2,1,0:T(8,128)}, u32[]{:S(2)}) copy-start(s32[1,256,128]{2,1,0:T(8,128)} %param.20) | copy-start | bytes 393220
  10.5 35.2 %all-to-all-start = ((s32[128,2,1]{1,2,0:T(1,128)}), s32[128,2,1]{1,2,0:T(1,128)S(1)}, u32[]{:S(2)}, u32[]{:S(2)}) async-start(s32[128,2,1]{1,2,0:T(1,128)} %bitcast.12), calls=%async_computation | async-start | bytes 131072 | tf_op jit(solution)/shard_map/all_to_all | solution.py:319
  33.6 27.7 %collective-permute-start = (f32[5,8,512]{2,1,0:T(8,128)S(1)}, f32[5,8,512]{2,1,0:T(8,128)S(1)}, u32[]{:S(2)}, u32[]{:S(2)}) collective-permute-start(f32[5,8,512]{2,1,0:T(8,128)S(1)} %get-tuple-element.10), channel_id=1, source_target_pairs={{0,4},{4,8},{8,12},{12,16},{16,20},{20,24},{24,28},{28,32},{32,36}... | collective-permute-start | bytes 245768 | tf_op jit(solution)/shard_map/ppermute | solution.py:273
  37.1 24.2 %collective-permute-start.1 = (f32[5,8,512]{2,1,0:T(8,128)S(1)}, f32[5,8,512]{2,1,0:T(8,128)S(1)}, u32[]{:S(2)}, u32[]{:S(2)}) collective-permute-start(f32[5,8,512]{2,1,0:T(8,128)S(1)} %get-tuple-element.11), channel_id=1, source_target_pairs={{4,0},{8,4},{12,8},{16,12},{20,16},{24,20},{28,24},{32,28},{36,32}... | collective-permute-start | bytes 245768 | tf_op jit(solution)/shard_map/ppermute | solution.py:274
  40.1 21.0 %copy-start.6 = (f32[12]{0:T(128)S(1)}, f32[12]{0:T(128)}, u32[]{:S(2)}) copy-start(f32[12]{0:T(128)} %param.16) | copy-start | bytes 148
  40.1 21.0 %copy-start.7 = (f32[12]{0:T(128)S(1)}, f32[12]{0:T(128)}, u32[]{:S(2)}) copy-start(f32[12]{0:T(128)} %param.15) | copy-start | bytes 148
  40.1 21.0 %copy-start.8 = (f32[12]{0:T(128)S(1)}, f32[12]{0:T(128)}, u32[]{:S(2)}) copy-start(f32[12]{0:T(128)} %param.14) | copy-start | bytes 148
  40.2 21.1 %copy-start.2 = (f32[2,64,512]{2,1,0:T(8,128)S(1)}, f32[2,64,512]{2,1,0:T(8,128)}, u32[]{:S(2)}) copy-start(f32[2,64,512]{2,1,0:T(8,128)} %param.11) | copy-start | bytes 786436
  48.8 28.1 %all-to-all-start.1 = ((f32[128,2,128]{2,1,0:T(2,128)}), f32[128,2,128]{2,1,0:T(2,128)S(1)}, u32[]{:S(2)}, u32[]{:S(2)}) async-start(f32[128,2,128]{2,1,0:T(2,128)} %broadcast_select_fusion.1), calls=%async_computation.1 | async-start | bytes 262144 | tf_op jit(solution)/shard_map/all_to_all | solution.py:321
  60.9 46.9 %all-gather.2.cloned.1.call-start = ((), (), s32[]{:S(2)}) async-start(), calls=%async_computation.3 | async-start | bytes 3276800 | tf_op jit(solution)/shard_map/all_gather | solution.py:306
  62.3 15.5 %copy-start.4 = (f32[1,256,128]{2,1,0:T(8,128)S(1)}, f32[1,256,128]{2,1,0:T(8,128)}, u32[]{:S(2)}) copy-start(f32[1,256,128]{2,1,0:T(8,128)} %param.21) | copy-start | bytes 393220
  94.0 9.8 %collective-permute-start.2 = (f32[2,8,512]{2,1,0:T(8,128)S(1)}, f32[2,8,512]{2,1,0:T(8,128)S(1)}, u32[]{:S(2)}, u32[]{:S(2)}) collective-permute-start(f32[2,8,512]{2,1,0:T(8,128)S(1)} %get-tuple-element.12), channel_id=1, source_target_pairs={{0,4},{4,8},{8,12},{12,16},{16,20},{20,24},{24,28},{28,32},{32,36}... | collective-permute-start | bytes 98312 | tf_op jit(solution)/shard_map/ppermute | solution.py:273
  101.6 5.6 %collective-permute-start.3 = (f32[2,8,512]{2,1,0:T(8,128)S(1)}, f32[2,8,512]{2,1,0:T(8,128)S(1)}, u32[]{:S(2)}, u32[]{:S(2)}) collective-permute-start(f32[2,8,512]{2,1,0:T(8,128)S(1)} %get-tuple-element.13), channel_id=1, source_target_pairs={{4,0},{8,4},{12,8},{16,12},{20,16},{24,20},{28,24},{32,28},{36,32}... | collective-permute-start | bytes 98312 | tf_op jit(solution)/shard_map/ppermute | solution.py:274
  107.8 1.7 copy-start.1
  138.6 32.8 %all-to-all-start.2 = ((f32[128,2,32]{2,1,0:T(2,128)}), f32[128,2,32]{2,1,0:T(2,128)S(1)}, u32[]{:S(2)}, u32[]{:S(2)}) async-start(f32[128,2,32]{2,1,0:T(2,128)} %broadcast_select_fusion), calls=%async_computation.2 | async-start | bytes 262144 | tf_op jit(solution)/shard_map/all_to_all | solution.py:353
Sparse Core Ops, SparseCore 0:
  63.8 43.8 all-gather.1

commit v9 on v8

--- a/solution.py
+++ b/solution.py
@@ -23,7 +23,7 @@
     (2, -1, LATERAL),
     (2, 1, LATERAL),
 )
-CHUNK = 2048
+CHUNK = 4096
 
 
 def beside(padded, axis_id, step):
@@ -297,13 +297,11 @@
     quarter = node_count // layer_count
     node_first = layer * quarter
 
-    planes = jnp.concatenate(
-        [head_start, soil_class.astype(jnp.float32), land_mask.astype(jnp.float32)[None]], axis=0
-    )
-    planes = with_ghost(planes, "tile", 1, GHOST)
-    extent = across + 2 * GHOST
-    fields = planes[: 2 * own_layers].reshape(2, own_layers, extent, breadth)
+    fields = jnp.stack([head_start, soil_class.astype(jnp.float32)])
     fields = lax.all_gather(fields, "layer", axis=1, tiled=True)
+    fields = with_ghost(fields, "tile", 2, GHOST)
+    land = with_ghost(land_mask.astype(jnp.float32), "tile", 0, GHOST)
+
     owners = cross_owner[0]
     positions = cross_local[0]
     node_cells = node_cell[0]
@@ -335,7 +333,7 @@
     )
     river = with_ghost(jnp.stack([top_diag, top_rhs]), "tile", 1, GHOST)
     tables = jnp.stack([ks_table, alpha_table, store_table])
-    head = stencil(tables, fields, planes[2 * own_layers], river, tile_count * across)
+    head = stencil(tables, fields, land, river, tile_count * across)
     kept = lax.dynamic_slice_in_dim(head[:, GHOST : GHOST + across], layer * own_layers, own_layers, 0)
 
     top_head = head[0, GHOST : GHOST + across]

time: 180 us -> 183 us (1.017)
  waiting for transfers between devices: 38.9 us -> 45 us
  starting transfers between devices: 64.4 us -> 60.2 us
  Pallas kernels: 41.8 us -> 43.7 us
    ppermute x2 -> x3, starting transfers between devices: 4.02 us -> 12.6 us  [with_ghost(): lax.ppermute(lax.slice_in_dim(block, 0, width, axis=dim), axis, backward)]
    all_to_all x1, waiting for transfers between devices: 5.05 us -> 13.1 us  [on_device(): asked = lax.all_to_all(wanted, 'tile', 0, 0, tiled=True)]
    all_to_all x1, starting transfers between devices: 12.1 us -> 5.67 us  [on_device(): sorted_section = lax.all_to_all(reply, 'tile', 0, 0, tiled=True)]
    all_to_all x1, starting transfers between devices: 20.4 us -> 16.5 us  [on_device(): asked = lax.all_to_all(wanted, 'tile', 0, 0, tiled=True)]
    ppermute x2 -> x3, waiting for transfers between devices: 3.5 us -> 0.01 us  [with_ghost(): lax.ppermute(lax.slice_in_dim(block, 0, width, axis=dim), axis, backward)]
    another operation x0 -> x2, other arithmetic: none -> 2.82 us  [on_device(): fields = jnp.stack([head_start, soil_class.astype(jnp.float32)])]
    ppermute x2 -> x3, starting transfers between devices: 11.2 us -> 9.39 us  [with_ghost(): lax.ppermute(lax.slice_in_dim(block, size - width, size, axis=dim), axis,...]
  transfers between devices with their start and end apart: 8 -> 10, of which waited for: 5 -> 4; matrix products, arithmetic and copies ran while one was open for 6% -> 6% of each run, Pallas kernels for 9% -> 9%
where the time goes in v9:
time: 183 us
  starting transfers between devices  60.2 us (33%)
  waiting for transfers between devices  45 us (25%)
  Pallas kernels  43.7 us (24%)
  between operations  14.5 us (8%)
  other arithmetic  12.6 us (7%)
  local copies, waits for them, and re-layouts  6.84 us (4%)
    pallas_call x1, Pallas kernels, stencil(): pl.pallas_call(functools.partial(stencil_kernel, total_rows), in_specs=[p...  24.6 us
    pallas_call x1, Pallas kernels, river_terms(): pl.pallas_call(scatter_kernel, grid=(count // chunk,), in_specs=[lane, la...  16.5 us
    all_to_all x1, starting transfers between devices, on_device(): asked = lax.all_to_all(wanted, 'tile', 0, 0, tiled=True)  16.5 us
    all_to_all x1, starting transfers between devices, on_device(): arrived = lax.all_to_all(sorted_in, 'tile', 0, 0, tiled=True)  15.9 us
    all_to_all x1, waiting for transfers between devices, on_device(): sorted_section = lax.all_to_all(reply, 'tile', 0, 0, tiled=True)  15.9 us
    all_to_all x1, waiting for transfers between devices, on_device(): arrived = lax.all_to_all(sorted_in, 'tile', 0, 0, tiled=True)  15.2 us
    all_to_all x1, waiting for transfers between devices, on_device(): asked = lax.all_to_all(wanted, 'tile', 0, 0, tiled=True)  13.1 us
    ppermute x3, starting transfers between devices, with_ghost(): lax.ppermute(lax.slice_in_dim(block, 0, width, axis=dim), axis, backward)  12.6 us
  transfers between devices with their start and end apart: 10, of which 4 were waited for; matrix products, arithmetic and copies ran while one was open for 6% of the time, Pallas kernels for 9%

profile of v9, /device:TPU:1, one launch (start us, length us, event | category | flops | bytes accessed | tf_op | source)
XLA Modules:
  0.0 182.9 jit_solution(18125614475406527495)
XLA Ops:
  7.2 1.0 convert_bitcast_fusion
  8.3 1.8 pad_maximum_fusion.1
  10.1 1.0 convert_element_type.10
  11.1 8.8 %collective-permute-start.3 = (f32[8,512]{1,0:T(8,128)S(1)}, f32[8,512]{1,0:T(8,128)S(1)}, u32[]{:S(2)}, u32[]{:S(2)}) collective-permute-start(f32[8,512]{1,0:T(8,128)S(1)} %get-tuple-element.17), channel_id=1, source_target_pairs={{4,0},{8,4},{12,8},{16,12},{20,16},{24,20},{28,24},{32,28},{36,32}... | collective-permute-start | bytes 49160 | tf_op jit(solution)/shard_map/ppermute | solution.py:274
  19.9 1.9 %collective-permute-start.2 = (f32[8,512]{1,0:T(8,128)S(1)}, f32[8,512]{1,0:T(8,128)S(1)}, u32[]{:S(2)}, u32[]{:S(2)}) collective-permute-start(f32[8,512]{1,0:T(8,128)S(1)} %get-tuple-element.16), channel_id=1, source_target_pairs={{0,4},{4,8},{8,12},{12,16},{16,20},{20,24},{24,28},{28,32},{32,36}... | collective-permute-start | bytes 49160 | tf_op jit(solution)/shard_map/ppermute | solution.py:273
  21.8 0.9 convert_reduce_fusion
  23.5 0.8 select_reduce_fusion.1
  24.3 0.8 all_to_all.20
  25.1 16.5 %all-to-all-start = ((s32[128,2,1]{1,2,0:T(1,128)}), s32[128,2,1]{1,2,0:T(1,128)S(1)}, u32[]{:S(2)}, u32[]{:S(2)}) async-start(s32[128,2,1]{1,2,0:T(1,128)} %bitcast.11), calls=%async_computation | async-start | bytes 131072 | tf_op jit(solution)/shard_map/all_to_all | solution.py:317
  41.6 1.0 fusion.1
  43.3 13.1 %all-to-all-done = s32[128,2,1]{1,2,0:T(1,128)S(1)} async-done(((s32[128,2,1]{1,2,0:T(1,128)}), s32[128,2,1]{1,2,0:T(1,128)S(1)}, u32[]{:S(2)}, u32[]{:S(2)}) %all-to-all-start) | async-done | bytes 1056 | tf_op jit(solution)/shard_map/all_to_all | solution.py:317
  56.9 0.8 reduce.8
  58.0 0.7 gather_fusion
  58.7 0.9 broadcast_select_fusion.1
  59.6 5.7 %all-to-all-start.1 = ((f32[128,2,128]{2,1,0:T(2,128)}), f32[128,2,128]{2,1,0:T(2,128)S(1)}, u32[]{:S(2)}, u32[]{:S(2)}) async-start(f32[128,2,128]{2,1,0:T(2,128)} %broadcast_select_fusion.1), calls=%async_computation.1 | async-start | bytes 262144 | tf_op jit(solution)/shard_map/all_to_all | solution.py:319
  65.5 15.9 %all-to-all-done.1 = f32[128,2,128]{2,1,0:T(2,128)S(1)} async-done(((f32[128,2,128]{2,1,0:T(2,128)}), f32[128,2,128]{2,1,0:T(2,128)S(1)}, u32[]{:S(2)}, u32[]{:S(2)}) %all-to-all-start.1) | async-done | bytes 131104 | tf_op jit(solution)/shard_map/all_to_all | solution.py:319
  81.3 0.7 gather_fusion.1
  82.5 16.5 %shard_map.122 = (f32[64,512]{1,0:T(8,128)S(1)}, f32[64,512]{1,0:T(8,128)S(1)}) custom-call(s32[1,32768]{1,0:T(1,128)S(1)} %get-tuple-element.15.rows_ref, s32[1,32768]{1,0:T(1,128)S(1)} %get-tuple-element.14.cols_ref, f32[1,32768]{1,0:T(1,128)S(1)} %get-tuple-element.9.diag_in_ref, f32[1,32768]{1,0:T(1,128)S(1)} %get-tuple-element.8.rhs_in_ref), custom_call_target="tpu_custom_call" | custom-call | flops 12884901888 | bytes 786432 | tf_op jit(solution)/shard_map/pallas_call | solution.py:110
  99.1 1.2 fusion.5
  100.3 1.9 %collective-permute-start.1 = (f32[2,8,8,512]{3,2,1,0:T(8,128)S(1)}, f32[2,8,8,512]{3,2,1,0:T(8,128)S(1)}, u32[]{:S(2)}, u32[]{:S(2)}) collective-permute-start(f32[2,8,8,512]{3,2,1,0:T(8,128)S(1)} %get-tuple-element.11), channel_id=1, source_target_pairs={{4,0},{8,4},{12,8},{16,12},{20,16},{24,20},{28,24},{32,28},{36,32}... | collective-permute-start | bytes 786440 | tf_op jit(solution)/shard_map/ppermute | solution.py:274
  102.2 3.6 %collective-permute-start = (f32[2,8,8,512]{3,2,1,0:T(8,128)S(1)}, f32[2,8,8,512]{3,2,1,0:T(8,128)S(1)}, u32[]{:S(2)}, u32[]{:S(2)}) collective-permute-start(f32[2,8,8,512]{3,2,1,0:T(8,128)S(1)} %get-tuple-element.10), channel_id=1, source_target_pairs={{0,4},{4,8},{8,12},{12,16},{16,20},{20,24},{24,28},{28,32},{32,36}... | collective-permute-start | bytes 786440 | tf_op jit(solution)/shard_map/ppermute | solution.py:273
  105.9 1.9 %collective-permute-start.5 = (f32[2,8,512]{2,1,0:T(8,128)S(1)}, f32[2,8,512]{2,1,0:T(8,128)S(1)}, u32[]{:S(2)}, u32[]{:S(2)}) collective-permute-start(f32[2,8,512]{2,1,0:T(8,128)S(1)} %get-tuple-element.13), channel_id=1, source_target_pairs={{4,0},{8,4},{12,8},{16,12},{20,16},{24,20},{28,24},{32,28},{36,32}... | collective-permute-start | bytes 98312 | tf_op jit(solution)/shard_map/ppermute | solution.py:274
  107.8 3.8 %collective-permute-start.4 = (f32[2,8,512]{2,1,0:T(8,128)S(1)}, f32[2,8,512]{2,1,0:T(8,128)S(1)}, u32[]{:S(2)}, u32[]{:S(2)}) collective-permute-start(f32[2,8,512]{2,1,0:T(8,128)S(1)} %get-tuple-element.12), channel_id=1, source_target_pairs={{0,4},{4,8},{8,12},{12,16},{16,20},{20,24},{24,28},{28,32},{32,36}... | collective-permute-start | bytes 98312 | tf_op jit(solution)/shard_map/ppermute | solution.py:273
  111.7 0.8 collective-permute-done.4
  112.9 24.6 %shard_map.123 = f32[8,80,512]{2,1,0:T(8,128)S(1)} custom-call(f32[3,12]{1,0:T(4,128)S(1)} %pad_maximum_fusion.6.tables_ref, f32[2,8,80,512]{3,2,1,0:T(8,128)S(1)} %pad_maximum_fusion.fields_ref, f32[80,512]{1,0:T(8,128)S(1)} %pad_maximum_fusion.3.land_ref, f32[2,80,512]{2,1,0:T(8,128)S(1)} %pad_maximum_fusion.2.river_ref), custom_call_target="tpu_custom_call" | custom-call | flops 131072000 | bytes 3932160 | tf_op jit(solution)/shard_map/pallas_call | solution.py:256
  137.6 2.5 %shard_map.124 = f32[1,8192]{1,0:T(1,128)S(1)} custom-call(f32[64,512]{1,0:T(8,128)S(1)} %slice_bitcast_fusion.top_ref, s32[1,8192]{1,0:T(1,128)S(1)} %get-tuple-element.19.rows_ref, s32[1,8192]{1,0:T(1,128)S(1)} %get-tuple-element.18.cols_ref), custom_call_target="tpu_custom_call" | custom-call | flops 1610612736 | bytes 229376 | tf_op jit(solution)/shard_map/pallas_call | solution.py:151
  141.6 0.7 gather_fusion.2
  142.3 0.9 broadcast_select_fusion
  143.2 15.9 %all-to-all-start.2 = ((f32[128,2,32]{2,1,0:T(2,128)}), f32[128,2,32]{2,1,0:T(2,128)S(1)}, u32[]{:S(2)}, u32[]{:S(2)}) async-start(f32[128,2,32]{2,1,0:T(2,128)} %broadcast_select_fusion), calls=%async_computation.2 | async-start | bytes 262144 | tf_op jit(solution)/shard_map/all_to_all | solution.py:351
  159.2 0.7 constant_dynamic-slice_fusion.1
  160.0 15.2 %all-to-all-done.2 = f32[128,2,32]{2,1,0:T(2,128)S(1)} async-done(((f32[128,2,32]{2,1,0:T(2,128)}), f32[128,2,32]{2,1,0:T(2,128)S(1)}, u32[]{:S(2)}, u32[]{:S(2)}) %all-to-all-start.2) | async-done | bytes 32800 | tf_op jit(solution)/shard_map/all_to_all | solution.py:351
  175.3 0.8 select_reduce_fusion
  (56 shorter events, 4.8 us)
Async XLA Ops:
  7.2 50.8 %copy-start = (f32[16,128]{1,0:T(8,128)S(1)}, f32[16,128]{1,0:T(8,128)}, u32[]{:S(2)}) copy-start(f32[16,128]{1,0:T(8,128)} %param.17) | copy-start | bytes 24580
  7.2 35.4 %copy-start.4 = (s32[1,256]{1,0:T(1,128)S(1)}, s32[1,256]{1,0:T(1,128)}, u32[]{:S(2)}) copy-start(s32[1,256]{1,0:T(1,128)} %param.18) | copy-start | bytes 3076
  7.2 34.4 %copy-start.2 = (s32[1,256,128]{2,1,0:T(8,128)S(1)}, s32[1,256,128]{2,1,0:T(8,128)}, u32[]{:S(2)}) copy-start(s32[1,256,128]{2,1,0:T(8,128)} %param.20) | copy-start | bytes 393220
  7.2 91.9 %all-gather.2.cloned.1.call-start = ((), (), s32[]{:S(2)}) async-start(), calls=%async_computation.3 | async-start | bytes 2621440 | tf_op jit(solution)/shard_map/all_gather | solution.py:301
  8.3 57.0 %copy-start.5 = (f32[12]{0:T(128)S(1)}, f32[12]{0:T(128)}, u32[]{:S(2)}) copy-start(f32[12]{0:T(128)} %param.16) | copy-start | bytes 148
  8.3 57.0 %copy-start.6 = (f32[12]{0:T(128)S(1)}, f32[12]{0:T(128)}, u32[]{:S(2)}) copy-start(f32[12]{0:T(128)} %param.15) | copy-start | bytes 148
  8.3 57.0 %copy-start.7 = (f32[12]{0:T(128)S(1)}, f32[12]{0:T(128)}, u32[]{:S(2)}) copy-start(f32[12]{0:T(128)} %param.14) | copy-start | bytes 148
  10.1 72.0 %copy-start.3 = (f32[1,256,128]{2,1,0:T(8,128)S(1)}, f32[1,256,128]{2,1,0:T(8,128)}, u32[]{:S(2)}) copy-start(f32[1,256,128]{2,1,0:T(8,128)} %param.21) | copy-start | bytes 393220
  11.1 96.7 %collective-permute-start.3 = (f32[8,512]{1,0:T(8,128)S(1)}, f32[8,512]{1,0:T(8,128)S(1)}, u32[]{:S(2)}, u32[]{:S(2)}) collective-permute-start(f32[8,512]{1,0:T(8,128)S(1)} %get-tuple-element.17), channel_id=1, source_target_pairs={{4,0},{8,4},{12,8},{16,12},{20,16},{24,20},{28,24},{32,28},{36,32}... | collective-permute-start | bytes 49160 | tf_op jit(solution)/shard_map/ppermute | solution.py:274
  19.9 91.8 %collective-permute-start.2 = (f32[8,512]{1,0:T(8,128)S(1)}, f32[8,512]{1,0:T(8,128)S(1)}, u32[]{:S(2)}, u32[]{:S(2)}) collective-permute-start(f32[8,512]{1,0:T(8,128)S(1)} %get-tuple-element.16), channel_id=1, source_target_pairs={{0,4},{4,8},{8,12},{12,16},{16,20},{20,24},{24,28},{28,32},{32,36}... | collective-permute-start | bytes 49160 | tf_op jit(solution)/shard_map/ppermute | solution.py:273
  25.1 31.4 %all-to-all-start = ((s32[128,2,1]{1,2,0:T(1,128)}), s32[128,2,1]{1,2,0:T(1,128)S(1)}, u32[]{:S(2)}, u32[]{:S(2)}) async-start(s32[128,2,1]{1,2,0:T(1,128)} %bitcast.11), calls=%async_computation | async-start | bytes 131072 | tf_op jit(solution)/shard_map/all_to_all | solution.py:317
  59.6 21.8 %all-to-all-start.1 = ((f32[128,2,128]{2,1,0:T(2,128)}), f32[128,2,128]{2,1,0:T(2,128)S(1)}, u32[]{:S(2)}, u32[]{:S(2)}) async-start(f32[128,2,128]{2,1,0:T(2,128)} %broadcast_select_fusion.1), calls=%async_computation.1 | async-start | bytes 262144 | tf_op jit(solution)/shard_map/all_to_all | solution.py:319
  99.1 13.5 %copy-start.1 = (f32[2,8,64,512]{3,2,1,0:T(8,128)S(1)}, f32[2,8,64,512]{3,2,1,0:T(8,128)}, u32[]{:S(2)}) copy-start(f32[2,8,64,512]{3,2,1,0:T(8,128)} %all-gather.2.cloned.1.call-done) | copy-start | bytes 6291460
  100.3 12.2 %collective-permute-start.1 = (f32[2,8,8,512]{3,2,1,0:T(8,128)S(1)}, f32[2,8,8,512]{3,2,1,0:T(8,128)S(1)}, u32[]{:S(2)}, u32[]{:S(2)}) collective-permute-start(f32[2,8,8,512]{3,2,1,0:T(8,128)S(1)} %get-tuple-element.11), channel_id=1, source_target_pairs={{4,0},{8,4},{12,8},{16,12},{20,16},{24,20},{28,24},{32,28},{36,32}... | collective-permute-start | bytes 786440 | tf_op jit(solution)/shard_map/ppermute | solution.py:274
  102.2 10.3 %collective-permute-start = (f32[2,8,8,512]{3,2,1,0:T(8,128)S(1)}, f32[2,8,8,512]{3,2,1,0:T(8,128)S(1)}, u32[]{:S(2)}, u32[]{:S(2)}) collective-permute-start(f32[2,8,8,512]{3,2,1,0:T(8,128)S(1)} %get-tuple-element.10), channel_id=1, source_target_pairs={{0,4},{4,8},{8,12},{12,16},{16,20},{20,24},{24,28},{28,32},{32,36}... | collective-permute-start | bytes 786440 | tf_op jit(solution)/shard_map/ppermute | solution.py:273
  105.9 5.8 %collective-permute-start.5 = (f32[2,8,512]{2,1,0:T(8,128)S(1)}, f32[2,8,512]{2,1,0:T(8,128)S(1)}, u32[]{:S(2)}, u32[]{:S(2)}) collective-permute-start(f32[2,8,512]{2,1,0:T(8,128)S(1)} %get-tuple-element.13), channel_id=1, source_target_pairs={{4,0},{8,4},{12,8},{16,12},{20,16},{24,20},{28,24},{32,28},{36,32}... | collective-permute-start | bytes 98312 | tf_op jit(solution)/shard_map/ppermute | solution.py:274
  107.8 4.7 %collective-permute-start.4 = (f32[2,8,512]{2,1,0:T(8,128)S(1)}, f32[2,8,512]{2,1,0:T(8,128)S(1)}, u32[]{:S(2)}, u32[]{:S(2)}) collective-permute-start(f32[2,8,512]{2,1,0:T(8,128)S(1)} %get-tuple-element.12), channel_id=1, source_target_pairs={{0,4},{4,8},{8,12},{12,16},{16,20},{20,24},{24,28},{28,32},{32,36}... | collective-permute-start | bytes 98312 | tf_op jit(solution)/shard_map/ppermute | solution.py:273
  143.2 32.0 %all-to-all-start.2 = ((f32[128,2,32]{2,1,0:T(2,128)}), f32[128,2,32]{2,1,0:T(2,128)S(1)}, u32[]{:S(2)}, u32[]{:S(2)}) async-start(f32[128,2,32]{2,1,0:T(2,128)} %broadcast_select_fusion), calls=%async_computation.2 | async-start | bytes 262144 | tf_op jit(solution)/shard_map/all_to_all | solution.py:351
Sparse Core Ops, SparseCore 0:
  10.3 43.8 all-gather.1

commit v10 on v9

--- a/solution.py
+++ b/solution.py
@@ -298,8 +298,11 @@
     node_first = layer * quarter
 
     fields = jnp.stack([head_start, soil_class.astype(jnp.float32)])
+    edges = with_ghost(fields, "tile", 2, GHOST)
+    edges = jnp.concatenate([edges[:, :, :GHOST], edges[:, :, GHOST + across :]], axis=2)
     fields = lax.all_gather(fields, "layer", axis=1, tiled=True)
-    fields = with_ghost(fields, "tile", 2, GHOST)
+    edges = lax.all_gather(edges, "layer", axis=1, tiled=True)
+    fields = jnp.concatenate([edges[:, :, :GHOST], fields, edges[:, :, GHOST:]], axis=2)
     land = with_ghost(land_mask.astype(jnp.float32), "tile", 0, GHOST)
 
     owners = cross_owner[0]

time: 183 us -> 184 us (level)
  waiting for transfers between devices: 45 us -> 32.9 us
  blocking collectives: 0 us -> 12.1 us
  starting transfers between devices: 60.2 us -> 66.4 us
  Pallas kernels: 43.7 us -> 40.1 us
    all_to_all x1, waiting for transfers between devices: 15.9 us -> 3.75 us  [on_device(): sorted_section = lax.all_to_all(reply, 'tile', 0, 0, tiled=True)]
    all_gather x0 -> x1, blocking collectives: none -> 12.1 us  [on_device(): edges = lax.all_gather(edges, 'layer', axis=1, tiled=True)]
    pallas_call x1, Pallas kernels: 16.5 us -> 12.9 us  [river_terms(): pl.pallas_call(scatter_kernel, grid=(count // chunk,), in_specs=[lane, la...]
    all_to_all x1, starting transfers between devices: 16.5 us -> 19.7 us  [on_device(): asked = lax.all_to_all(wanted, 'tile', 0, 0, tiled=True)]
    all_to_all x1, starting transfers between devices: 15.9 us -> 18.8 us  [on_device(): arrived = lax.all_to_all(sorted_in, 'tile', 0, 0, tiled=True)]
    concatenate x0 -> x2, other arithmetic: none -> 1.93 us  [the longest x1 1.92 us: on_device(): jnp.concatenate([edges[:, :, :GHOST], fields, edges[:, :, GHOST:]], axis=2)]
  transfers between devices with their start and end apart: 10 -> 10, of which waited for: 4 -> 4; matrix products, arithmetic and copies ran while one was open for 6% -> 5% of each run, Pallas kernels for 9% -> 7%
where the time goes in v10:
time: 184 us
  starting transfers between devices  66.4 us (36%)
  Pallas kernels  40.1 us (22%)
  waiting for transfers between devices  32.9 us (18%)
  between operations  14.6 us (8%)
  blocking collectives  12.1 us (7%)
  other arithmetic  11.9 us (6%)
  local copies, waits for them, and re-layouts  5.66 us (3%)
    pallas_call x1, Pallas kernels, stencil(): pl.pallas_call(functools.partial(stencil_kernel, total_rows), in_specs=[p...  24.7 us
    all_to_all x1, starting transfers between devices, on_device(): asked = lax.all_to_all(wanted, 'tile', 0, 0, tiled=True)  19.7 us
    all_to_all x1, starting transfers between devices, on_device(): arrived = lax.all_to_all(sorted_in, 'tile', 0, 0, tiled=True)  18.8 us
    all_to_all x1, waiting for transfers between devices, on_device(): arrived = lax.all_to_all(sorted_in, 'tile', 0, 0, tiled=True)  15.2 us
    ppermute x3, starting transfers between devices, with_ghost(): lax.ppermute(lax.slice_in_dim(block, 0, width, axis=dim), axis, backward)  13.1 us
    all_to_all x1, waiting for transfers between devices, on_device(): asked = lax.all_to_all(wanted, 'tile', 0, 0, tiled=True)  13.1 us
    pallas_call x1, Pallas kernels, river_terms(): pl.pallas_call(scatter_kernel, grid=(count // chunk,), in_specs=[lane, la...  12.9 us
    all_gather x1, blocking collectives, on_device(): edges = lax.all_gather(edges, 'layer', axis=1, tiled=True)  12.1 us
  transfers between devices with their start and end apart: 10, of which 4 were waited for; matrix products, arithmetic and copies ran while one was open for 5% of the time, Pallas kernels for 7%

profile of v10, /device:TPU:1, one launch (start us, length us, event | category | flops | bytes accessed | tf_op | source)
XLA Modules:
  0.0 183.6 jit_solution(13459363765736453631)
XLA Ops:
  7.3 1.0 convert_bitcast_fusion
  8.3 0.8 fusion.4
  9.1 8.8 %collective-permute-start.1 = (f32[2,2,8,512]{3,2,1,0:T(8,128)S(1)}, f32[2,2,8,512]{3,2,1,0:T(8,128)S(1)}, u32[]{:S(2)}, u32[]{:S(2)}) collective-permute-start(f32[2,2,8,512]{3,2,1,0:T(8,128)S(1)} %get-tuple-element.13), channel_id=1, source_target_pairs={{4,0},{8,4},{12,8},{16,12},{20,16},{24,20},{28,24},{32,28},{36,32}... | collective-permute-start | bytes 196616 | tf_op jit(solution)/shard_map/ppermute | solution.py:274
  17.9 2.1 %collective-permute-start = (f32[2,2,8,512]{3,2,1,0:T(8,128)S(1)}, f32[2,2,8,512]{3,2,1,0:T(8,128)S(1)}, u32[]{:S(2)}, u32[]{:S(2)}) collective-permute-start(f32[2,2,8,512]{3,2,1,0:T(8,128)S(1)} %get-tuple-element.12), channel_id=1, source_target_pairs={{0,4},{4,8},{8,12},{12,16},{16,20},{20,24},{24,28},{28,32},{32,36}... | collective-permute-start | bytes 196616 | tf_op jit(solution)/shard_map/ppermute | solution.py:273
  20.0 1.8 pad_maximum_fusion.1
  21.9 2.4 %collective-permute-start.3 = (f32[8,512]{1,0:T(8,128)S(1)}, f32[8,512]{1,0:T(8,128)S(1)}, u32[]{:S(2)}, u32[]{:S(2)}) collective-permute-start(f32[8,512]{1,0:T(8,128)S(1)} %get-tuple-element.19), channel_id=1, source_target_pairs={{4,0},{8,4},{12,8},{16,12},{20,16},{24,20},{28,24},{32,28},{36,32}... | collective-permute-start | bytes 49160 | tf_op jit(solution)/shard_map/ppermute | solution.py:274
  24.3 3.2 %collective-permute-start.2 = (f32[8,512]{1,0:T(8,128)S(1)}, f32[8,512]{1,0:T(8,128)S(1)}, u32[]{:S(2)}, u32[]{:S(2)}) collective-permute-start(f32[8,512]{1,0:T(8,128)S(1)} %get-tuple-element.18), channel_id=1, source_target_pairs={{0,4},{4,8},{8,12},{12,16},{16,20},{20,24},{24,28},{28,32},{32,36}... | collective-permute-start | bytes 49160 | tf_op jit(solution)/shard_map/ppermute | solution.py:273
  27.8 0.8 all_to_all.20
  28.6 19.7 %all-to-all-start = ((s32[128,2,1]{1,2,0:T(1,128)}), s32[128,2,1]{1,2,0:T(1,128)S(1)}, u32[]{:S(2)}, u32[]{:S(2)}) async-start(s32[128,2,1]{1,2,0:T(1,128)} %bitcast.11), calls=%async_computation | async-start | bytes 131072 | tf_op jit(solution)/shard_map/all_to_all | solution.py:320
  48.4 1.0 fusion.1
  50.1 13.1 %all-to-all-done = s32[128,2,1]{1,2,0:T(1,128)S(1)} async-done(((s32[128,2,1]{1,2,0:T(1,128)}), s32[128,2,1]{1,2,0:T(1,128)S(1)}, u32[]{:S(2)}, u32[]{:S(2)}) %all-to-all-start) | async-done | bytes 1056 | tf_op jit(solution)/shard_map/all_to_all | solution.py:320
  63.7 0.8 reduce.8
  64.7 0.7 gather_fusion
  65.4 0.9 broadcast_select_fusion.1
  66.3 5.7 %all-to-all-start.1 = ((f32[128,2,128]{2,1,0:T(2,128)}), f32[128,2,128]{2,1,0:T(2,128)S(1)}, u32[]{:S(2)}, u32[]{:S(2)}) async-start(f32[128,2,128]{2,1,0:T(2,128)} %broadcast_select_fusion.1), calls=%async_computation.1 | async-start | bytes 262144 | tf_op jit(solution)/shard_map/all_to_all | solution.py:322
  72.3 12.1 %all_gather.6 = f32[2,8,16,512]{3,2,1,0:T(8,128)S(1)} all-gather(f32[2,2,16,512]{3,2,1,0:T(8,128)S(1)} %pad_maximum_fusion.4), channel_id=1, replica_groups=mesh['tile'=128,'layer'=4] {'layer'}, dimensions={1}, use_global_device_ids=true | all-gather | bytes 655360 | tf_op jit(solution)/shard_map/all_gather | solution.py:304
  84.3 3.7 %all-to-all-done.1 = f32[128,2,128]{2,1,0:T(2,128)S(1)} async-done(((f32[128,2,128]{2,1,0:T(2,128)}), f32[128,2,128]{2,1,0:T(2,128)S(1)}, u32[]{:S(2)}, u32[]{:S(2)}) %all-to-all-start.1) | async-done | bytes 131104 | tf_op jit(solution)/shard_map/all_to_all | solution.py:322
  88.1 0.7 gather_fusion.1
  89.2 12.9 %shard_map.122 = (f32[64,512]{1,0:T(8,128)S(1)}, f32[64,512]{1,0:T(8,128)S(1)}) custom-call(s32[1,32768]{1,0:T(1,128)S(1)} %get-tuple-element.17.rows_ref, s32[1,32768]{1,0:T(1,128)S(1)} %get-tuple-element.16.cols_ref, f32[1,32768]{1,0:T(1,128)S(1)} %get-tuple-element.9.diag_in_ref, f32[1,32768]{1,0:T(1,128)S(1)} %get-tuple-element.8.rhs_in_ref), custom_call_target="tpu_custom_call" | custom-call | flops 12884901888 | bytes 786432 | tf_op jit(solution)/shard_map/pallas_call | solution.py:110
  102.2 1.9 %collective-permute-start.5 = (f32[2,8,512]{2,1,0:T(8,128)S(1)}, f32[2,8,512]{2,1,0:T(8,128)S(1)}, u32[]{:S(2)}, u32[]{:S(2)}) collective-permute-start(f32[2,8,512]{2,1,0:T(8,128)S(1)} %get-tuple-element.15), channel_id=1, source_target_pairs={{4,0},{8,4},{12,8},{16,12},{20,16},{24,20},{28,24},{32,28},{36,32}... | collective-permute-start | bytes 98312 | tf_op jit(solution)/shard_map/ppermute | solution.py:274
  104.1 3.8 %collective-permute-start.4 = (f32[2,8,512]{2,1,0:T(8,128)S(1)}, f32[2,8,512]{2,1,0:T(8,128)S(1)}, u32[]{:S(2)}, u32[]{:S(2)}) collective-permute-start(f32[2,8,512]{2,1,0:T(8,128)S(1)} %get-tuple-element.14), channel_id=1, source_target_pairs={{0,4},{4,8},{8,12},{12,16},{16,20},{20,24},{24,28},{28,32},{32,36}... | collective-permute-start | bytes 98312 | tf_op jit(solution)/shard_map/ppermute | solution.py:273
  108.0 0.8 collective-permute-done.4
  108.8 1.9 %pad_maximum_fusion.fields_ref = f32[2,8,80,512]{3,2,1,0:T(8,128)S(1)} fusion(f32[2,8,8,512]{3,2,1,0:T(8,128)S(1)} %get-tuple-element.11, f32[2,8,64,512]{3,2,1,0:T(8,128)} %all-gather.2.cloned.1.call-done, f32[2,8,8,512]{3,2,1,0:T(8,128)S(1)} %get-tuple-element.10), kind=kLoop, calls=%fused_computation.3 | loop fusion | flops 1310720 | bytes 5242880 | tf_op jit(solution)/shard_map/concatenate | solution.py:305
  110.7 24.7 %shard_map.123 = f32[8,80,512]{2,1,0:T(8,128)S(1)} custom-call(f32[3,12]{1,0:T(4,128)S(1)} %pad_maximum_fusion.7.tables_ref, f32[2,8,80,512]{3,2,1,0:T(8,128)S(1)} %pad_maximum_fusion.fields_ref, f32[80,512]{1,0:T(8,128)S(1)} %pad_maximum_fusion.3.land_ref, f32[2,80,512]{2,1,0:T(8,128)S(1)} %pad_maximum_fusion.2.river_ref), custom_call_target="tpu_custom_call" | custom-call | flops 131072000 | bytes 3932160 | tf_op jit(solution)/shard_map/pallas_call | solution.py:256
  135.4 2.5 %shard_map.124 = f32[1,8192]{1,0:T(1,128)S(1)} custom-call(f32[64,512]{1,0:T(8,128)S(1)} %slice_bitcast_fusion.top_ref, s32[1,8192]{1,0:T(1,128)S(1)} %get-tuple-element.21.rows_ref, s32[1,8192]{1,0:T(1,128)S(1)} %get-tuple-element.20.cols_ref), custom_call_target="tpu_custom_call" | custom-call | flops 1610612736 | bytes 229376 | tf_op jit(solution)/shard_map/pallas_call | solution.py:151
  138.5 0.7 reduce.9
  139.5 0.7 gather_fusion.2
  140.2 0.9 broadcast_select_fusion
  141.0 18.8 %all-to-all-start.2 = ((f32[128,2,32]{2,1,0:T(2,128)}), f32[128,2,32]{2,1,0:T(2,128)S(1)}, u32[]{:S(2)}, u32[]{:S(2)}) async-start(f32[128,2,32]{2,1,0:T(2,128)} %broadcast_select_fusion), calls=%async_computation.2 | async-start | bytes 262144 | tf_op jit(solution)/shard_map/all_to_all | solution.py:354
  160.0 0.7 constant_dynamic-slice_fusion.1
  160.7 15.2 %all-to-all-done.2 = f32[128,2,32]{2,1,0:T(2,128)S(1)} async-done(((f32[128,2,32]{2,1,0:T(2,128)}), f32[128,2,32]{2,1,0:T(2,128)S(1)}, u32[]{:S(2)}, u32[]{:S(2)}) %all-to-all-start.2) | async-done | bytes 32800 | tf_op jit(solution)/shard_map/all_to_all | solution.py:354
  176.0 0.8 select_reduce_fusion
  (61 shorter events, 3.4 us)
Async XLA Ops:
  7.2 57.5 %copy-start = (f32[16,128]{1,0:T(8,128)S(1)}, f32[16,128]{1,0:T(8,128)}, u32[]{:S(2)}) copy-start(f32[16,128]{1,0:T(8,128)} %param.17) | copy-start | bytes 24580
  7.2 14.7 %copy-start.3 = (s32[64,512]{1,0:T(8,128)S(1)}, s32[64,512]{1,0:T(8,128)}, u32[]{:S(2)}) copy-start(s32[64,512]{1,0:T(8,128)} %param.13) | copy-start | bytes 393220
  7.2 20.3 %copy-start.4 = (s32[1,256]{1,0:T(1,128)S(1)}, s32[1,256]{1,0:T(1,128)}, u32[]{:S(2)}) copy-start(s32[1,256]{1,0:T(1,128)} %param.18) | copy-start | bytes 3076
  7.2 20.5 %copy-start.5 = (s32[1,256]{1,0:T(1,128)S(1)}, s32[1,256]{1,0:T(1,128)}, u32[]{:S(2)}) copy-start(s32[1,256]{1,0:T(1,128)} %param.19) | copy-start | bytes 3076
  7.2 41.2 %copy-start.1 = (s32[1,256,128]{2,1,0:T(8,128)S(1)}, s32[1,256,128]{2,1,0:T(8,128)}, u32[]{:S(2)}) copy-start(s32[1,256,128]{2,1,0:T(8,128)} %param.20) | copy-start | bytes 393220
  7.2 101.6 %all-gather.2.cloned.1.call-start = ((), (), s32[]{:S(2)}) async-start(), calls=%async_computation.3 | async-start | bytes 2621440 | tf_op jit(solution)/shard_map/all_gather | solution.py:303
  9.1 63.1 %collective-permute-start.1 = (f32[2,2,8,512]{3,2,1,0:T(8,128)S(1)}, f32[2,2,8,512]{3,2,1,0:T(8,128)S(1)}, u32[]{:S(2)}, u32[]{:S(2)}) collective-permute-start(f32[2,2,8,512]{3,2,1,0:T(8,128)S(1)} %get-tuple-element.13), channel_id=1, source_target_pairs={{4,0},{8,4},{12,8},{16,12},{20,16},{24,20},{28,24},{32,28},{36,32}... | collective-permute-start | bytes 196616 | tf_op jit(solution)/shard_map/ppermute | solution.py:274
  17.9 54.1 %copy-start.6 = (f32[12]{0:T(128)S(1)}, f32[12]{0:T(128)}, u32[]{:S(2)}) copy-start(f32[12]{0:T(128)} %param.16) | copy-start | bytes 148
  17.9 54.1 %copy-start.7 = (f32[12]{0:T(128)S(1)}, f32[12]{0:T(128)}, u32[]{:S(2)}) copy-start(f32[12]{0:T(128)} %param.15) | copy-start | bytes 148
  17.9 54.1 %copy-start.8 = (f32[12]{0:T(128)S(1)}, f32[12]{0:T(128)}, u32[]{:S(2)}) copy-start(f32[12]{0:T(128)} %param.14) | copy-start | bytes 148
  17.9 54.3 %collective-permute-start = (f32[2,2,8,512]{3,2,1,0:T(8,128)S(1)}, f32[2,2,8,512]{3,2,1,0:T(8,128)S(1)}, u32[]{:S(2)}, u32[]{:S(2)}) collective-permute-start(f32[2,2,8,512]{3,2,1,0:T(8,128)S(1)} %get-tuple-element.12), channel_id=1, source_target_pairs={{0,4},{4,8},{8,12},{12,16},{16,20},{20,24},{24,28},{28,32},{32,36}... | collective-permute-start | bytes 196616 | tf_op jit(solution)/shard_map/ppermute | solution.py:273
  21.9 50.3 %collective-permute-start.3 = (f32[8,512]{1,0:T(8,128)S(1)}, f32[8,512]{1,0:T(8,128)S(1)}, u32[]{:S(2)}, u32[]{:S(2)}) collective-permute-start(f32[8,512]{1,0:T(8,128)S(1)} %get-tuple-element.19), channel_id=1, source_target_pairs={{4,0},{8,4},{12,8},{16,12},{20,16},{24,20},{28,24},{32,28},{36,32}... | collective-permute-start | bytes 49160 | tf_op jit(solution)/shard_map/ppermute | solution.py:274
  24.3 47.9 %collective-permute-start.2 = (f32[8,512]{1,0:T(8,128)S(1)}, f32[8,512]{1,0:T(8,128)S(1)}, u32[]{:S(2)}, u32[]{:S(2)}) collective-permute-start(f32[8,512]{1,0:T(8,128)S(1)} %get-tuple-element.18), channel_id=1, source_target_pairs={{0,4},{4,8},{8,12},{12,16},{16,20},{20,24},{24,28},{28,32},{32,36}... | collective-permute-start | bytes 49160 | tf_op jit(solution)/shard_map/ppermute | solution.py:273
  28.6 34.6 %all-to-all-start = ((s32[128,2,1]{1,2,0:T(1,128)}), s32[128,2,1]{1,2,0:T(1,128)S(1)}, u32[]{:S(2)}, u32[]{:S(2)}) async-start(s32[128,2,1]{1,2,0:T(1,128)} %bitcast.11), calls=%async_computation | async-start | bytes 131072 | tf_op jit(solution)/shard_map/all_to_all | solution.py:320
  49.7 39.3 %copy-start.2 = (f32[1,256,128]{2,1,0:T(8,128)S(1)}, f32[1,256,128]{2,1,0:T(8,128)}, u32[]{:S(2)}) copy-start(f32[1,256,128]{2,1,0:T(8,128)} %param.21) | copy-start | bytes 393220
  66.3 21.8 %all-to-all-start.1 = ((f32[128,2,128]{2,1,0:T(2,128)}), f32[128,2,128]{2,1,0:T(2,128)S(1)}, u32[]{:S(2)}, u32[]{:S(2)}) async-start(f32[128,2,128]{2,1,0:T(2,128)} %broadcast_select_fusion.1), calls=%async_computation.1 | async-start | bytes 262144 | tf_op jit(solution)/shard_map/all_to_all | solution.py:322
  102.2 5.8 %collective-permute-start.5 = (f32[2,8,512]{2,1,0:T(8,128)S(1)}, f32[2,8,512]{2,1,0:T(8,128)S(1)}, u32[]{:S(2)}, u32[]{:S(2)}) collective-permute-start(f32[2,8,512]{2,1,0:T(8,128)S(1)} %get-tuple-element.15), channel_id=1, source_target_pairs={{4,0},{8,4},{12,8},{16,12},{20,16},{24,20},{28,24},{32,28},{36,32}... | collective-permute-start | bytes 98312 | tf_op jit(solution)/shard_map/ppermute | solution.py:274
  104.1 4.7 %collective-permute-start.4 = (f32[2,8,512]{2,1,0:T(8,128)S(1)}, f32[2,8,512]{2,1,0:T(8,128)S(1)}, u32[]{:S(2)}, u32[]{:S(2)}) collective-permute-start(f32[2,8,512]{2,1,0:T(8,128)S(1)} %get-tuple-element.14), channel_id=1, source_target_pairs={{0,4},{4,8},{8,12},{12,16},{16,20},{20,24},{24,28},{28,32},{32,36}... | collective-permute-start | bytes 98312 | tf_op jit(solution)/shard_map/ppermute | solution.py:273
  141.0 34.9 %all-to-all-start.2 = ((f32[128,2,32]{2,1,0:T(2,128)}), f32[128,2,32]{2,1,0:T(2,128)S(1)}, u32[]{:S(2)}, u32[]{:S(2)}) async-start(f32[128,2,32]{2,1,0:T(2,128)} %broadcast_select_fusion), calls=%async_computation.2 | async-start | bytes 262144 | tf_op jit(solution)/shard_map/all_to_all | solution.py:354
Sparse Core Ops, SparseCore 0:
  22.0 40.0 all-gather.1

commit v11 on v8

--- a/solution.py
+++ b/solution.py
@@ -210,14 +210,19 @@
         def weigh(z, carry):
             c = cond_s[z]
             co = open_s[z]
-            above = jnp.maximum(z - 1, 0)
             below = jnp.minimum(z + 1, layers - 1)
-            far = [jnp.where(z > 0, cond_s[above], 0.0), jnp.where(z < layers - 1, cond_s[below], 0.0)]
-            far_open = [jnp.where(z > 0, open_s[above], 0.0), jnp.where(z < layers - 1, open_s[below], 0.0)]
-            far += shifted(c)
-            far_open += shifted(co)
-            for i, (_, _, factor) in enumerate(NEIGHBOURS):
-                w_s[i, z] = factor * 2.0 * co * far_open[i] / (c + far[i])
+            far = jnp.where(z < layers - 1, cond_s[below], 0.0)
+            far_open = jnp.where(z < layers - 1, open_s[below], 0.0)
+            w_s[1, z] = VERTICAL * 2.0 * co * far_open / (c + far)
+            w_s[0, z] = jnp.where(z > 0, w_s[1, jnp.maximum(z - 1, 0)], 0.0)
+            for axis, first, second in ((0, 0, 1), (1, 2, 3)):
+                _, shift, adjacent = moves[first]
+                face = LATERAL * 2.0 * co * jnp.where(adjacent, pltpu.roll(co, shift, axis), 0.0) / (
+                    c + jnp.where(adjacent, pltpu.roll(c, shift, axis), 0.0)
+                )
+                _, back, back_adjacent = moves[second]
+                w_s[2 * axis + 2, z] = face
+                w_s[2 * axis + 3, z] = jnp.where(back_adjacent, pltpu.roll(face, back, axis), 0.0)
             return carry
 
         lax.fori_loop(0, layers, weigh, 0)

time: 180 us -> 180 us (level)
  starting transfers between devices: 64.4 us -> 59.1 us
  waiting for transfers between devices: 38.9 us -> 42.1 us
  Pallas kernels: 41.8 us -> 44 us
    ppermute x2, starting transfers between devices: 11.2 us -> 5.46 us  [with_ghost(): lax.ppermute(lax.slice_in_dim(block, size - width, size, axis=dim), axis,...]
    all_gather x1, waiting for transfers between devices: 0.47 us -> 4.16 us  [on_device(): fields = lax.all_gather(fields, 'layer', axis=1, tiled=True)]
    pallas_call x1, Pallas kernels: 15.9 us -> 17.9 us  [river_terms(): pl.pallas_call(scatter_kernel, grid=(count // chunk,), in_specs=[lane, la...]
  transfers between devices with their start and end apart: 8 -> 8, of which waited for: 5 -> 5; matrix products, arithmetic and copies ran while one was open for 6% -> 6% of each run, Pallas kernels for 9% -> 10%
where the time goes in v11:
time: 180 us; the launch traced here: 179 us
  starting transfers between devices  59.1 us (33%)
  Pallas kernels  44 us (24%)
  waiting for transfers between devices  42.1 us (23%)
  between operations  14.5 us (8%)
  other arithmetic  11.2 us (6%)
  local copies, waits for them, and re-layouts  8.22 us (5%)
    pallas_call x1, Pallas kernels, stencil(): pl.pallas_call(functools.partial(stencil_kernel, total_rows), in_specs=[p...  23.3 us
    all_to_all x1, starting transfers between devices, on_device(): asked = lax.all_to_all(wanted, 'tile', 0, 0, tiled=True)  20.4 us
    pallas_call x1, Pallas kernels, river_terms(): pl.pallas_call(scatter_kernel, grid=(count // chunk,), in_specs=[lane, la...  17.9 us
    all_to_all x1, starting transfers between devices, on_device(): arrived = lax.all_to_all(sorted_in, 'tile', 0, 0, tiled=True)  16.7 us
    all_to_all x1, waiting for transfers between devices, on_device(): arrived = lax.all_to_all(sorted_in, 'tile', 0, 0, tiled=True)  15.3 us
    all_to_all x1, waiting for transfers between devices, on_device(): sorted_section = lax.all_to_all(reply, 'tile', 0, 0, tiled=True)  14.6 us
    all_to_all x1, starting transfers between devices, on_device(): sorted_section = lax.all_to_all(reply, 'tile', 0, 0, tiled=True)  12.1 us
    ppermute x2, starting transfers between devices, with_ghost(): lax.ppermute(lax.slice_in_dim(block, size - width, size, axis=dim), axis,...  5.46 us
  transfers between devices with their start and end apart: 8, of which 5 were waited for; matrix products, arithmetic and copies ran while one was open for 6% of the time, Pallas kernels for 10%

profile of v11, /device:TPU:1, one launch (start us, length us, event | category | flops | bytes accessed | tf_op | source)
XLA Modules:
  0.0 179.2 jit_solution(10080642961493778915)
XLA Ops:
  7.2 1.0 convert_reduce_fusion
  8.9 0.8 select_reduce_fusion.1
  9.7 0.8 all_to_all.20
  10.5 20.4 %all-to-all-start = ((s32[128,2,1]{1,2,0:T(1,128)}), s32[128,2,1]{1,2,0:T(1,128)S(1)}, u32[]{:S(2)}, u32[]{:S(2)}) async-start(s32[128,2,1]{1,2,0:T(1,128)} %bitcast.12), calls=%async_computation | async-start | bytes 131072 | tf_op jit(solution)/shard_map/all_to_all | solution.py:324
  30.9 1.0 convert_element_type.9
  31.9 0.9 convert_bitcast_fusion
  32.8 0.8 pad_maximum_fusion.4
  33.6 3.5 %collective-permute-start = (f32[5,8,512]{2,1,0:T(8,128)S(1)}, f32[5,8,512]{2,1,0:T(8,128)S(1)}, u32[]{:S(2)}, u32[]{:S(2)}) collective-permute-start(f32[5,8,512]{2,1,0:T(8,128)S(1)} %get-tuple-element.10), channel_id=1, source_target_pairs={{0,4},{4,8},{8,12},{12,16},{16,20},{20,24},{24,28},{28,32},{32,36}... | collective-permute-start | bytes 245768 | tf_op jit(solution)/shard_map/ppermute | solution.py:278
  37.1 1.9 %collective-permute-start.1 = (f32[5,8,512]{2,1,0:T(8,128)S(1)}, f32[5,8,512]{2,1,0:T(8,128)S(1)}, u32[]{:S(2)}, u32[]{:S(2)}) collective-permute-start(f32[5,8,512]{2,1,0:T(8,128)S(1)} %get-tuple-element.11), channel_id=1, source_target_pairs={{4,0},{8,4},{12,8},{16,12},{20,16},{24,20},{28,24},{32,28},{36,32}... | collective-permute-start | bytes 245768 | tf_op jit(solution)/shard_map/ppermute | solution.py:279
  39.1 1.0 fusion.1
  40.7 5.0 %all-to-all-done = s32[128,2,1]{1,2,0:T(1,128)S(1)} async-done(((s32[128,2,1]{1,2,0:T(1,128)}), s32[128,2,1]{1,2,0:T(1,128)S(1)}, u32[]{:S(2)}, u32[]{:S(2)}) %all-to-all-start) | async-done | bytes 1056 | tf_op jit(solution)/shard_map/all_to_all | solution.py:324
  46.2 0.8 reduce.8
  47.2 0.7 gather_fusion
  48.0 0.9 broadcast_select_fusion.1
  48.8 12.1 %all-to-all-start.1 = ((f32[128,2,128]{2,1,0:T(2,128)}), f32[128,2,128]{2,1,0:T(2,128)S(1)}, u32[]{:S(2)}, u32[]{:S(2)}) async-start(f32[128,2,128]{2,1,0:T(2,128)} %broadcast_select_fusion.1), calls=%async_computation.1 | async-start | bytes 262144 | tf_op jit(solution)/shard_map/all_to_all | solution.py:326
  61.4 0.9 slice.38
  62.3 14.6 %all-to-all-done.1 = f32[128,2,128]{2,1,0:T(2,128)S(1)} async-done(((f32[128,2,128]{2,1,0:T(2,128)}), f32[128,2,128]{2,1,0:T(2,128)S(1)}, u32[]{:S(2)}, u32[]{:S(2)}) %all-to-all-start.1) | async-done | bytes 131104 | tf_op jit(solution)/shard_map/all_to_all | solution.py:326
  77.0 0.7 gather_fusion.1
  78.1 17.9 %shard_map.122 = (f32[64,512]{1,0:T(8,128)S(1)}, f32[64,512]{1,0:T(8,128)S(1)}) custom-call(s32[1,32768]{1,0:T(1,128)S(1)} %get-tuple-element.15.rows_ref, s32[1,32768]{1,0:T(1,128)S(1)} %get-tuple-element.14.cols_ref, f32[1,32768]{1,0:T(1,128)S(1)} %get-tuple-element.9.diag_in_ref, f32[1,32768]{1,0:T(1,128)S(1)} %get-tuple-element.8.rhs_in_ref), custom_call_target="tpu_custom_call" | custom-call | flops 12884901888 | bytes 786432 | tf_op jit(solution)/shard_map/pallas_call | solution.py:110
  96.0 1.9 %collective-permute-start.2 = (f32[2,8,512]{2,1,0:T(8,128)S(1)}, f32[2,8,512]{2,1,0:T(8,128)S(1)}, u32[]{:S(2)}, u32[]{:S(2)}) collective-permute-start(f32[2,8,512]{2,1,0:T(8,128)S(1)} %get-tuple-element.12), channel_id=1, source_target_pairs={{0,4},{4,8},{8,12},{12,16},{16,20},{20,24},{24,28},{28,32},{32,36}... | collective-permute-start | bytes 98312 | tf_op jit(solution)/shard_map/ppermute | solution.py:278
  97.9 2.6 %collective-permute-start.3 = (f32[2,8,512]{2,1,0:T(8,128)S(1)}, f32[2,8,512]{2,1,0:T(8,128)S(1)}, u32[]{:S(2)}, u32[]{:S(2)}) collective-permute-start(f32[2,8,512]{2,1,0:T(8,128)S(1)} %get-tuple-element.13), channel_id=1, source_target_pairs={{4,0},{8,4},{12,8},{16,12},{20,16},{24,20},{28,24},{32,28},{36,32}... | collective-permute-start | bytes 98312 | tf_op jit(solution)/shard_map/ppermute | solution.py:279
  100.6 3.0 %collective-permute-done.3 = f32[2,8,512]{2,1,0:T(8,128)S(1)} collective-permute-done((f32[2,8,512]{2,1,0:T(8,128)S(1)}, f32[2,8,512]{2,1,0:T(8,128)S(1)}, u32[]{:S(2)}, u32[]{:S(2)}) %collective-permute-start.3) | collective-permute-done | bytes 32800 | tf_op jit(solution)/shard_map/ppermute | solution.py:279
  103.6 4.2 %all-gather.2.cloned.1.call-done.fields_ref = f32[2,8,80,512]{3,2,1,0:T(8,128)} async-done(((f32[2,2,80,512]{3,2,1,0:T(8,128)}), f32[2,8,80,512]{3,2,1,0:T(8,128)}) %all-gather.2.cloned.1.call-update) | async-done | bytes 2621456 | tf_op jit(solution)/shard_map/all_gather | solution.py:311
  107.8 1.7 copy-done.1
  109.5 23.3 %shard_map.123 = f32[8,80,512]{2,1,0:T(8,128)S(1)} custom-call(f32[3,12]{1,0:T(4,128)S(1)} %pad_maximum_fusion.7.tables_ref, f32[2,8,80,512]{3,2,1,0:T(8,128)S(1)} %copy-done.1, f32[80,512]{1,0:T(8,128)S(1)} %maximum_bitcast_fusion.land_ref, f32[2,80,512]{2,1,0:T(8,128)S(1)} %pad_maximum_fusion.1.river_ref), custom_call_target="tpu_custom_call" | custom-call | flops 131072000 | bytes 3932160 | tf_op jit(solution)/shard_map/pallas_call | solution.py:261
  132.9 2.8 %shard_map.124 = f32[1,8192]{1,0:T(1,128)S(1)} custom-call(f32[64,512]{1,0:T(8,128)S(1)} %slice_bitcast_fusion.top_ref, s32[1,8192]{1,0:T(1,128)S(1)} %get-tuple-element.17.rows_ref, s32[1,8192]{1,0:T(1,128)S(1)} %get-tuple-element.16.cols_ref), custom_call_target="tpu_custom_call" | custom-call | flops 1610612736 | bytes 229376 | tf_op jit(solution)/shard_map/pallas_call | solution.py:151
  137.2 0.7 gather_fusion.2
  137.9 0.9 broadcast_select_fusion
  138.7 16.7 %all-to-all-start.2 = ((f32[128,2,32]{2,1,0:T(2,128)}), f32[128,2,32]{2,1,0:T(2,128)S(1)}, u32[]{:S(2)}, u32[]{:S(2)}) async-start(f32[128,2,32]{2,1,0:T(2,128)} %broadcast_select_fusion), calls=%async_computation.2 | async-start | bytes 262144 | tf_op jit(solution)/shard_map/all_to_all | solution.py:358
  155.5 0.7 constant_dynamic-slice_fusion.1
  156.2 15.3 %all-to-all-done.2 = f32[128,2,32]{2,1,0:T(2,128)S(1)} async-done(((f32[128,2,32]{2,1,0:T(2,128)}), f32[128,2,32]{2,1,0:T(2,128)S(1)}, u32[]{:S(2)}, u32[]{:S(2)}) %all-to-all-start.2) | async-done | bytes 32800 | tf_op jit(solution)/shard_map/all_to_all | solution.py:358
  171.6 0.8 select_reduce_fusion
  (53 shorter events, 4.4 us)
Async XLA Ops:
  7.2 40.1 %copy-start = (f32[16,128]{1,0:T(8,128)S(1)}, f32[16,128]{1,0:T(8,128)}, u32[]{:S(2)}) copy-start(f32[16,128]{1,0:T(8,128)} %param.17) | copy-start | bytes 24580
  7.2 31.9 %copy-start.5 = (s32[1,256]{1,0:T(1,128)S(1)}, s32[1,256]{1,0:T(1,128)}, u32[]{:S(2)}) copy-start(s32[1,256]{1,0:T(1,128)} %param.18) | copy-start | bytes 3076
  7.2 31.9 %copy-start.3 = (s32[1,256,128]{2,1,0:T(8,128)S(1)}, s32[1,256,128]{2,1,0:T(8,128)}, u32[]{:S(2)}) copy-start(s32[1,256,128]{2,1,0:T(8,128)} %param.20) | copy-start | bytes 393220
  10.5 35.2 %all-to-all-start = ((s32[128,2,1]{1,2,0:T(1,128)}), s32[128,2,1]{1,2,0:T(1,128)S(1)}, u32[]{:S(2)}, u32[]{:S(2)}) async-start(s32[128,2,1]{1,2,0:T(1,128)} %bitcast.12), calls=%async_computation | async-start | bytes 131072 | tf_op jit(solution)/shard_map/all_to_all | solution.py:324
  33.6 27.7 %collective-permute-start = (f32[5,8,512]{2,1,0:T(8,128)S(1)}, f32[5,8,512]{2,1,0:T(8,128)S(1)}, u32[]{:S(2)}, u32[]{:S(2)}) collective-permute-start(f32[5,8,512]{2,1,0:T(8,128)S(1)} %get-tuple-element.10), channel_id=1, source_target_pairs={{0,4},{4,8},{8,12},{12,16},{16,20},{20,24},{24,28},{28,32},{32,36}... | collective-permute-start | bytes 245768 | tf_op jit(solution)/shard_map/ppermute | solution.py:278
  37.1 24.2 %collective-permute-start.1 = (f32[5,8,512]{2,1,0:T(8,128)S(1)}, f32[5,8,512]{2,1,0:T(8,128)S(1)}, u32[]{:S(2)}, u32[]{:S(2)}) collective-permute-start(f32[5,8,512]{2,1,0:T(8,128)S(1)} %get-tuple-element.11), channel_id=1, source_target_pairs={{4,0},{8,4},{12,8},{16,12},{20,16},{24,20},{28,24},{32,28},{36,32}... | collective-permute-start | bytes 245768 | tf_op jit(solution)/shard_map/ppermute | solution.py:279
  40.1 21.0 %copy-start.6 = (f32[12]{0:T(128)S(1)}, f32[12]{0:T(128)}, u32[]{:S(2)}) copy-start(f32[12]{0:T(128)} %param.16) | copy-start | bytes 148
  40.1 21.0 %copy-start.7 = (f32[12]{0:T(128)S(1)}, f32[12]{0:T(128)}, u32[]{:S(2)}) copy-start(f32[12]{0:T(128)} %param.15) | copy-start | bytes 148
  40.1 21.0 %copy-start.8 = (f32[12]{0:T(128)S(1)}, f32[12]{0:T(128)}, u32[]{:S(2)}) copy-start(f32[12]{0:T(128)} %param.14) | copy-start | bytes 148
  40.2 21.1 %copy-start.2 = (f32[2,64,512]{2,1,0:T(8,128)S(1)}, f32[2,64,512]{2,1,0:T(8,128)}, u32[]{:S(2)}) copy-start(f32[2,64,512]{2,1,0:T(8,128)} %param.11) | copy-start | bytes 786436
  48.8 28.1 %all-to-all-start.1 = ((f32[128,2,128]{2,1,0:T(2,128)}), f32[128,2,128]{2,1,0:T(2,128)S(1)}, u32[]{:S(2)}, u32[]{:S(2)}) async-start(f32[128,2,128]{2,1,0:T(2,128)} %broadcast_select_fusion.1), calls=%async_computation.1 | async-start | bytes 262144 | tf_op jit(solution)/shard_map/all_to_all | solution.py:326
  60.9 46.9 %all-gather.2.cloned.1.call-start = ((), (), s32[]{:S(2)}) async-start(), calls=%async_computation.3 | async-start | bytes 3276800 | tf_op jit(solution)/shard_map/all_gather | solution.py:311
  62.3 15.5 %copy-start.4 = (f32[1,256,128]{2,1,0:T(8,128)S(1)}, f32[1,256,128]{2,1,0:T(8,128)}, u32[]{:S(2)}) copy-start(f32[1,256,128]{2,1,0:T(8,128)} %param.21) | copy-start | bytes 393220
  96.0 4.5 %collective-permute-start.2 = (f32[2,8,512]{2,1,0:T(8,128)S(1)}, f32[2,8,512]{2,1,0:T(8,128)S(1)}, u32[]{:S(2)}, u32[]{:S(2)}) collective-permute-start(f32[2,8,512]{2,1,0:T(8,128)S(1)} %get-tuple-element.12), channel_id=1, source_target_pairs={{0,4},{4,8},{8,12},{12,16},{16,20},{20,24},{24,28},{28,32},{32,36}... | collective-permute-start | bytes 98312 | tf_op jit(solution)/shard_map/ppermute | solution.py:278
  97.9 5.6 %collective-permute-start.3 = (f32[2,8,512]{2,1,0:T(8,128)S(1)}, f32[2,8,512]{2,1,0:T(8,128)S(1)}, u32[]{:S(2)}, u32[]{:S(2)}) collective-permute-start(f32[2,8,512]{2,1,0:T(8,128)S(1)} %get-tuple-element.13), channel_id=1, source_target_pairs={{4,0},{8,4},{12,8},{16,12},{20,16},{24,20},{28,24},{32,28},{36,32}... | collective-permute-start | bytes 98312 | tf_op jit(solution)/shard_map/ppermute | solution.py:279
  107.8 1.7 copy-start.1
  138.7 32.7 %all-to-all-start.2 = ((f32[128,2,32]{2,1,0:T(2,128)}), f32[128,2,32]{2,1,0:T(2,128)S(1)}, u32[]{:S(2)}, u32[]{:S(2)}) async-start(f32[128,2,32]{2,1,0:T(2,128)} %broadcast_select_fusion), calls=%async_computation.2 | async-start | bytes 262144 | tf_op jit(solution)/shard_map/all_to_all | solution.py:358
Sparse Core Ops, SparseCore 0:
  63.8 43.8 all-gather.1

commit v12 on v11

--- a/solution.py
+++ b/solution.py
@@ -307,8 +307,9 @@
     )
     planes = with_ghost(planes, "tile", 1, GHOST)
     extent = across + 2 * GHOST
-    fields = planes[: 2 * own_layers].reshape(2, own_layers, extent, breadth)
-    fields = lax.all_gather(fields, "layer", axis=1, tiled=True)
+    raw = jnp.stack([head_start, soil_class.astype(jnp.float32)])
+    edges = planes[: 2 * own_layers].reshape(2, own_layers, extent, breadth)
+    edges = jnp.concatenate([edges[:, :, :GHOST], edges[:, :, GHOST + across :]], axis=2)
     owners = cross_owner[0]
     positions = cross_local[0]
     node_cells = node_cell[0]
@@ -322,6 +323,10 @@
     at_place = place[None, :] == order[:, None]
     wanted = jnp.sum(jnp.where(at_place, positions[None, :], 0), axis=1)
     asked = lax.all_to_all(wanted, "tile", 0, 0, tiled=True)
+    asked, raw = lax.optimization_barrier((asked, raw))
+    raw = lax.all_gather(raw, "layer", axis=1, tiled=True)
+    edges = lax.all_gather(edges, "layer", axis=1, tiled=True)
+    fields = jnp.concatenate([edges[:, :, :GHOST], raw, edges[:, :, GHOST:]], axis=2)
     reply = jnp.take(section, asked, axis=0)
     sorted_section = lax.all_to_all(reply, "tile", 0, 0, tiled=True)
     slot_section = jnp.take(sorted_section, place, axis=0)

time: 180 us -> 181 us (level)
  waiting for transfers between devices: 42.1 us -> 27.5 us
  blocking collectives: 0 us -> 14.3 us
  other arithmetic: 11.2 us -> 16.3 us
  local copies, waits for them, and re-layouts: 8.22 us -> 5.72 us
    all_gather x0 -> x1, blocking collectives: none -> 14.3 us  [on_device(): edges = lax.all_gather(edges, 'layer', axis=1, tiled=True)]
    all_to_all x1, waiting for transfers between devices: 14.6 us -> 1.45 us  [on_device(): sorted_section = lax.all_to_all(reply, 'tile', 0, 0, tiled=True)]
    ppermute x2, starting transfers between devices: 4.5 us -> 13.4 us  [with_ghost(): lax.ppermute(lax.slice_in_dim(block, 0, width, axis=dim), axis, backward)]
    all_to_all x1, starting transfers between devices: 12.1 us -> 6.2 us  [on_device(): sorted_section = lax.all_to_all(reply, 'tile', 0, 0, tiled=True)]
    all_to_all x1, waiting for transfers between devices: 5.05 us -> 9.91 us  [on_device(): asked = lax.all_to_all(wanted, 'tile', 0, 0, tiled=True)]
    all_gather x1, waiting for transfers between devices: 4.16 us -> 0.02 us  [on_device(): raw = lax.all_gather(raw, 'layer', axis=1, tiled=True)]
    all_to_all x1, starting transfers between devices: 20.4 us -> 16.5 us  [on_device(): asked = lax.all_to_all(wanted, 'tile', 0, 0, tiled=True)]
    all_to_all x1, starting transfers between devices: 16.7 us -> 19.8 us  [on_device(): arrived = lax.all_to_all(sorted_in, 'tile', 0, 0, tiled=True)]
  transfers between devices with their start and end apart: 8 -> 8, of which waited for: 5 -> 4; matrix products, arithmetic and copies ran while one was open for 6% -> 7% of each run, Pallas kernels for 10% -> 8%
where the time goes in v12:
time: 181 us
  starting transfers between devices  60.1 us (33%)
  Pallas kernels  42.4 us (23%)
  waiting for transfers between devices  27.5 us (15%)
  other arithmetic  16.3 us (9%)
  between operations  14.5 us (8%)
  blocking collectives  14.3 us (8%)
  local copies, waits for them, and re-layouts  5.72 us (3%)
    pallas_call x1, Pallas kernels, stencil(): pl.pallas_call(functools.partial(stencil_kernel, total_rows), in_specs=[p...  24.8 us
    all_to_all x1, starting transfers between devices, on_device(): arrived = lax.all_to_all(sorted_in, 'tile', 0, 0, tiled=True)  19.8 us
    all_to_all x1, starting transfers between devices, on_device(): asked = lax.all_to_all(wanted, 'tile', 0, 0, tiled=True)  16.5 us
    all_to_all x1, waiting for transfers between devices, on_device(): arrived = lax.all_to_all(sorted_in, 'tile', 0, 0, tiled=True)  15.2 us
    pallas_call x1, Pallas kernels, river_terms(): pl.pallas_call(scatter_kernel, grid=(count // chunk,), in_specs=[lane, la...  14.9 us
    all_gather x1, blocking collectives, on_device(): edges = lax.all_gather(edges, 'layer', axis=1, tiled=True)  14.3 us
    ppermute x2, starting transfers between devices, with_ghost(): lax.ppermute(lax.slice_in_dim(block, 0, width, axis=dim), axis, backward)  13.4 us
    all_to_all x1, waiting for transfers between devices, on_device(): asked = lax.all_to_all(wanted, 'tile', 0, 0, tiled=True)  9.91 us
  transfers between devices with their start and end apart: 8, of which 4 were waited for; matrix products, arithmetic and copies ran while one was open for 7% of the time, Pallas kernels for 8%

profile of v12, /device:TPU:1, one launch (start us, length us, event | category | flops | bytes accessed | tf_op | source)
XLA Modules:
  0.0 180.8 jit_solution(5493995638719906960)
XLA Ops:
  7.2 1.0 convert_bitcast_fusion
  8.2 1.0 convert_bitcast_fusion.1
  9.2 0.8 pad_maximum_fusion.7
  10.0 8.8 %collective-permute-start.1 = (f32[5,8,512]{2,1,0:T(8,128)S(1)}, f32[5,8,512]{2,1,0:T(8,128)S(1)}, u32[]{:S(2)}, u32[]{:S(2)}) collective-permute-start(f32[5,8,512]{2,1,0:T(8,128)S(1)} %get-tuple-element.17), channel_id=1, source_target_pairs={{4,0},{8,4},{12,8},{16,12},{20,16},{24,20},{28,24},{32,28},{36,32}... | collective-permute-start | bytes 245768 | tf_op jit(solution)/shard_map/ppermute | solution.py:279
  18.8 1.9 %collective-permute-start = (f32[5,8,512]{2,1,0:T(8,128)S(1)}, f32[5,8,512]{2,1,0:T(8,128)S(1)}, u32[]{:S(2)}, u32[]{:S(2)}) collective-permute-start(f32[5,8,512]{2,1,0:T(8,128)S(1)} %get-tuple-element.16), channel_id=1, source_target_pairs={{0,4},{4,8},{8,12},{12,16},{16,20},{20,24},{24,28},{28,32},{32,36}... | collective-permute-start | bytes 245768 | tf_op jit(solution)/shard_map/ppermute | solution.py:278
  20.8 0.9 convert_reduce_fusion
  22.4 0.8 select_reduce_fusion.1
  23.2 0.8 all_to_all.18
  24.0 16.5 %all-to-all-start = ((s32[128,2,1]{1,2,0:T(1,128)}), s32[128,2,1]{1,2,0:T(1,128)S(1)}, u32[]{:S(2)}, u32[]{:S(2)}) async-start(s32[128,2,1]{1,2,0:T(1,128)} %bitcast.9), calls=%async_computation | async-start | bytes 131072 | tf_op jit(solution)/shard_map/all_to_all | solution.py:325
  41.3 1.9 %fusion.1 = (s32[1,32768]{1,0:T(1,128)S(1)}, s32[1,32768]{1,0:T(1,128)S(1)}) fusion(s32[1,32768]{1,0:T(1,128)} %bitcast.48), kind=kLoop, calls=%fused_computation.21 | loop fusion | flops 720896 | bytes 393216 | tf_op jit(solution)/shard_map/jit(_where)/select_n | solution.py:337
  44.6 0.8 pad_maximum_fusion.2
  45.4 9.9 %all-to-all-done = s32[128,2,1]{1,2,0:T(1,128)S(1)} async-done(((s32[128,2,1]{1,2,0:T(1,128)}), s32[128,2,1]{1,2,0:T(1,128)S(1)}, u32[]{:S(2)}, u32[]{:S(2)}) %all-to-all-start) | async-done | bytes 1056 | tf_op jit(solution)/shard_map/all_to_all | solution.py:325
  55.9 0.8 reduce.6
  57.0 0.7 gather_fusion
  57.8 0.9 broadcast_select_fusion.1
  58.6 6.2 %all-to-all-start.1 = ((f32[128,2,128]{2,1,0:T(2,128)}), f32[128,2,128]{2,1,0:T(2,128)S(1)}, u32[]{:S(2)}, u32[]{:S(2)}) async-start(f32[128,2,128]{2,1,0:T(2,128)} %broadcast_select_fusion.1), calls=%async_computation.1 | async-start | bytes 262144 | tf_op jit(solution)/shard_map/all_to_all | solution.py:331
  65.0 14.3 %all_gather.6 = f32[2,8,16,512]{3,2,1,0:T(8,128)S(1)} all-gather(f32[2,2,16,512]{3,2,1,0:T(8,128)S(1)} %pad_maximum_fusion.4), channel_id=1, replica_groups=mesh['tile'=128,'layer'=4] {'layer'}, dimensions={1}, use_global_device_ids=true | all-gather | bytes 655360 | tf_op jit(solution)/shard_map/all_gather | solution.py:328
  79.4 1.5 all-to-all-done.1
  80.8 0.7 gather_fusion.1
  82.0 14.9 %shard_map.122 = (f32[64,512]{1,0:T(8,128)S(1)}, f32[64,512]{1,0:T(8,128)S(1)}) custom-call(s32[1,32768]{1,0:T(1,128)S(1)} %get-tuple-element.25.rows_ref, s32[1,32768]{1,0:T(1,128)S(1)} %get-tuple-element.24.cols_ref, f32[1,32768]{1,0:T(1,128)S(1)} %get-tuple-element.13.diag_in_ref, f32[1,32768]{1,0:T(1,128)S(1)} %get-tuple-element.12.rhs_in_ref), custom_call_target="tpu_custom_call" | custom-call | flops 12884901888 | bytes 786432 | tf_op jit(solution)/shard_map/pallas_call | solution.py:110
  96.9 4.6 %collective-permute-start.3 = (f32[2,8,512]{2,1,0:T(8,128)S(1)}, f32[2,8,512]{2,1,0:T(8,128)S(1)}, u32[]{:S(2)}, u32[]{:S(2)}) collective-permute-start(f32[2,8,512]{2,1,0:T(8,128)S(1)} %get-tuple-element.21), channel_id=1, source_target_pairs={{4,0},{8,4},{12,8},{16,12},{20,16},{24,20},{28,24},{32,28},{36,32}... | collective-permute-start | bytes 98312 | tf_op jit(solution)/shard_map/ppermute | solution.py:279
  101.5 2.2 %collective-permute-start.2 = (f32[2,8,512]{2,1,0:T(8,128)S(1)}, f32[2,8,512]{2,1,0:T(8,128)S(1)}, u32[]{:S(2)}, u32[]{:S(2)}) collective-permute-start(f32[2,8,512]{2,1,0:T(8,128)S(1)} %get-tuple-element.20), channel_id=1, source_target_pairs={{0,4},{4,8},{8,12},{12,16},{16,20},{20,24},{24,28},{28,32},{32,36}... | collective-permute-start | bytes 98312 | tf_op jit(solution)/shard_map/ppermute | solution.py:278
  103.7 0.9 collective-permute-done.2
  104.6 1.9 %pad_maximum_fusion.fields_ref = f32[2,8,80,512]{3,2,1,0:T(8,128)S(1)} fusion(f32[2,8,8,512]{3,2,1,0:T(8,128)S(1)} %get-tuple-element.19, f32[2,8,64,512]{3,2,1,0:T(8,128)} %all-gather.2.cloned.1.call-done, f32[2,8,8,512]{3,2,1,0:T(8,128)S(1)} %get-tuple-element.18), kind=kLoop, calls=%fused_computation.3 | loop fusion | flops 1310720 | bytes 5242880 | tf_op jit(solution)/shard_map/concatenate | solution.py:329
  106.6 24.8 %shard_map.123 = f32[8,80,512]{2,1,0:T(8,128)S(1)} custom-call(f32[3,12]{1,0:T(4,128)S(1)} %pad_maximum_fusion.10.tables_ref, f32[2,8,80,512]{3,2,1,0:T(8,128)S(1)} %pad_maximum_fusion.fields_ref, f32[80,512]{1,0:T(8,128)S(1)} %maximum_bitcast_fusion.land_ref, f32[2,80,512]{2,1,0:T(8,128)S(1)} %pad_maximum_fusion.3.river_ref), custom_call_target="tpu_custom_call" | custom-call | flops 131072000 | bytes 3932160 | tf_op jit(solution)/shard_map/pallas_call | solution.py:261
  131.4 2.8 %shard_map.124 = f32[1,8192]{1,0:T(1,128)S(1)} custom-call(f32[64,512]{1,0:T(8,128)S(1)} %slice_bitcast_fusion.top_ref, s32[1,8192]{1,0:T(1,128)S(1)} %get-tuple-element.27.rows_ref, s32[1,8192]{1,0:T(1,128)S(1)} %get-tuple-element.26.cols_ref), custom_call_target="tpu_custom_call" | custom-call | flops 1610612736 | bytes 229376 | tf_op jit(solution)/shard_map/pallas_call | solution.py:151
  135.7 0.7 gather_fusion.2
  136.4 0.9 broadcast_select_fusion
  137.3 19.8 %all-to-all-start.2 = ((f32[128,2,32]{2,1,0:T(2,128)}), f32[128,2,32]{2,1,0:T(2,128)S(1)}, u32[]{:S(2)}, u32[]{:S(2)}) async-start(f32[128,2,32]{2,1,0:T(2,128)} %broadcast_select_fusion), calls=%async_computation.2 | async-start | bytes 262144 | tf_op jit(solution)/shard_map/all_to_all | solution.py:363
  157.2 0.7 constant_dynamic-slice_fusion.1
  157.9 15.2 %all-to-all-done.2 = f32[128,2,32]{2,1,0:T(2,128)S(1)} async-done(((f32[128,2,32]{2,1,0:T(2,128)}), f32[128,2,32]{2,1,0:T(2,128)S(1)}, u32[]{:S(2)}, u32[]{:S(2)}) %all-to-all-start.2) | async-done | bytes 32800 | tf_op jit(solution)/shard_map/all_to_all | solution.py:363
  173.2 0.8 select_reduce_fusion
  (55 shorter events, 5.9 us)
Async XLA Ops:
  7.2 49.9 %copy-start = (f32[16,128]{1,0:T(8,128)S(1)}, f32[16,128]{1,0:T(8,128)}, u32[]{:S(2)}) copy-start(f32[16,128]{1,0:T(8,128)} %param.17) | copy-start | bytes 24580
  7.2 37.4 %copy-start.1 = (f32[2,64,512]{2,1,0:T(8,128)S(1)}, f32[2,64,512]{2,1,0:T(8,128)}, u32[]{:S(2)}) copy-start(f32[2,64,512]{2,1,0:T(8,128)} %param.11) | copy-start | bytes 786436
  7.2 36.8 %copy-start.2 = (s32[1,256,128]{2,1,0:T(8,128)S(1)}, s32[1,256,128]{2,1,0:T(8,128)}, u32[]{:S(2)}) copy-start(s32[1,256,128]{2,1,0:T(8,128)} %param.20) | copy-start | bytes 393220
  7.2 38.2 %copy-start.4 = (f32[12]{0:T(128)S(1)}, f32[12]{0:T(128)}, u32[]{:S(2)}) copy-start(f32[12]{0:T(128)} %param.16) | copy-start | bytes 148
  7.2 38.2 %copy-start.5 = (f32[12]{0:T(128)S(1)}, f32[12]{0:T(128)}, u32[]{:S(2)}) copy-start(f32[12]{0:T(128)} %param.15) | copy-start | bytes 148
  7.2 38.2 %copy-start.6 = (f32[12]{0:T(128)S(1)}, f32[12]{0:T(128)}, u32[]{:S(2)}) copy-start(f32[12]{0:T(128)} %param.14) | copy-start | bytes 148
  10.0 54.8 %collective-permute-start.1 = (f32[5,8,512]{2,1,0:T(8,128)S(1)}, f32[5,8,512]{2,1,0:T(8,128)S(1)}, u32[]{:S(2)}, u32[]{:S(2)}) collective-permute-start(f32[5,8,512]{2,1,0:T(8,128)S(1)} %get-tuple-element.17), channel_id=1, source_target_pairs={{4,0},{8,4},{12,8},{16,12},{20,16},{24,20},{28,24},{32,28},{36,32}... | collective-permute-start | bytes 245768 | tf_op jit(solution)/shard_map/ppermute | solution.py:279
  18.8 46.0 %collective-permute-start = (f32[5,8,512]{2,1,0:T(8,128)S(1)}, f32[5,8,512]{2,1,0:T(8,128)S(1)}, u32[]{:S(2)}, u32[]{:S(2)}) collective-permute-start(f32[5,8,512]{2,1,0:T(8,128)S(1)} %get-tuple-element.16), channel_id=1, source_target_pairs={{0,4},{4,8},{8,12},{12,16},{16,20},{20,24},{24,28},{28,32},{32,36}... | collective-permute-start | bytes 245768 | tf_op jit(solution)/shard_map/ppermute | solution.py:278
  24.0 31.4 %all-to-all-start = ((s32[128,2,1]{1,2,0:T(1,128)}), s32[128,2,1]{1,2,0:T(1,128)S(1)}, u32[]{:S(2)}, u32[]{:S(2)}) async-start(s32[128,2,1]{1,2,0:T(1,128)} %bitcast.9), calls=%async_computation | async-start | bytes 131072 | tf_op jit(solution)/shard_map/all_to_all | solution.py:325
  40.5 64.1 %all-gather.2.cloned.1.call-start = ((), (), s32[]{:S(2)}) async-start(), calls=%async_computation.3 | async-start | bytes 2621440 | tf_op jit(solution)/shard_map/all_gather | solution.py:327
  58.6 22.2 %all-to-all-start.1 = ((f32[128,2,128]{2,1,0:T(2,128)}), f32[128,2,128]{2,1,0:T(2,128)S(1)}, u32[]{:S(2)}, u32[]{:S(2)}) async-start(f32[128,2,128]{2,1,0:T(2,128)} %broadcast_select_fusion.1), calls=%async_computation.1 | async-start | bytes 262144 | tf_op jit(solution)/shard_map/all_to_all | solution.py:331
  64.9 16.7 %copy-start.3 = (f32[1,256,128]{2,1,0:T(8,128)S(1)}, f32[1,256,128]{2,1,0:T(8,128)}, u32[]{:S(2)}) copy-start(f32[1,256,128]{2,1,0:T(8,128)} %param.21) | copy-start | bytes 393220
  96.9 6.8 %collective-permute-start.3 = (f32[2,8,512]{2,1,0:T(8,128)S(1)}, f32[2,8,512]{2,1,0:T(8,128)S(1)}, u32[]{:S(2)}, u32[]{:S(2)}) collective-permute-start(f32[2,8,512]{2,1,0:T(8,128)S(1)} %get-tuple-element.21), channel_id=1, source_target_pairs={{4,0},{8,4},{12,8},{16,12},{20,16},{24,20},{28,24},{32,28},{36,32}... | collective-permute-start | bytes 98312 | tf_op jit(solution)/shard_map/ppermute | solution.py:279
  101.5 3.1 %collective-permute-start.2 = (f32[2,8,512]{2,1,0:T(8,128)S(1)}, f32[2,8,512]{2,1,0:T(8,128)S(1)}, u32[]{:S(2)}, u32[]{:S(2)}) collective-permute-start(f32[2,8,512]{2,1,0:T(8,128)S(1)} %get-tuple-element.20), channel_id=1, source_target_pairs={{0,4},{4,8},{8,12},{12,16},{16,20},{20,24},{24,28},{28,32},{32,36}... | collective-permute-start | bytes 98312 | tf_op jit(solution)/shard_map/ppermute | solution.py:278
  137.3 35.8 %all-to-all-start.2 = ((f32[128,2,32]{2,1,0:T(2,128)}), f32[128,2,32]{2,1,0:T(2,128)S(1)}, u32[]{:S(2)}, u32[]{:S(2)}) async-start(f32[128,2,32]{2,1,0:T(2,128)} %broadcast_select_fusion), calls=%async_computation.2 | async-start | bytes 262144 | tf_op jit(solution)/shard_map/all_to_all | solution.py:363
Sparse Core Ops, SparseCore 0:
  57.0 33.8 all-gather.1

commit v13 on v12

--- a/solution.py
+++ b/solution.py
@@ -23,7 +23,7 @@
     (2, -1, LATERAL),
     (2, 1, LATERAL),
 )
-CHUNK = 2048
+CHUNK = 4096
 
 
 def beside(padded, axis_id, step):

time: 181 us -> 178 us (0.983)
  starting transfers between devices: 60.1 us -> 57.1 us
    ppermute x2, starting transfers between devices: 13.4 us -> 10.7 us  [with_ghost(): lax.ppermute(lax.slice_in_dim(block, 0, width, axis=dim), axis, backward)]
    all_to_all x1, starting transfers between devices: 19.8 us -> 17.9 us  [on_device(): arrived = lax.all_to_all(sorted_in, 'tile', 0, 0, tiled=True)]
where the time goes in v13:
time: 178 us; the launch traced here: 177 us
  starting transfers between devices  57.1 us (32%)
  Pallas kernels  42 us (24%)
  waiting for transfers between devices  27.4 us (15%)
  other arithmetic  16.3 us (9%)
  between operations  14.5 us (8%)
  blocking collectives  14.3 us (8%)
  local copies, waits for them, and re-layouts  5.72 us (3%)
    pallas_call x1, Pallas kernels, stencil(): pl.pallas_call(functools.partial(stencil_kernel, total_rows), in_specs=[p...  24.8 us
    all_to_all x1, starting transfers between devices, on_device(): arrived = lax.all_to_all(sorted_in, 'tile', 0, 0, tiled=True)  17.9 us
    all_to_all x1, starting transfers between devices, on_device(): asked = lax.all_to_all(wanted, 'tile', 0, 0, tiled=True)  16.5 us
    all_to_all x1, waiting for transfers between devices, on_device(): arrived = lax.all_to_all(sorted_in, 'tile', 0, 0, tiled=True)  15.2 us
    pallas_call x1, Pallas kernels, river_terms(): pl.pallas_call(scatter_kernel, grid=(count // chunk,), in_specs=[lane, la...  14.7 us
    all_gather x1, blocking collectives, on_device(): edges = lax.all_gather(edges, 'layer', axis=1, tiled=True)  14.3 us
    ppermute x2, starting transfers between devices, with_ghost(): lax.ppermute(lax.slice_in_dim(block, 0, width, axis=dim), axis, backward)  10.7 us
    all_to_all x1, waiting for transfers between devices, on_device(): asked = lax.all_to_all(wanted, 'tile', 0, 0, tiled=True)  9.91 us
  transfers between devices with their start and end apart: 8, of which 4 were waited for; matrix products, arithmetic and copies ran while one was open for 7% of the time, Pallas kernels for 8%

profile of v13, /device:TPU:1, one launch (start us, length us, event | category | flops | bytes accessed | tf_op | source)
XLA Modules:
  0.0 177.3 jit_solution(3663629374102528708)
XLA Ops:
  7.2 1.0 convert_bitcast_fusion
  8.2 1.0 convert_bitcast_fusion.1
  9.2 0.8 pad_maximum_fusion.7
  10.0 8.8 %collective-permute-start.1 = (f32[5,8,512]{2,1,0:T(8,128)S(1)}, f32[5,8,512]{2,1,0:T(8,128)S(1)}, u32[]{:S(2)}, u32[]{:S(2)}) collective-permute-start(f32[5,8,512]{2,1,0:T(8,128)S(1)} %get-tuple-element.17), channel_id=1, source_target_pairs={{4,0},{8,4},{12,8},{16,12},{20,16},{24,20},{28,24},{32,28},{36,32}... | collective-permute-start | bytes 245768 | tf_op jit(solution)/shard_map/ppermute | solution.py:279
  18.8 1.9 %collective-permute-start = (f32[5,8,512]{2,1,0:T(8,128)S(1)}, f32[5,8,512]{2,1,0:T(8,128)S(1)}, u32[]{:S(2)}, u32[]{:S(2)}) collective-permute-start(f32[5,8,512]{2,1,0:T(8,128)S(1)} %get-tuple-element.16), channel_id=1, source_target_pairs={{0,4},{4,8},{8,12},{12,16},{16,20},{20,24},{24,28},{28,32},{32,36}... | collective-permute-start | bytes 245768 | tf_op jit(solution)/shard_map/ppermute | solution.py:278
  20.8 0.9 convert_reduce_fusion
  22.4 0.8 select_reduce_fusion.1
  23.2 0.8 all_to_all.18
  24.0 16.5 %all-to-all-start = ((s32[128,2,1]{1,2,0:T(1,128)}), s32[128,2,1]{1,2,0:T(1,128)S(1)}, u32[]{:S(2)}, u32[]{:S(2)}) async-start(s32[128,2,1]{1,2,0:T(1,128)} %bitcast.9), calls=%async_computation | async-start | bytes 131072 | tf_op jit(solution)/shard_map/all_to_all | solution.py:325
  41.3 1.9 %fusion.1 = (s32[1,32768]{1,0:T(1,128)S(1)}, s32[1,32768]{1,0:T(1,128)S(1)}) fusion(s32[1,32768]{1,0:T(1,128)} %bitcast.48), kind=kLoop, calls=%fused_computation.21 | loop fusion | flops 720896 | bytes 393216 | tf_op jit(solution)/shard_map/jit(_where)/select_n | solution.py:337
  44.6 0.8 pad_maximum_fusion.2
  45.4 9.9 %all-to-all-done = s32[128,2,1]{1,2,0:T(1,128)S(1)} async-done(((s32[128,2,1]{1,2,0:T(1,128)}), s32[128,2,1]{1,2,0:T(1,128)S(1)}, u32[]{:S(2)}, u32[]{:S(2)}) %all-to-all-start) | async-done | bytes 1056 | tf_op jit(solution)/shard_map/all_to_all | solution.py:325
  55.9 0.8 reduce.6
  57.0 0.7 gather_fusion
  57.8 0.9 broadcast_select_fusion.1
  58.6 6.2 %all-to-all-start.1 = ((f32[128,2,128]{2,1,0:T(2,128)}), f32[128,2,128]{2,1,0:T(2,128)S(1)}, u32[]{:S(2)}, u32[]{:S(2)}) async-start(f32[128,2,128]{2,1,0:T(2,128)} %broadcast_select_fusion.1), calls=%async_computation.1 | async-start | bytes 262144 | tf_op jit(solution)/shard_map/all_to_all | solution.py:331
  65.0 14.3 %all_gather.6 = f32[2,8,16,512]{3,2,1,0:T(8,128)S(1)} all-gather(f32[2,2,16,512]{3,2,1,0:T(8,128)S(1)} %pad_maximum_fusion.4), channel_id=1, replica_groups=mesh['tile'=128,'layer'=4] {'layer'}, dimensions={1}, use_global_device_ids=true | all-gather | bytes 655360 | tf_op jit(solution)/shard_map/all_gather | solution.py:328
  79.4 1.5 all-to-all-done.1
  80.8 0.7 gather_fusion.1
  82.0 14.7 %shard_map.122 = (f32[64,512]{1,0:T(8,128)S(1)}, f32[64,512]{1,0:T(8,128)S(1)}) custom-call(s32[1,32768]{1,0:T(1,128)S(1)} %get-tuple-element.25.rows_ref, s32[1,32768]{1,0:T(1,128)S(1)} %get-tuple-element.24.cols_ref, f32[1,32768]{1,0:T(1,128)S(1)} %get-tuple-element.13.diag_in_ref, f32[1,32768]{1,0:T(1,128)S(1)} %get-tuple-element.12.rhs_in_ref), custom_call_target="tpu_custom_call" | custom-call | flops 12884901888 | bytes 786432 | tf_op jit(solution)/shard_map/pallas_call | solution.py:110
  96.7 1.9 %collective-permute-start.3 = (f32[2,8,512]{2,1,0:T(8,128)S(1)}, f32[2,8,512]{2,1,0:T(8,128)S(1)}, u32[]{:S(2)}, u32[]{:S(2)}) collective-permute-start(f32[2,8,512]{2,1,0:T(8,128)S(1)} %get-tuple-element.21), channel_id=1, source_target_pairs={{4,0},{8,4},{12,8},{16,12},{20,16},{24,20},{28,24},{32,28},{36,32}... | collective-permute-start | bytes 98312 | tf_op jit(solution)/shard_map/ppermute | solution.py:279
  98.7 3.8 %collective-permute-start.2 = (f32[2,8,512]{2,1,0:T(8,128)S(1)}, f32[2,8,512]{2,1,0:T(8,128)S(1)}, u32[]{:S(2)}, u32[]{:S(2)}) collective-permute-start(f32[2,8,512]{2,1,0:T(8,128)S(1)} %get-tuple-element.20), channel_id=1, source_target_pairs={{0,4},{4,8},{8,12},{12,16},{16,20},{20,24},{24,28},{28,32},{32,36}... | collective-permute-start | bytes 98312 | tf_op jit(solution)/shard_map/ppermute | solution.py:278
  102.5 0.8 collective-permute-done.2
  103.4 1.9 %pad_maximum_fusion.fields_ref = f32[2,8,80,512]{3,2,1,0:T(8,128)S(1)} fusion(f32[2,8,8,512]{3,2,1,0:T(8,128)S(1)} %get-tuple-element.19, f32[2,8,64,512]{3,2,1,0:T(8,128)} %all-gather.2.cloned.1.call-done, f32[2,8,8,512]{3,2,1,0:T(8,128)S(1)} %get-tuple-element.18), kind=kLoop, calls=%fused_computation.3 | loop fusion | flops 1310720 | bytes 5242880 | tf_op jit(solution)/shard_map/concatenate | solution.py:329
  105.3 24.8 %shard_map.123 = f32[8,80,512]{2,1,0:T(8,128)S(1)} custom-call(f32[3,12]{1,0:T(4,128)S(1)} %pad_maximum_fusion.10.tables_ref, f32[2,8,80,512]{3,2,1,0:T(8,128)S(1)} %pad_maximum_fusion.fields_ref, f32[80,512]{1,0:T(8,128)S(1)} %maximum_bitcast_fusion.land_ref, f32[2,80,512]{2,1,0:T(8,128)S(1)} %pad_maximum_fusion.3.river_ref), custom_call_target="tpu_custom_call" | custom-call | flops 131072000 | bytes 3932160 | tf_op jit(solution)/shard_map/pallas_call | solution.py:261
  130.1 2.5 %shard_map.124 = f32[1,8192]{1,0:T(1,128)S(1)} custom-call(f32[64,512]{1,0:T(8,128)S(1)} %slice_bitcast_fusion.top_ref, s32[1,8192]{1,0:T(1,128)S(1)} %get-tuple-element.27.rows_ref, s32[1,8192]{1,0:T(1,128)S(1)} %get-tuple-element.26.cols_ref), custom_call_target="tpu_custom_call" | custom-call | flops 1610612736 | bytes 229376 | tf_op jit(solution)/shard_map/pallas_call | solution.py:151
  134.1 0.7 gather_fusion.2
  134.9 0.9 broadcast_select_fusion
  135.7 17.9 %all-to-all-start.2 = ((f32[128,2,32]{2,1,0:T(2,128)}), f32[128,2,32]{2,1,0:T(2,128)S(1)}, u32[]{:S(2)}, u32[]{:S(2)}) async-start(f32[128,2,32]{2,1,0:T(2,128)} %broadcast_select_fusion), calls=%async_computation.2 | async-start | bytes 262144 | tf_op jit(solution)/shard_map/all_to_all | solution.py:363
  153.7 0.7 constant_dynamic-slice_fusion.1
  154.4 15.2 %all-to-all-done.2 = f32[128,2,32]{2,1,0:T(2,128)S(1)} async-done(((f32[128,2,32]{2,1,0:T(2,128)}), f32[128,2,32]{2,1,0:T(2,128)S(1)}, u32[]{:S(2)}, u32[]{:S(2)}) %all-to-all-start.2) | async-done | bytes 32800 | tf_op jit(solution)/shard_map/all_to_all | solution.py:363
  169.7 0.8 select_reduce_fusion
  (55 shorter events, 5.9 us)
Async XLA Ops:
  7.2 49.9 %copy-start = (f32[16,128]{1,0:T(8,128)S(1)}, f32[16,128]{1,0:T(8,128)}, u32[]{:S(2)}) copy-start(f32[16,128]{1,0:T(8,128)} %param.17) | copy-start | bytes 24580
  7.2 37.4 %copy-start.1 = (f32[2,64,512]{2,1,0:T(8,128)S(1)}, f32[2,64,512]{2,1,0:T(8,128)}, u32[]{:S(2)}) copy-start(f32[2,64,512]{2,1,0:T(8,128)} %param.11) | copy-start | bytes 786436
  7.2 36.8 %copy-start.2 = (s32[1,256,128]{2,1,0:T(8,128)S(1)}, s32[1,256,128]{2,1,0:T(8,128)}, u32[]{:S(2)}) copy-start(s32[1,256,128]{2,1,0:T(8,128)} %param.20) | copy-start | bytes 393220
  7.2 38.2 %copy-start.4 = (f32[12]{0:T(128)S(1)}, f32[12]{0:T(128)}, u32[]{:S(2)}) copy-start(f32[12]{0:T(128)} %param.16) | copy-start | bytes 148
  7.2 38.2 %copy-start.5 = (f32[12]{0:T(128)S(1)}, f32[12]{0:T(128)}, u32[]{:S(2)}) copy-start(f32[12]{0:T(128)} %param.15) | copy-start | bytes 148
  7.2 38.2 %copy-start.6 = (f32[12]{0:T(128)S(1)}, f32[12]{0:T(128)}, u32[]{:S(2)}) copy-start(f32[12]{0:T(128)} %param.14) | copy-start | bytes 148
  10.0 54.8 %collective-permute-start.1 = (f32[5,8,512]{2,1,0:T(8,128)S(1)}, f32[5,8,512]{2,1,0:T(8,128)S(1)}, u32[]{:S(2)}, u32[]{:S(2)}) collective-permute-start(f32[5,8,512]{2,1,0:T(8,128)S(1)} %get-tuple-element.17), channel_id=1, source_target_pairs={{4,0},{8,4},{12,8},{16,12},{20,16},{24,20},{28,24},{32,28},{36,32}... | collective-permute-start | bytes 245768 | tf_op jit(solution)/shard_map/ppermute | solution.py:279
  18.8 46.0 %collective-permute-start = (f32[5,8,512]{2,1,0:T(8,128)S(1)}, f32[5,8,512]{2,1,0:T(8,128)S(1)}, u32[]{:S(2)}, u32[]{:S(2)}) collective-permute-start(f32[5,8,512]{2,1,0:T(8,128)S(1)} %get-tuple-element.16), channel_id=1, source_target_pairs={{0,4},{4,8},{8,12},{12,16},{16,20},{20,24},{24,28},{28,32},{32,36}... | collective-permute-start | bytes 245768 | tf_op jit(solution)/shard_map/ppermute | solution.py:278
  24.0 31.4 %all-to-all-start = ((s32[128,2,1]{1,2,0:T(1,128)}), s32[128,2,1]{1,2,0:T(1,128)S(1)}, u32[]{:S(2)}, u32[]{:S(2)}) async-start(s32[128,2,1]{1,2,0:T(1,128)} %bitcast.9), calls=%async_computation | async-start | bytes 131072 | tf_op jit(solution)/shard_map/all_to_all | solution.py:325
  40.5 62.8 %all-gather.2.cloned.1.call-start = ((), (), s32[]{:S(2)}) async-start(), calls=%async_computation.3 | async-start | bytes 2621440 | tf_op jit(solution)/shard_map/all_gather | solution.py:327
  58.6 22.2 %all-to-all-start.1 = ((f32[128,2,128]{2,1,0:T(2,128)}), f32[128,2,128]{2,1,0:T(2,128)S(1)}, u32[]{:S(2)}, u32[]{:S(2)}) async-start(f32[128,2,128]{2,1,0:T(2,128)} %broadcast_select_fusion.1), calls=%async_computation.1 | async-start | bytes 262144 | tf_op jit(solution)/shard_map/all_to_all | solution.py:331
  64.9 16.7 %copy-start.3 = (f32[1,256,128]{2,1,0:T(8,128)S(1)}, f32[1,256,128]{2,1,0:T(8,128)}, u32[]{:S(2)}) copy-start(f32[1,256,128]{2,1,0:T(8,128)} %param.21) | copy-start | bytes 393220
  96.7 5.8 %collective-permute-start.3 = (f32[2,8,512]{2,1,0:T(8,128)S(1)}, f32[2,8,512]{2,1,0:T(8,128)S(1)}, u32[]{:S(2)}, u32[]{:S(2)}) collective-permute-start(f32[2,8,512]{2,1,0:T(8,128)S(1)} %get-tuple-element.21), channel_id=1, source_target_pairs={{4,0},{8,4},{12,8},{16,12},{20,16},{24,20},{28,24},{32,28},{36,32}... | collective-permute-start | bytes 98312 | tf_op jit(solution)/shard_map/ppermute | solution.py:279
  98.7 4.7 %collective-permute-start.2 = (f32[2,8,512]{2,1,0:T(8,128)S(1)}, f32[2,8,512]{2,1,0:T(8,128)S(1)}, u32[]{:S(2)}, u32[]{:S(2)}) collective-permute-start(f32[2,8,512]{2,1,0:T(8,128)S(1)} %get-tuple-element.20), channel_id=1, source_target_pairs={{0,4},{4,8},{8,12},{12,16},{16,20},{20,24},{24,28},{28,32},{32,36}... | collective-permute-start | bytes 98312 | tf_op jit(solution)/shard_map/ppermute | solution.py:278
  135.7 33.9 %all-to-all-start.2 = ((f32[128,2,32]{2,1,0:T(2,128)}), f32[128,2,32]{2,1,0:T(2,128)S(1)}, u32[]{:S(2)}, u32[]{:S(2)}) async-start(f32[128,2,32]{2,1,0:T(2,128)} %broadcast_select_fusion), calls=%async_computation.2 | async-start | bytes 262144 | tf_op jit(solution)/shard_map/all_to_all | solution.py:363
Sparse Core Ops, SparseCore 0:
  57.0 33.8 all-gather.1

commit v14 on v13

--- a/solution.py
+++ b/solution.py
@@ -23,7 +23,7 @@
     (2, -1, LATERAL),
     (2, 1, LATERAL),
 )
-CHUNK = 4096
+CHUNK = 8192
 
 
 def beside(padded, axis_id, step):

time: 178 us -> 178 us (level)
  no operation moved by 1% of the time
where the time goes in v14:
time: 178 us
  starting transfers between devices  58.1 us (33%)
  Pallas kernels  42 us (24%)
  waiting for transfers between devices  27.4 us (15%)
  other arithmetic  16.3 us (9%)
  between operations  14.5 us (8%)
  blocking collectives  14.3 us (8%)
  local copies, waits for them, and re-layouts  5.73 us (3%)
    pallas_call x1, Pallas kernels, stencil(): pl.pallas_call(functools.partial(stencil_kernel, total_rows), in_specs=[p...  24.8 us
    all_to_all x1, starting transfers between devices, on_device(): arrived = lax.all_to_all(sorted_in, 'tile', 0, 0, tiled=True)  18.9 us
    all_to_all x1, starting transfers between devices, on_device(): asked = lax.all_to_all(wanted, 'tile', 0, 0, tiled=True)  16.5 us
    all_to_all x1, waiting for transfers between devices, on_device(): arrived = lax.all_to_all(sorted_in, 'tile', 0, 0, tiled=True)  15.2 us
    pallas_call x1, Pallas kernels, river_terms(): pl.pallas_call(scatter_kernel, grid=(count // chunk,), in_specs=[lane, la...  14.8 us
    all_gather x1, blocking collectives, on_device(): edges = lax.all_gather(edges, 'layer', axis=1, tiled=True)  14.3 us
    ppermute x2, starting transfers between devices, with_ghost(): lax.ppermute(lax.slice_in_dim(block, 0, width, axis=dim), axis, backward)  10.7 us
    all_to_all x1, waiting for transfers between devices, on_device(): asked = lax.all_to_all(wanted, 'tile', 0, 0, tiled=True)  9.91 us
  transfers between devices with their start and end apart: 8, of which 4 were waited for; matrix products, arithmetic and copies ran while one was open for 7% of the time, Pallas kernels for 8%

profile of v14, /device:TPU:1, one launch (start us, length us, event | category | flops | bytes accessed | tf_op | source)
XLA Modules:
  0.0 178.3 jit_solution(14249485270691438151)
XLA Ops:
  7.2 1.0 convert_bitcast_fusion
  8.2 1.0 convert_bitcast_fusion.1
  9.2 0.8 pad_maximum_fusion.7
  10.0 8.8 %collective-permute-start.1 = (f32[5,8,512]{2,1,0:T(8,128)S(1)}, f32[5,8,512]{2,1,0:T(8,128)S(1)}, u32[]{:S(2)}, u32[]{:S(2)}) collective-permute-start(f32[5,8,512]{2,1,0:T(8,128)S(1)} %get-tuple-element.17), channel_id=1, source_target_pairs={{4,0},{8,4},{12,8},{16,12},{20,16},{24,20},{28,24},{32,28},{36,32}... | collective-permute-start | bytes 245768 | tf_op jit(solution)/shard_map/ppermute | solution.py:279
  18.8 1.9 %collective-permute-start = (f32[5,8,512]{2,1,0:T(8,128)S(1)}, f32[5,8,512]{2,1,0:T(8,128)S(1)}, u32[]{:S(2)}, u32[]{:S(2)}) collective-permute-start(f32[5,8,512]{2,1,0:T(8,128)S(1)} %get-tuple-element.16), channel_id=1, source_target_pairs={{0,4},{4,8},{8,12},{12,16},{16,20},{20,24},{24,28},{28,32},{32,36}... | collective-permute-start | bytes 245768 | tf_op jit(solution)/shard_map/ppermute | solution.py:278
  20.8 0.9 convert_reduce_fusion
  22.4 0.8 select_reduce_fusion.1
  23.2 0.8 all_to_all.18
  24.0 16.5 %all-to-all-start = ((s32[128,2,1]{1,2,0:T(1,128)}), s32[128,2,1]{1,2,0:T(1,128)S(1)}, u32[]{:S(2)}, u32[]{:S(2)}) async-start(s32[128,2,1]{1,2,0:T(1,128)} %bitcast.9), calls=%async_computation | async-start | bytes 131072 | tf_op jit(solution)/shard_map/all_to_all | solution.py:325
  41.3 1.9 %fusion.1 = (s32[1,32768]{1,0:T(1,128)S(1)}, s32[1,32768]{1,0:T(1,128)S(1)}) fusion(s32[1,32768]{1,0:T(1,128)} %bitcast.48), kind=kLoop, calls=%fused_computation.21 | loop fusion | flops 720896 | bytes 393216 | tf_op jit(solution)/shard_map/jit(_where)/select_n | solution.py:337
  44.6 0.8 pad_maximum_fusion.2
  45.4 9.9 %all-to-all-done = s32[128,2,1]{1,2,0:T(1,128)S(1)} async-done(((s32[128,2,1]{1,2,0:T(1,128)}), s32[128,2,1]{1,2,0:T(1,128)S(1)}, u32[]{:S(2)}, u32[]{:S(2)}) %all-to-all-start) | async-done | bytes 1056 | tf_op jit(solution)/shard_map/all_to_all | solution.py:325
  55.9 0.8 reduce.6
  57.0 0.7 gather_fusion
  57.8 0.9 broadcast_select_fusion.1
  58.6 6.2 %all-to-all-start.1 = ((f32[128,2,128]{2,1,0:T(2,128)}), f32[128,2,128]{2,1,0:T(2,128)S(1)}, u32[]{:S(2)}, u32[]{:S(2)}) async-start(f32[128,2,128]{2,1,0:T(2,128)} %broadcast_select_fusion.1), calls=%async_computation.1 | async-start | bytes 262144 | tf_op jit(solution)/shard_map/all_to_all | solution.py:331
  65.0 14.3 %all_gather.6 = f32[2,8,16,512]{3,2,1,0:T(8,128)S(1)} all-gather(f32[2,2,16,512]{3,2,1,0:T(8,128)S(1)} %pad_maximum_fusion.4), channel_id=1, replica_groups=mesh['tile'=128,'layer'=4] {'layer'}, dimensions={1}, use_global_device_ids=true | all-gather | bytes 655360 | tf_op jit(solution)/shard_map/all_gather | solution.py:328
  79.4 1.5 all-to-all-done.1
  80.8 0.7 gather_fusion.1
  82.0 14.8 %shard_map.122 = (f32[64,512]{1,0:T(8,128)S(1)}, f32[64,512]{1,0:T(8,128)S(1)}) custom-call(s32[1,32768]{1,0:T(1,128)S(1)} %get-tuple-element.25.rows_ref, s32[1,32768]{1,0:T(1,128)S(1)} %get-tuple-element.24.cols_ref, f32[1,32768]{1,0:T(1,128)S(1)} %get-tuple-element.13.diag_in_ref, f32[1,32768]{1,0:T(1,128)S(1)} %get-tuple-element.12.rhs_in_ref), custom_call_target="tpu_custom_call" | custom-call | flops 12884901888 | bytes 786432 | tf_op jit(solution)/shard_map/pallas_call | solution.py:110
  96.8 1.9 %collective-permute-start.3 = (f32[2,8,512]{2,1,0:T(8,128)S(1)}, f32[2,8,512]{2,1,0:T(8,128)S(1)}, u32[]{:S(2)}, u32[]{:S(2)}) collective-permute-start(f32[2,8,512]{2,1,0:T(8,128)S(1)} %get-tuple-element.21), channel_id=1, source_target_pairs={{4,0},{8,4},{12,8},{16,12},{20,16},{24,20},{28,24},{32,28},{36,32}... | collective-permute-start | bytes 98312 | tf_op jit(solution)/shard_map/ppermute | solution.py:279
  98.8 3.8 %collective-permute-start.2 = (f32[2,8,512]{2,1,0:T(8,128)S(1)}, f32[2,8,512]{2,1,0:T(8,128)S(1)}, u32[]{:S(2)}, u32[]{:S(2)}) collective-permute-start(f32[2,8,512]{2,1,0:T(8,128)S(1)} %get-tuple-element.20), channel_id=1, source_target_pairs={{0,4},{4,8},{8,12},{12,16},{16,20},{20,24},{24,28},{28,32},{32,36}... | collective-permute-start | bytes 98312 | tf_op jit(solution)/shard_map/ppermute | solution.py:278
  102.7 0.8 collective-permute-done.2
  103.5 1.9 %pad_maximum_fusion.fields_ref = f32[2,8,80,512]{3,2,1,0:T(8,128)S(1)} fusion(f32[2,8,8,512]{3,2,1,0:T(8,128)S(1)} %get-tuple-element.19, f32[2,8,64,512]{3,2,1,0:T(8,128)} %all-gather.2.cloned.1.call-done, f32[2,8,8,512]{3,2,1,0:T(8,128)S(1)} %get-tuple-element.18), kind=kLoop, calls=%fused_computation.3 | loop fusion | flops 1310720 | bytes 5242880 | tf_op jit(solution)/shard_map/concatenate | solution.py:329
  105.4 24.8 %shard_map.123 = f32[8,80,512]{2,1,0:T(8,128)S(1)} custom-call(f32[3,12]{1,0:T(4,128)S(1)} %pad_maximum_fusion.10.tables_ref, f32[2,8,80,512]{3,2,1,0:T(8,128)S(1)} %pad_maximum_fusion.fields_ref, f32[80,512]{1,0:T(8,128)S(1)} %maximum_bitcast_fusion.land_ref, f32[2,80,512]{2,1,0:T(8,128)S(1)} %pad_maximum_fusion.3.river_ref), custom_call_target="tpu_custom_call" | custom-call | flops 131072000 | bytes 3932160 | tf_op jit(solution)/shard_map/pallas_call | solution.py:261
  130.3 2.3 %shard_map.124 = f32[1,8192]{1,0:T(1,128)S(1)} custom-call(f32[64,512]{1,0:T(8,128)S(1)} %slice_bitcast_fusion.top_ref, s32[1,8192]{1,0:T(1,128)S(1)} %get-tuple-element.27.rows_ref, s32[1,8192]{1,0:T(1,128)S(1)} %get-tuple-element.26.cols_ref), custom_call_target="tpu_custom_call" | custom-call | flops 1610612736 | bytes 229376 | tf_op jit(solution)/shard_map/pallas_call | solution.py:151
  134.1 0.7 gather_fusion.2
  134.9 0.9 broadcast_select_fusion
  135.7 18.9 %all-to-all-start.2 = ((f32[128,2,32]{2,1,0:T(2,128)}), f32[128,2,32]{2,1,0:T(2,128)S(1)}, u32[]{:S(2)}, u32[]{:S(2)}) async-start(f32[128,2,32]{2,1,0:T(2,128)} %broadcast_select_fusion), calls=%async_computation.2 | async-start | bytes 262144 | tf_op jit(solution)/shard_map/all_to_all | solution.py:363
  154.7 0.7 constant_dynamic-slice_fusion.1
  155.5 15.2 %all-to-all-done.2 = f32[128,2,32]{2,1,0:T(2,128)S(1)} async-done(((f32[128,2,32]{2,1,0:T(2,128)}), f32[128,2,32]{2,1,0:T(2,128)S(1)}, u32[]{:S(2)}, u32[]{:S(2)}) %all-to-all-start.2) | async-done | bytes 32800 | tf_op jit(solution)/shard_map/all_to_all | solution.py:363
  170.7 0.8 select_reduce_fusion
  (55 shorter events, 5.9 us)
Async XLA Ops:
  7.2 49.9 %copy-start = (f32[16,128]{1,0:T(8,128)S(1)}, f32[16,128]{1,0:T(8,128)}, u32[]{:S(2)}) copy-start(f32[16,128]{1,0:T(8,128)} %param.17) | copy-start | bytes 24580
  7.2 37.4 %copy-start.1 = (f32[2,64,512]{2,1,0:T(8,128)S(1)}, f32[2,64,512]{2,1,0:T(8,128)}, u32[]{:S(2)}) copy-start(f32[2,64,512]{2,1,0:T(8,128)} %param.11) | copy-start | bytes 786436
  7.2 36.8 %copy-start.2 = (s32[1,256,128]{2,1,0:T(8,128)S(1)}, s32[1,256,128]{2,1,0:T(8,128)}, u32[]{:S(2)}) copy-start(s32[1,256,128]{2,1,0:T(8,128)} %param.20) | copy-start | bytes 393220
  7.2 38.2 %copy-start.4 = (f32[12]{0:T(128)S(1)}, f32[12]{0:T(128)}, u32[]{:S(2)}) copy-start(f32[12]{0:T(128)} %param.16) | copy-start | bytes 148
  7.2 38.2 %copy-start.5 = (f32[12]{0:T(128)S(1)}, f32[12]{0:T(128)}, u32[]{:S(2)}) copy-start(f32[12]{0:T(128)} %param.15) | copy-start | bytes 148
  7.2 38.2 %copy-start.6 = (f32[12]{0:T(128)S(1)}, f32[12]{0:T(128)}, u32[]{:S(2)}) copy-start(f32[12]{0:T(128)} %param.14) | copy-start | bytes 148
  10.0 54.8 %collective-permute-start.1 = (f32[5,8,512]{2,1,0:T(8,128)S(1)}, f32[5,8,512]{2,1,0:T(8,128)S(1)}, u32[]{:S(2)}, u32[]{:S(2)}) collective-permute-start(f32[5,8,512]{2,1,0:T(8,128)S(1)} %get-tuple-element.17), channel_id=1, source_target_pairs={{4,0},{8,4},{12,8},{16,12},{20,16},{24,20},{28,24},{32,28},{36,32}... | collective-permute-start | bytes 245768 | tf_op jit(solution)/shard_map/ppermute | solution.py:279
  18.8 46.0 %collective-permute-start = (f32[5,8,512]{2,1,0:T(8,128)S(1)}, f32[5,8,512]{2,1,0:T(8,128)S(1)}, u32[]{:S(2)}, u32[]{:S(2)}) collective-permute-start(f32[5,8,512]{2,1,0:T(8,128)S(1)} %get-tuple-element.16), channel_id=1, source_target_pairs={{0,4},{4,8},{8,12},{12,16},{16,20},{20,24},{24,28},{28,32},{32,36}... | collective-permute-start | bytes 245768 | tf_op jit(solution)/shard_map/ppermute | solution.py:278
  24.0 31.4 %all-to-all-start = ((s32[128,2,1]{1,2,0:T(1,128)}), s32[128,2,1]{1,2,0:T(1,128)S(1)}, u32[]{:S(2)}, u32[]{:S(2)}) async-start(s32[128,2,1]{1,2,0:T(1,128)} %bitcast.9), calls=%async_computation | async-start | bytes 131072 | tf_op jit(solution)/shard_map/all_to_all | solution.py:325
  40.5 63.0 %all-gather.2.cloned.1.call-start = ((), (), s32[]{:S(2)}) async-start(), calls=%async_computation.3 | async-start | bytes 2621440 | tf_op jit(solution)/shard_map/all_gather | solution.py:327
  58.6 22.2 %all-to-all-start.1 = ((f32[128,2,128]{2,1,0:T(2,128)}), f32[128,2,128]{2,1,0:T(2,128)S(1)}, u32[]{:S(2)}, u32[]{:S(2)}) async-start(f32[128,2,128]{2,1,0:T(2,128)} %broadcast_select_fusion.1), calls=%async_computation.1 | async-start | bytes 262144 | tf_op jit(solution)/shard_map/all_to_all | solution.py:331
  64.9 16.7 %copy-start.3 = (f32[1,256,128]{2,1,0:T(8,128)S(1)}, f32[1,256,128]{2,1,0:T(8,128)}, u32[]{:S(2)}) copy-start(f32[1,256,128]{2,1,0:T(8,128)} %param.21) | copy-start | bytes 393220
  96.8 5.8 %collective-permute-start.3 = (f32[2,8,512]{2,1,0:T(8,128)S(1)}, f32[2,8,512]{2,1,0:T(8,128)S(1)}, u32[]{:S(2)}, u32[]{:S(2)}) collective-permute-start(f32[2,8,512]{2,1,0:T(8,128)S(1)} %get-tuple-element.21), channel_id=1, source_target_pairs={{4,0},{8,4},{12,8},{16,12},{20,16},{24,20},{28,24},{32,28},{36,32}... | collective-permute-start | bytes 98312 | tf_op jit(solution)/shard_map/ppermute | solution.py:279
  98.8 4.7 %collective-permute-start.2 = (f32[2,8,512]{2,1,0:T(8,128)S(1)}, f32[2,8,512]{2,1,0:T(8,128)S(1)}, u32[]{:S(2)}, u32[]{:S(2)}) collective-permute-start(f32[2,8,512]{2,1,0:T(8,128)S(1)} %get-tuple-element.20), channel_id=1, source_target_pairs={{0,4},{4,8},{8,12},{12,16},{16,20},{20,24},{24,28},{28,32},{32,36}... | collective-permute-start | bytes 98312 | tf_op jit(solution)/shard_map/ppermute | solution.py:278
  135.7 34.9 %all-to-all-start.2 = ((f32[128,2,32]{2,1,0:T(2,128)}), f32[128,2,32]{2,1,0:T(2,128)S(1)}, u32[]{:S(2)}, u32[]{:S(2)}) async-start(f32[128,2,32]{2,1,0:T(2,128)} %broadcast_select_fusion), calls=%async_computation.2 | async-start | bytes 262144 | tf_op jit(solution)/shard_map/all_to_all | solution.py:363
Sparse Core Ops, SparseCore 0:
  57.0 33.9 all-gather.1
